TPU v7x, 32 devices: a whole 2x2x4 slice. The times are simulated.
32 devices in a mesh: pos: 2 (over x), gz: 16 (over z, y, core).
Axes of the slice: x: 2, y: 2, z: 4, core: 2. Of those that a mesh axis runs over, the one named last changes fastest.
Arguments:
- source: float32 [16, 512, 256], P('gz', 'pos'), parts along dimension 1
- regions: int32 [16, 512, 256], P('gz', 'pos'), parts along dimension 1, may hold values from 0 to 3
- reluctivity: float32 [4], replicated, may hold values from 0.25 to 2
- levels: float32 [4], replicated, may hold values from 0.5 to 1.5
- seeds: int32 [4, 4], replicated, may hold values from 0 to 3, as said below
- band_cells: int32 [4096], P('pos'), parts along dimension 0, may hold values from 0 to 65535, as said below
- sector_order: int32 [4096], P('pos'), parts along dimension 0, may hold values from 0 to 2047, each once
Outputs:
- solution: float32 [4, 16, 512, 256], P(None, 'gz', 'pos'), parts along dimension 2
- forces: float32 [2, 8, 32, 16], P(None, 'pos', 'gz'), parts along dimension 1
There are 2 independent parts, one for each index of `pos`. A program takes and returns all parts, laid end to end along the dimension named above; an argument that names none is the same for every part. Nothing has to cross between parts.
Inputs may be any that keep to these rules, and one draw needn't show every extreme that they name: `seeds`: every level is named by exactly 4 entries. `band_cells`: distinct cells. `sector_order`: each band entry once.
All inputs are finite; a program needn't handle non-finite values.
Results may differ from a plain program's by a relative error of at most 0.0003.
Values sent between devices are 32-bit elements; how exact they have to be, the bound alone decides.
No kernel may reach another device: no remote copies, remote signals or barrier semaphores. Data moves between devices by JAX's collectives and lax.ppermute only.
A program may use at most 128 MiB of HBM per device.

v0:
```python
import jax
import jax.numpy as jnp
from jax import lax
from jax.sharding import PartitionSpec as P

ITERS = 2
PER_SEC = 64


MASS_SHIFT = 0.5


def with_halo(block, sides, width):
    for axis, dim in sides:
        count = lax.axis_size(axis)
        forward = [(i, i + 1) for i in range(count - 1)]
        backward = [(target, source) for source, target in forward]
        low = lax.ppermute(
            lax.slice_in_dim(block, block.shape[dim] - width, None, axis=dim), axis, forward
        )
        high = lax.ppermute(lax.slice_in_dim(block, 0, width, axis=dim), axis, backward)
        block = jnp.concatenate([low, block, high], axis=dim)
    return block


def face_weights(reluct_cell, padded):
    return (
        0.5 * (reluct_cell + padded[:-2, 1:-1, 1:-1]),
        0.5 * (reluct_cell + padded[2:, 1:-1, 1:-1]),
        0.5 * (reluct_cell + padded[1:-1, :-2, 1:-1]),
        0.5 * (reluct_cell + padded[1:-1, 2:, 1:-1]),
        0.5 * (reluct_cell + padded[1:-1, 1:-1, :-2]),
        0.5 * (reluct_cell + padded[1:-1, 1:-1, 2:]),
    )


def apply_stencil(field, padded, weights):
    total = MASS_SHIFT * field
    total = total + weights[0][None] * (field - padded[:, :-2, 1:-1, 1:-1])
    total = total + weights[1][None] * (field - padded[:, 2:, 1:-1, 1:-1])
    total = total + weights[2][None] * (field - padded[:, 1:-1, :-2, 1:-1])
    total = total + weights[3][None] * (field - padded[:, 1:-1, 2:, 1:-1])
    total = total + weights[4][None] * (field - padded[:, 1:-1, 1:-1, :-2])
    total = total + weights[5][None] * (field - padded[:, 1:-1, 1:-1, 2:])
    return total


def operate(field, weights):
    axial = with_halo(field, (("gz", 1),), 1)
    padded = jnp.pad(axial, ((0, 0), (0, 0), (1, 1), (1, 1)))
    return apply_stencil(field, padded, weights)


def band_stress(field, band_cells, sector_order):
    count_cols, depth, width_x, width_y = field.shape
    padded = jnp.pad(field, ((0, 0), (0, 0), (1, 1), (1, 1)))
    flux_x = 0.5 * (padded[:, :, 1:-1, 2:] - padded[:, :, 1:-1, :-2])
    flux_y = -0.5 * (padded[:, :, 2:, 1:-1] - padded[:, :, :-2, 1:-1])
    ordered = jnp.take(band_cells, sector_order)
    picked_x = jnp.take(flux_x.reshape(count_cols, depth, width_x * width_y), ordered, axis=2)
    picked_y = jnp.take(flux_y.reshape(count_cols, depth, width_x * width_y), ordered, axis=2)
    row_index = (ordered // width_y).astype(jnp.float32)
    column_index = (ordered % width_y).astype(jnp.float32)
    normal_x = (row_index - 0.5 * (width_x - 1)) / (0.5 * width_x)
    normal_y = (column_index - 0.5 * (width_y - 1)) / (0.5 * width_y)
    normal_part = picked_x * normal_x + picked_y * normal_y
    half_square = 0.5 * (picked_x * picked_x + picked_y * picked_y)
    force_x = picked_x * normal_part - half_square * normal_x
    force_y = picked_y * normal_part - half_square * normal_y
    return jnp.stack([force_x, force_y])


def column_sum(first, second):
    return jnp.sum(first * second, axis=(1, 2, 3))


def widen(vector):
    return vector[:, None, None, None]


def squares(residual):
    return lax.psum(column_sum(residual, residual), "gz")


def body(source, regions, reluctivity, levels, seeds, band_cells, sector_order):
    count_regions = reluctivity.shape[0]
    count_levels = levels.shape[0]
    count_cols = seeds.shape[0]
    level_pick = (
        seeds[:, :, None] == jnp.arange(count_levels, dtype=jnp.int32)[None, None, :]
    ).astype(jnp.float32)
    strength = jnp.sum(level_pick * levels[None, None, :], axis=2)
    reluct_cell = jnp.zeros(source.shape, jnp.float32)
    scaling = jnp.zeros((count_cols,) + source.shape, jnp.float32)
    for region in range(count_regions):
        member = (regions == region).astype(jnp.float32)
        reluct_cell = reluct_cell + reluctivity[region] * member
        scaling = scaling + widen(strength[:, region]) * member[None]
    right_side = scaling * source[None]
    axial_reluct = with_halo(reluct_cell, (("gz", 0),), 1)
    weights = face_weights(reluct_cell, jnp.pad(axial_reluct, ((0, 0), (1, 1), (1, 1))))
    solution = jnp.zeros_like(right_side)
    residual = right_side
    direction = right_side
    norm_now = squares(residual)
    for iteration in range(ITERS):
        image = operate(direction, weights)
        curvature = lax.psum(column_sum(direction, image), "gz")
        step_size = norm_now / curvature
        solution = solution + widen(step_size) * direction
        residual = residual - widen(step_size) * image
        if iteration + 1 < ITERS:
            norm_next = squares(residual)
            direction = residual + widen(norm_next / norm_now) * direction
            norm_now = norm_next
    stress = band_stress(solution, band_cells, sector_order)
    depth = stress.shape[2]
    band_total = stress.shape[3]
    cell_forces = stress.reshape(2 * count_cols, depth, band_total // PER_SEC, PER_SEC)
    sector_sums = jnp.sum(cell_forces, axis=-1)
    gathered = lax.all_to_all(sector_sums, "gz", split_axis=2, concat_axis=1, tiled=True)
    full_depth = gathered.shape[1]
    local_sectors = gathered.shape[2]
    return (
        solution,
        gathered.reshape(2, count_cols, full_depth, local_sectors).transpose(0, 1, 3, 2),
    )


def solution(mesh):
    in_specs = (P("gz", "pos", None), P("gz", "pos", None), P(), P(), P(), P("pos"), P("pos"))
    out_specs = (P(None, "gz", "pos", None), P(None, "pos", "gz", None))
    return jax.shard_map(body, mesh=mesh, in_specs=in_specs, out_specs=out_specs, check_vma=False)
```

profile of v0, /device:TPU:0, one launch (start us, length us, event | category | flops | bytes accessed | tf_op | source)
XLA Modules:
  0.0 248.1 jit_solution(8172619403252615749)
XLA Ops:
  0.6 0.0 copy-start
  0.6 1.5 fusion.45
  2.1 0.9 select_reduce_fusion
  3.0 0.2 slice_reduce_fusion.3
  3.2 3.7 %select_add_fusion = (f32[1,256,256]{2,1,0:T(8,128)S(1)}, pred[1,256,256]{2,1,0:T(8,128)(4,1)S(1)}, pred[1,256,256]{2,1,0:T(8,128)(4,1)S(1)}, pred[1,256,256]{2,1,0:T(8,128)(4,1)S(1)}, pred[1,256,256]{2,1,0:T(8,128)(4,1)S(1)}) fusion(f32[]{:T(128)} %bitcast.8, f32[]{:T(128)} %bitcast.7, f32[]{:T(128)} %bitcast.6, f32[]{:T(128)} %bitcast.5, ...), kind=kLoop, calls=%fused_computation.82 | loop fusion | flops 720896 | bytes 786448 | tf_op jit(solution)/shard_map/add | solution.py:97
  7.0 1.3 add_multiply_fusion
  8.3 2.4 collective-permute-start.1
  10.7 1.3 collective-permute-start.3
  12.0 5.1 %collective-permute-start = (f32[1,256,256]{2,1,0:T(8,128)S(1)}, f32[1,256,256]{2,1,0:T(8,128)S(1)}, u32[]{:S(2)}, u32[]{:S(2)}) collective-permute-start(f32[1,256,256]{2,1,0:T(8,128)S(1)} %get-tuple-element.24), channel_id=1, source_target_pairs={{0,1},{1,2},{2,3},{3,4},{4,5},{5,6},{6,7},{7,8},{8,9},{9,10},{10,1... | collective-permute-start | bytes 786440 | tf_op jit(solution)/shard_map/ppermute | solution.py:18
  17.2 1.3 collective-permute-start.2
  18.5 0.0 collective-permute-done
  18.5 3.3 %collective-permute-done.2 = f32[1,256,256]{2,1,0:T(8,128)S(1)} collective-permute-done((f32[1,256,256]{2,1,0:T(8,128)S(1)}, f32[1,256,256]{2,1,0:T(8,128)S(1)}, u32[]{:S(2)}, u32[]{:S(2)}) %collective-permute-start.2) | collective-permute-done | bytes 262176 | tf_op jit(solution)/shard_map/ppermute | solution.py:21
  21.8 0.4 select_maximum_fusion.4
  22.2 0.0 copy-start.2
  22.2 0.3 fusion.35
  22.5 0.0 copy-start.4
  22.5 0.0 copy-start.6
  22.6 0.0 copy-start.8
  22.6 0.0 copy-start.10
  22.6 0.0 copy-start.12
  22.6 0.0 copy-start.14
  22.6 0.0 collective-permute-done.1
  22.6 0.0 collective-permute-done.3
  22.6 2.4 select_maximum_fusion.2
  25.0 0.0 copy-done.2
  25.0 1.8 multiply_reduce_fusion.1
  26.8 0.0 copy-done.4
  26.8 0.0 copy-done.6
  26.8 0.0 copy-done.8
  26.9 0.0 copy-done.10
  26.9 0.0 copy-start.16
  26.9 50.9 %all-reduce.4 = (f32[4]{0:T(128)S(1)}, f32[4]{0:T(128)S(1)}) all-reduce(f32[4]{0:T(128)S(1)} %get-tuple-element.14, f32[4]{0:T(128)S(1)} %get-tuple-element.13), channel_id=1, replica_groups=mesh['pos'=2,'gz'=16] {'gz'}, use_global_device_ids=true, to_apply=%region_2.3 | all-reduce | flops 8 | bytes 64 | tf_op jit(solution)/shard_map/psum | solution.py:82
  77.8 0.6 multiply_reduce_fusion
  78.3 29.5 %psum.30 = f32[4]{0:T(128)S(1)} all-reduce(f32[4]{0:T(128)S(1)} %multiply_reduce_fusion), channel_id=1, replica_groups=mesh['pos'=2,'gz'=16] {'gz'}, use_global_device_ids=true, to_apply=%region_6.7 | all-reduce | flops 4 | bytes 32 | tf_op jit(solution)/shard_map/psum | solution.py:82
  107.8 0.5 multiply_add_fusion.1
  108.3 1.8 collective-permute-start.4
  110.2 1.3 collective-permute-start.5
  111.5 11.8 %gather_fusion = s32[2048]{0:T(1024)S(1)} fusion(s32[2048]{0:T(1024)S(1)} %copy-done, s32[2048]{0:T(1024)S(1)} %fusion.41), kind=kCustom, calls=%fused_computation.2 | custom fusion | bytes 24576 | tf_op jit(solution)/shard_map/jit(_take)/gather | solution.py:59
  123.3 0.0 copy-start.5
  123.3 0.0 copy-start.7
  123.4 0.0 collective-permute-done.4
  123.4 0.0 collective-permute-done.5
  123.4 3.5 %select_maximum_fusion = f32[4,3,258,258]{3,2,1,0:T(8,128)S(1)} fusion(f32[4,1,256,256]{3,2,1,0:T(8,128)} %collective-permute-done.5, f32[4,1,256,256]{3,2,1,0:T(8,128)S(1)} %multiply_add_fusion.1, f32[4,1,256,256]{3,2,1,0:T(8,128)S(1)} %collective-permute-done.4), kind=kLoop, calls=%fused_computation.7 | loop fusion | flops 11981520 | bytes 6340800 | tf_op jit(solution)/shard_map/concatenate | solution.py:22
  127.0 2.5 %fusion.13 = f32[4]{0:T(128)S(1)} fusion(f32[4,1,256,256]{3,2,1,0:T(8,128)S(1)} %multiply_add_fusion.1, f32[4,3,258,258]{3,2,1,0:T(8,128)S(1)} %select_maximum_fusion, f32[4,1,256,256]{3,2,1,0:T(8,128)} %collective-permute-done.5, f32[4,1,256,256]{3,2,1,0:T(8,128)S(1)} %collective-permute-done.4, f32[256,256]{1,0:T(8,128)S(1)} %copy-done.7, ...), kind=kLoop, calls=%fused_computation.35 | loop fusion | flops 5505020 | bytes 8912912 | tf_op jit(solution)/shard_map/reduce_sum | solution.py:74
  129.5 39.2 %psum.31 = f32[4]{0:T(128)S(1)} all-reduce(f32[4]{0:T(128)S(1)} %fusion.13), channel_id=1, replica_groups=mesh['pos'=2,'gz'=16] {'gz'}, use_global_device_ids=true, to_apply=%region_8.9 | all-reduce | flops 4 | bytes 32 | tf_op jit(solution)/shard_map/psum | solution.py:108
  168.8 0.4 multiply_add_fusion
  169.2 0.0 copy-start.3
  169.2 1.0 copy-done.3
  170.2 0.7 fusion.9
  170.9 16.5 %copy.33 = f32[4,1,256,256]{0,3,2,1:T(8,128)} copy(f32[4,1,256,256]{3,2,1,0:T(8,128)S(1)} %get-tuple-element.34) | data formatting | bytes 2097152 | tf_op jit(solution)/shard_map/mul | solution.py:57
  187.4 16.0 %gather_fusion.1 = f32[2048,4]{1,0:T(8,128)S(1)} fusion(f32[4,65536]{0,1:T(8,128)} %bitcast.64, s32[2048]{0:T(1024)S(1)} %fusion.42), kind=kCustom, calls=%fused_computation.clone | custom fusion | bytes 73728 | tf_op jit(solution)/shard_map/jit(_take)/gather | solution.py:60
  203.4 0.3 copy.34
  203.8 16.5 %copy.35 = f32[4,1,256,256]{0,3,2,1:T(8,128)} copy(f32[4,1,256,256]{3,2,1,0:T(8,128)S(1)} %get-tuple-element.33) | data formatting | bytes 2097152 | tf_op jit(solution)/shard_map/mul | solution.py:58
  220.3 16.0 %gather_fusion.2 = f32[2048,4]{1,0:T(8,128)S(1)} fusion(f32[4,65536]{0,1:T(8,128)} %bitcast.63, s32[2048]{0:T(1024)S(1)} %fusion.42), kind=kCustom, calls=%fused_computation.1.clone | custom fusion | bytes 73728 | tf_op jit(solution)/shard_map/jit(_take)/gather | solution.py:61
  236.3 0.3 copy.36
  236.6 0.1 subtract_bitcast_fusion.1
  236.7 0.1 reshape.211
  236.8 0.1 reduce_sum.61
  236.9 0.1 copy.37
  237.0 9.1 %all_to_all.4 = f32[8,1,32]{0,1,2:T(1,128)S(1)} all-to-all(f32[8,1,32]{0,1,2:T(1,128)S(1)} %copy.37), channel_id=1, replica_groups=mesh['pos'=2,'gz'=16] {'gz'}, dimensions={2} | all-to-all | bytes 2048 | tf_op jit(solution)/shard_map/all_to_all | solution.py:121
  246.1 0.5 broadcast.493
  246.6 0.7 reduce.12
  247.3 0.1 reshape.212
  247.4 0.7 copy.38
  (27 shorter events, 0.2 us)
Async XLA Ops:
  0.6 110.9 %copy-start = (s32[2048]{0:T(1024)S(1)}, s32[2048]{0:T(1024)}, u32[]{:S(2)}) copy-start(s32[2048]{0:T(1024)} %param.14) | copy-start | bytes 24580
  8.3 14.3 %collective-permute-start.1 = (f32[4,1,256,256]{3,2,1,0:T(8,128)S(1)}, f32[4,1,256,256]{3,2,1,0:T(8,128)S(1)}, u32[]{:S(2)}, u32[]{:S(2)}) collective-permute-start(f32[4,1,256,256]{3,2,1,0:T(8,128)S(1)} %add_multiply_fusion), channel_id=1, source_target_pairs={{0,1},{1,2},{2,3},{3,4},{4,5},{5,6},{6,7},{7,8},{8,9},{9,10},{10,1... | collective-permute-start | bytes 3145736 | tf_op jit(solution)/shard_map/ppermute | solution.py:18
  10.7 11.9 %collective-permute-start.3 = (f32[4,1,256,256]{3,2,1,0:T(8,128)S(1)}, f32[4,1,256,256]{3,2,1,0:T(8,128)S(1)}, u32[]{:S(2)}, u32[]{:S(2)}) collective-permute-start(f32[4,1,256,256]{3,2,1,0:T(8,128)S(1)} %add_multiply_fusion), channel_id=1, source_target_pairs={{1,0},{2,1},{3,2},{4,3},{5,4},{6,5},{7,6},{8,7},{9,8},{10,9},{11,1... | collective-permute-start | bytes 3145736 | tf_op jit(solution)/shard_map/ppermute | solution.py:21
  12.0 6.4 %collective-permute-start = (f32[1,256,256]{2,1,0:T(8,128)S(1)}, f32[1,256,256]{2,1,0:T(8,128)S(1)}, u32[]{:S(2)}, u32[]{:S(2)}) collective-permute-start(f32[1,256,256]{2,1,0:T(8,128)S(1)} %get-tuple-element.24), channel_id=1, source_target_pairs={{0,1},{1,2},{2,3},{3,4},{4,5},{5,6},{6,7},{7,8},{8,9},{9,10},{10,1... | collective-permute-start | bytes 786440 | tf_op jit(solution)/shard_map/ppermute | solution.py:18
  17.2 4.7 %collective-permute-start.2 = (f32[1,256,256]{2,1,0:T(8,128)S(1)}, f32[1,256,256]{2,1,0:T(8,128)S(1)}, u32[]{:S(2)}, u32[]{:S(2)}) collective-permute-start(f32[1,256,256]{2,1,0:T(8,128)S(1)} %get-tuple-element.24), channel_id=1, source_target_pairs={{1,0},{2,1},{3,2},{4,3},{5,4},{6,5},{7,6},{8,7},{9,8},{10,9},{11,1... | collective-permute-start | bytes 786440 | tf_op jit(solution)/shard_map/ppermute | solution.py:21
  22.2 2.8 %copy-start.2 = (f32[1,256,256]{2,1,0:T(8,128)S(1)}, f32[1,256,256]{2,1,0:T(8,128)}, u32[]{:S(2)}) copy-start(f32[1,256,256]{2,1,0:T(8,128)} %param.9) | copy-start | bytes 786436
  22.5 4.3 %copy-start.4 = (f32[256,256]{1,0:T(8,128)}, f32[256,256]{1,0:T(8,128)S(1)}, u32[]{:S(2)}) copy-start(f32[256,256]{1,0:T(8,128)S(1)} %get-tuple-element.29) | copy-start | bytes 786436
  22.5 4.3 %copy-start.6 = (f32[256,256]{1,0:T(8,128)}, f32[256,256]{1,0:T(8,128)S(1)}, u32[]{:S(2)}) copy-start(f32[256,256]{1,0:T(8,128)S(1)} %get-tuple-element.30) | copy-start | bytes 786436
  22.6 4.3 %copy-start.8 = (f32[256,256]{1,0:T(8,128)}, f32[256,256]{1,0:T(8,128)S(1)}, u32[]{:S(2)}) copy-start(f32[256,256]{1,0:T(8,128)S(1)} %get-tuple-element.31) | copy-start | bytes 786436
  22.6 4.3 %copy-start.10 = (f32[256,256]{1,0:T(8,128)}, f32[256,256]{1,0:T(8,128)S(1)}, u32[]{:S(2)}) copy-start(f32[256,256]{1,0:T(8,128)S(1)} %get-tuple-element.32) | copy-start | bytes 786436
  22.6 4.3 %copy-start.12 = (f32[256,256]{1,0:T(8,128)}, f32[256,256]{1,0:T(8,128)S(1)}, u32[]{:S(2)}) copy-start(f32[256,256]{1,0:T(8,128)S(1)} %get-tuple-element.35) | copy-start | bytes 786436
  22.6 4.3 %copy-start.14 = (f32[256,256]{1,0:T(8,128)}, f32[256,256]{1,0:T(8,128)S(1)}, u32[]{:S(2)}) copy-start(f32[256,256]{1,0:T(8,128)S(1)} %get-tuple-element.36) | copy-start | bytes 786436
  26.9 84.6 %copy-start.16 = (s32[2048]{0:T(1024)S(1)}, s32[2048]{0:T(1024)}, u32[]{:S(2)}) copy-start(s32[2048]{0:T(1024)} %param.15) | copy-start | bytes 24580
  108.3 15.1 %collective-permute-start.4 = (f32[4,1,256,256]{3,2,1,0:T(8,128)S(1)}, f32[4,1,256,256]{3,2,1,0:T(8,128)S(1)}, u32[]{:S(2)}, u32[]{:S(2)}) collective-permute-start(f32[4,1,256,256]{3,2,1,0:T(8,128)S(1)} %multiply_add_fusion.1), channel_id=1, source_target_pairs={{0,1},{1,2},{2,3},{3,4},{4,5},{5,6},{6,7},{7,8},{8,9},{9,10},{10,1... | collective-permute-start | bytes 3145736 | tf_op jit(solution)/shard_map/ppermute | solution.py:18
  110.2 13.3 %collective-permute-start.5 = (f32[4,1,256,256]{3,2,1,0:T(8,128)S(1)}, f32[4,1,256,256]{3,2,1,0:T(8,128)}, u32[]{:S(2)}, u32[]{:S(2)}) collective-permute-start(f32[4,1,256,256]{3,2,1,0:T(8,128)S(1)} %multiply_add_fusion.1), channel_id=1, source_target_pairs={{1,0},{2,1},{3,2},{4,3},{5,4},{6,5},{7,6},{8,7},{9,8},{10,9},{11,1... | collective-permute-start | bytes 3145736 | tf_op jit(solution)/shard_map/ppermute | solution.py:21
  123.3 3.7 %copy-start.5 = (f32[256,256]{1,0:T(8,128)S(1)}, f32[256,256]{1,0:T(8,128)}, u32[]{:S(2)}) copy-start(f32[256,256]{1,0:T(8,128)} %copy-done.4) | copy-start | bytes 786436
  123.3 3.7 %copy-start.7 = (f32[256,256]{1,0:T(8,128)S(1)}, f32[256,256]{1,0:T(8,128)}, u32[]{:S(2)}) copy-start(f32[256,256]{1,0:T(8,128)} %copy-done.6) | copy-start | bytes 786436
  123.3 3.7 %copy-start.9 = (f32[256,256]{1,0:T(8,128)S(1)}, f32[256,256]{1,0:T(8,128)}, u32[]{:S(2)}) copy-start(f32[256,256]{1,0:T(8,128)} %copy-done.8) | copy-start | bytes 786436
  123.3 3.7 %copy-start.11 = (f32[256,256]{1,0:T(8,128)S(1)}, f32[256,256]{1,0:T(8,128)}, u32[]{:S(2)}) copy-start(f32[256,256]{1,0:T(8,128)} %copy-done.10) | copy-start | bytes 786436
  123.3 3.7 %copy-start.13 = (f32[256,256]{1,0:T(8,128)S(1)}, f32[256,256]{1,0:T(8,128)}, u32[]{:S(2)}) copy-start(f32[256,256]{1,0:T(8,128)} %copy-done.12) | copy-start | bytes 786436
  123.3 3.7 %copy-start.15 = (f32[256,256]{1,0:T(8,128)S(1)}, f32[256,256]{1,0:T(8,128)}, u32[]{:S(2)}) copy-start(f32[256,256]{1,0:T(8,128)} %copy-done.14) | copy-start | bytes 786436
  169.2 1.0 copy-start.3
  203.8 44.3 %copy-start.1 = (s32[2048]{0:T(1024)S(1)}, s32[2048]{0:T(1024)}, u32[]{:S(2)}) copy-start(s32[2048]{0:T(1024)} %param.14) | copy-start | bytes 24580
where the time goes:
time: 249 us; the launch traced here: 248 us
  blocking collectives  129 us (52%)
  local copies, waits for them, and re-layouts  81.7 us (33%)
  other arithmetic  20.1 us (8%)
  starting transfers between devices  13.2 us (5%)
  waiting for transfers between devices  3.36 us (1%)
    psum x2, blocking collectives, squares(): return lax.psum(column_sum(residual, residual), 'gz')  80.3 us
    psum x1, blocking collectives, body(): curvature = lax.psum(column_sum(direction, image), 'gz')  39.2 us
    mul x1, local copies, waits for them, and re-layouts, band_stress(): flux_x = 0.5 * (padded[:, :, 1:-1, 2:] - padded[:, :, 1:-1, :-2])  16.5 us
    mul x1, local copies, waits for them, and re-layouts, band_stress(): flux_y = -0.5 * (padded[:, :, 2:, 1:-1] - padded[:, :, :-2, 1:-1])  16.5 us
    gather x2, local copies, waits for them, and re-layouts, band_stress(): jnp.take(flux_x.reshape(count_cols, depth, width_x * width_y), ordered, a...  16.3 us
    gather x2, local copies, waits for them, and re-layouts, band_stress(): jnp.take(flux_y.reshape(count_cols, depth, width_x * width_y), ordered, a...  16.3 us
    gather x1, local copies, waits for them, and re-layouts, band_stress(): ordered = jnp.take(band_cells, sector_order)  11.8 us
    ppermute x3, starting transfers between devices, with_halo(): lax.ppermute(lax.slice_in_dim(block, block.shape[dim] - width, None, axis...  9.37 us
  transfers between devices with their start and end apart: 6, of which 1 were waited for; matrix products, arithmetic and copies ran while one was open for 5% of the time, Pallas kernels for 0%

commit v1 on v0

v1 whole, which is shorter than its diff:
```python
import functools

import jax
import jax.numpy as jnp
from jax import lax
from jax.experimental import pallas as pl
from jax.experimental.pallas import tpu as pltpu
from jax.sharding import PartitionSpec as P

PER_SEC = 64
LANES = 128
FIELDS = 6
BLOCK = 32
M_BB, M_BW, M_WW, M_SIG, M_PP, M_PW, M_FPP, M_FPW, M_FWW = range(96, 105)

VMEM = pl.BlockSpec(memory_space=pltpu.VMEM)
SMEM = pl.BlockSpec(memory_space=pltpu.SMEM)
ANY = pl.BlockSpec(memory_space=pl.ANY)


def iota(shape, dim):
    return lax.broadcasted_iota(jnp.int32, shape, dim)


def build(x_ref, row, half, even, table):
    strength, reluct = table
    source = jnp.where(even, x_ref[0, pl.ds(row, 1), :], x_ref[0, pl.ds(row + half, 1), :])
    region = jnp.where(even, x_ref[1, pl.ds(row, 1), :], x_ref[1, pl.ds(row + half, 1), :])
    scale = strength[0]
    rho = jnp.zeros_like(source)
    for index in range(len(strength)):
        member = region == float(index + 1)
        rho = jnp.where(member, reluct[index], rho)
        if index:
            scale = jnp.where(member, strength[index], scale)
    return scale * source, rho


def load_table(tab_ref, width):
    count = tab_ref.shape[0] // 2
    rows = [jnp.concatenate([tab_ref[i]] * (width // LANES), axis=1) for i in range(2 * count)]
    return rows[:count], rows[count:]


def seams(ref, even):
    last = ref.shape[0] - 1
    edge = ref[last - 1]
    ref[0] = jnp.where(even, 0.0, pltpu.roll(edge, 1, 0))
    edge = ref[1]
    ref[last] = jnp.where(even, pltpu.roll(edge, 7, 0), 0.0)


def after(value, last_lane):
    return jnp.where(last_lane, 0.0, pltpu.roll(value, value.shape[1] - 1, 1))


def before(value, first_lane):
    return jnp.where(first_lane, 0.0, pltpu.roll(value, 1, 1))


def in_plane(value, rho, value_next, rho_next, flow_prev, first_lane, last_lane):
    flow = (rho + rho_next) * (value - value_next)
    along = (rho + after(rho, last_lane)) * (value - after(value, last_lane))
    back = jnp.where(first_lane, -rho * value, pltpu.roll(along, 1, 1))
    return (flow - flow_prev) + (along - back), flow


def own_kernel(reluct_ref, levels_ref, seeds_ref, x_ref, tab_ref, b_ref, rho_ref, part_ref):
    half, _, width = part_ref.shape
    count = reluct_ref.shape[0]
    cols = seeds_ref.shape[0]
    column = iota((8, LANES), 0) // 2
    for region in range(count):
        strength = jnp.zeros((8, LANES), jnp.float32)
        for c in range(cols):
            strength = jnp.where(column == c, levels_ref[seeds_ref[c, region]], strength)
        tab_ref[region] = strength
        tab_ref[count + region] = jnp.full((8, LANES), reluct_ref[region], jnp.float32)
    table = load_table(tab_ref, width)
    even = iota((8, width), 0) % 2 == 0
    lane = iota((8, width), 1)
    first_lane, last_lane = lane == 0, lane == width - 1

    def fill(block, carry):
        for step in range(8):
            row = block * 8 + step
            b_ref[row + 1], rho_ref[row + 1] = build(x_ref, row, half, even, table)
        return carry

    lax.fori_loop(0, half // 8, fill, 0)
    seams(b_ref, even)
    seams(rho_ref, even)

    def apply(block, carry):
        value, rho, flow = carry
        for step in range(4):
            row = block * 4 + step
            value_next, rho_next = b_ref[row + 2], rho_ref[row + 2]
            total, flow = in_plane(value, rho, value_next, rho_next, flow, first_lane, last_lane)
            part_ref[row] = value + total
            value, rho = value_next, rho_next
        return value, rho, flow

    value, rho = b_ref[1], rho_ref[1]
    flow = (rho_ref[0] + rho) * (b_ref[0] - value)
    lax.fori_loop(0, half // 4, apply, (value, rho, flow))


def lane_sum(value):
    return jnp.sum(value, axis=1, keepdims=True)


def halves_sum(value, even):
    return value + jnp.where(even, pltpu.roll(value, 7, 0), pltpu.roll(value, 1, 0))


def field_kernel(
    tab_ref, b_ref, rho_ref, part_ref, low_ref, high_ref, band_ref, order_ref,
    w_ref, b1_ref, rho1_ref, sums_ref, mom_ref,
    field_ref, band_smem, order_smem, sems,
):
    half, _, width = part_ref.shape
    copies = [
        pltpu.make_async_copy(band_ref, band_smem, sems.at[0]),
        pltpu.make_async_copy(order_ref, order_smem, sems.at[1]),
    ]
    for copy in copies:
        copy.start()
    table = load_table(tab_ref, width)
    even = iota((8, width), 0) % 2 == 0
    lane = iota((8, width), 1)
    first_lane, last_lane = lane == 0, lane == width - 1
    zero = jnp.zeros((8, width), jnp.float32)

    def finish(block, carry):
        bb, bw, ww = carry
        for step in range(4):
            row = block * 4 + step
            b, rho = b_ref[row + 1], rho_ref[row + 1]
            b_low, rho_low = build(low_ref, row, half, even, table)
            b_high, rho_high = build(high_ref, row, half, even, table)
            b1_ref[row + 1], rho1_ref[row + 1] = b_high, rho_high
            w = 0.5 * (part_ref[row] + (rho + rho_low) * (b - b_low) + (rho + rho_high) * (b - b_high))
            w_ref[row + 1] = w
            bb, bw, ww = bb + b * b, bw + b * w, ww + w * w
        return bb, bw, ww

    bb, bw, ww = lax.fori_loop(0, half // 4, finish, (zero, zero, zero))
    seams(w_ref, even)
    seams(b1_ref, even)
    seams(rho1_ref, even)
    even_tile = even[:, :LANES]
    tile = jnp.zeros((8, LANES), jnp.float32)
    bb, bw, ww = (lane_sum(total) + tile for total in (bb, bw, ww))
    whole_bw, whole_ww = halves_sum(bw, even_tile), halves_sum(ww, even_tile)
    shift = jnp.where(whole_ww > 0.0, whole_bw / whole_ww, 0.0)
    mom_ref[0], mom_ref[1], mom_ref[2] = bb, bw, ww
    mom_ref[3] = jnp.minimum(jnp.maximum(shift, 0.0), 2.0)

    normal_y = (lane.astype(jnp.float32) - 0.5 * (width - 1)) / (0.5 * width)
    upper = jnp.where(even, 0.0, 1.0)

    def forces(block, carry):
        for step in range(2):
            row = block * 2 + step
            gx_b = after(b_ref[row + 1], last_lane) - before(b_ref[row + 1], first_lane)
            gx_w = after(w_ref[row + 1], last_lane) - before(w_ref[row + 1], first_lane)
            gy_b = b_ref[row + 2] - b_ref[row]
            gy_w = w_ref[row + 2] - w_ref[row]
            normal_x = upper + (row.astype(jnp.float32) - (half - 0.5)) / half
            pairs = (
                (gx_b * gx_b - gy_b * gy_b, 2.0 * (gx_b * gy_b)),
                (2.0 * (gx_b * gx_w - gy_b * gy_w), 2.0 * (gx_b * gy_w + gx_w * gy_b)),
                (gx_w * gx_w - gy_w * gy_w, 2.0 * (gx_w * gy_w)),
            )
            for index, (diff, cross) in enumerate(pairs):
                force_x = normal_x * diff - normal_y * cross
                force_y = normal_x * cross + normal_y * diff
                for tile_index in range(width // LANES):
                    part = slice(tile_index * LANES, (tile_index + 1) * LANES)
                    at = row * (width // LANES) + tile_index
                    field_ref[at, 2 * index] = force_x[:, part]
                    field_ref[at, 2 * index + 1] = force_y[:, part]
        return carry

    lax.fori_loop(0, half // 2, forces, 0)
    for copy in copies:
        copy.wait()

    tiles = half * (width // LANES)
    place = iota((8, LANES), 1) + (iota((8, LANES), 0) % 2) * (tiles * LANES)
    lane_tile = iota((8, LANES), 1)
    count = sums_ref.shape[0]
    sectors = band_smem.shape[0] // (PER_SEC * count)
    unroll = 16

    def owner(index, carry):
        out = tile
        for sector in range(sectors):
            base = (index * sectors + sector) * PER_SEC

            def gather(block, accs):
                accs = list(accs)
                for step in range(unroll):
                    cell = band_smem[order_smem[base + block * unroll + step]]
                    at = (cell // LANES) % tiles
                    here = place == cell - at * LANES
                    for field in range(FIELDS):
                        accs[field] += jnp.where(here, field_ref[at, field], 0.0)
                return tuple(accs)

            accs = lax.fori_loop(0, PER_SEC // unroll, gather, (tile,) * FIELDS)
            for field in range(FIELDS):
                spot = (field // 2) * BLOCK + sector * 2 + field % 2
                out = jnp.where(lane_tile == spot, lane_sum(accs[field]), out)
        sums_ref[index] = out
        return carry

    lax.fori_loop(0, count, owner, 0)


def face_kernel(
    bottom_ref, tab_ref, b_ref, rho_ref, w_ref, b1_ref, rho1_ref, far_ref, sums_ref, mom_ref, out_ref
):
    half, width = b_ref.shape[0] - 2, b_ref.shape[2]
    table = load_table(tab_ref, width)
    even = iota((8, width), 0) % 2 == 0
    lane = iota((8, width), 1)
    first_lane, last_lane = lane == 0, lane == width - 1
    zero = jnp.zeros((8, width), jnp.float32)
    shift = jnp.concatenate([mom_ref[3]] * (width // LANES), axis=1)
    outside = jnp.where(first_lane, 1.0, 0.0) + bottom_ref[0]

    def rows(block, carry):
        b, w, p, rho, b1, rho1, flow, pp, pw, fpp, fpw, fww = carry
        for step in range(4):
            row = block * 4 + step
            b_next, w_next, rho_next = b_ref[row + 2], w_ref[row + 2], rho_ref[row + 2]
            p_next = b_next - shift * w_next
            b1_next, rho1_next = b1_ref[row + 2], rho1_ref[row + 2]
            b2, rho2 = build(far_ref, row, half, even, table)
            total, flow = in_plane(b1, rho1, b1_next, rho1_next, flow, first_lane, last_lane)
            w1 = 0.5 * (b1 + total + (rho1 + rho) * (b1 - b) + (rho1 + rho2) * (b1 - b2))
            w1 = jnp.where(rho1 > 0.0, w1, 0.0)
            p1 = b1 - shift * w1
            pp, pw = pp + p * p, pw + p * w
            coef = 1.0 + rho * outside
            up, uw = coef * p, coef * w
            fpp, fpw, fww = fpp + up * p, fpw + up * w, fww + uw * w
            for other_rho, other_p, other_w in (
                (rho_next, p_next, w_next),
                (after(rho, last_lane), after(p, last_lane), after(w, last_lane)),
                (rho1, p1, w1),
            ):
                weight, dp, dw = rho + other_rho, p - other_p, w - other_w
                up, uw = weight * dp, weight * dw
                fpp, fpw, fww = fpp + up * dp, fpw + up * dw, fww + uw * dw
            b, w, p, rho, b1, rho1 = b_next, w_next, p_next, rho_next, b1_next, rho1_next
        return b, w, p, rho, b1, rho1, flow, pp, pw, fpp, fpw, fww

    b, w, rho, b1, rho1 = b_ref[1], w_ref[1], rho_ref[1], b1_ref[1], rho1_ref[1]
    p = b - shift * w
    flow = (rho1_ref[0] + rho1) * (b1_ref[0] - b1)
    edge = jnp.where(even, rho, 0.0)
    first = (zero, zero, edge * p * p, edge * p * w, edge * w * w)
    carry = lax.fori_loop(0, half // 4, rows, (b, w, p, rho, b1, rho1, flow) + first)
    pp, pw, fpp, fpw, fww = carry[-5:]
    lane_tile = iota((8, LANES), 1)
    scalars = {
        M_BB: mom_ref[0], M_BW: mom_ref[1], M_WW: mom_ref[2], M_SIG: 0.5 * mom_ref[3],
        M_PP: lane_sum(pp), M_PW: lane_sum(pw),
        M_FPP: 0.5 * lane_sum(fpp), M_FPW: 0.5 * lane_sum(fpw), M_FWW: 0.5 * lane_sum(fww),
    }
    tile = jnp.zeros((8, LANES), jnp.float32)
    for spot, value in scalars.items():
        tile = jnp.where(lane_tile == spot, value, tile)
    for index in range(out_ref.shape[0]):
        out_ref[index] = sums_ref[index] + tile


def final_kernel(got_ref, b_ref, w_ref, sol_ref, force_ref):
    half, width = b_ref.shape[0] - 2, b_ref.shape[2]
    count = got_ref.shape[0]
    _, cols, sectors, _ = force_ref.shape
    even = iota((8, LANES), 0) % 2 == 0
    lane = iota((8, LANES), 1)

    def column(value, spot):
        return value[:, spot:spot + 1]

    whole = [halves_sum(got_ref[index], even) for index in range(count)]
    zeroth = functools.reduce(jnp.add, whole)
    norm = column(zeroth, M_BB)
    curve = column(zeroth, M_BW)
    step = norm / curve
    first = jnp.zeros((8, LANES), jnp.float32)
    second = first
    for value in whole:
        offset = step - column(value, M_SIG)
        scaled = offset * value
        first = first + scaled
        second = second + offset * scaled
    new = column(zeroth, M_PP) - 2.0 * column(first, M_PW) + column(second, M_WW)
    image_residual = column(zeroth, M_PW) - column(first, M_WW)
    energy = column(zeroth, M_FPP) - 2.0 * column(first, M_FPW) + column(second, M_FWW)
    ratio = new / norm
    step_two = new / (energy + 2.0 * ratio * image_residual + ratio * ratio * curve)
    alpha = step + step_two * (1.0 + ratio)
    gamma = -(step_two * step)

    wide_alpha = alpha + jnp.zeros((8, width), jnp.float32)
    wide_gamma = gamma + jnp.zeros((8, width), jnp.float32)

    def rows(block, carry):
        stack = []
        for step_index in range(8):
            row = block * 8 + step_index
            stack.append(wide_alpha * b_ref[row + 1] + wide_gamma * w_ref[row + 1])
        turned = jnp.swapaxes(jnp.stack(stack), 0, 1)
        for sub in range(8):
            sol_ref[sub, pl.ds(block * 8, 8), :] = turned[sub]
        return carry

    lax.fori_loop(0, half // 8, rows, 0)

    sign = jnp.where(lane % 2 == 0, 0.125, -0.125)
    coef = sign * jnp.where(
        lane < BLOCK, alpha * alpha, jnp.where(lane < 2 * BLOCK, alpha * gamma, gamma * gamma)
    )
    tiles = [jnp.zeros((8, LANES), jnp.float32)] * (2 * sectors)
    for index, value in enumerate(whole):
        value = coef * value
        value = value + pltpu.roll(value, LANES - BLOCK, 1) + pltpu.roll(value, LANES - 2 * BLOCK, 1)
        for spot in range(2 * sectors):
            tiles[spot] = jnp.where(lane == index, column(value, spot), tiles[spot])
    for sector in range(sectors):
        for part in range(2):
            for c in range(cols):
                force_ref[part, c, sector:sector + 1, :] = tiles[2 * sector + part][2 * c:2 * c + 1, :count]


def call(kernel, outs, in_specs, out_specs=None, scratch=(), limit=None, cost=None):
    shapes = [jax.ShapeDtypeStruct(shape, jnp.float32) for shape in outs]
    return pl.pallas_call(
        kernel,
        out_shape=shapes,
        in_specs=in_specs,
        out_specs=[VMEM] * len(outs) if out_specs is None else out_specs,
        scratch_shapes=list(scratch),
        compiler_params=pltpu.CompilerParams(vmem_limit_bytes=limit),
        cost_estimate=cost,
    )


def estimate(micros):
    return pl.CostEstimate(flops=int(micros * 1e6), transcendentals=0, bytes_accessed=int(micros * 3e6))


def body(source, regions, reluctivity, levels, seeds, band_cells, sector_order):
    count = lax.axis_size("gz")
    _, width_x, width_y = source.shape
    cols = seeds.shape[0]
    count_regions = reluctivity.shape[0]
    half = width_x // 2
    band = band_cells.shape[0]
    sectors = band // (PER_SEC * count)
    packed, padded = (half, 8, width_y), (half + 2, 8, width_y)

    own = jnp.concatenate([source, (regions + 1).astype(jnp.float32)], axis=0)
    low = lax.ppermute(own, "gz", [(i, i + 1) for i in range(count - 1)])
    high = lax.ppermute(own, "gz", [(i + 1, i) for i in range(count - 1)])
    far = lax.ppermute(own, "gz", [(i + 2, i) for i in range(count - 2)])

    table, b, rho, part = call(
        own_kernel,
        [(2 * count_regions, 8, LANES), padded, padded, packed],
        [SMEM, SMEM, SMEM, VMEM],
        cost=estimate(4),
    )(reluctivity, levels, seeds, own)
    w, b1, rho1, sums, moments = call(
        field_kernel,
        [padded, padded, padded, (count, 8, LANES), (4, 8, LANES)],
        [VMEM] * 6 + [ANY] * 2,
        scratch=[
            pltpu.VMEM((half * (width_y // LANES), FIELDS, 8, LANES), jnp.float32),
            pltpu.SMEM((band,), jnp.int32),
            pltpu.SMEM((band,), jnp.int32),
            pltpu.SemaphoreType.DMA((2,)),
        ],
        limit=24 * 2**20,
        cost=estimate(10),
    )(table, b, rho, part, low, high, band_cells, sector_order)
    bottom = (lax.axis_index("gz") == 0).astype(jnp.float32).reshape(1)
    (payload,) = call(
        face_kernel,
        [(count, 8, LANES)],
        [SMEM] + [VMEM] * 9,
        cost=estimate(4),
    )(bottom, table, b, rho, w, b1, rho1, far, sums, moments)
    got = lax.all_to_all(payload, "gz", split_axis=0, concat_axis=0, tiled=True)
    solved, forces = call(
        final_kernel,
        [(8, half, width_y), (2, cols, sectors, count)],
        [VMEM] * 3,
        cost=estimate(2),
    )(got, b, w)
    return solved.reshape(cols, 1, width_x, width_y), forces


def solution(mesh):
    in_specs = (P("gz", "pos", None), P("gz", "pos", None), P(), P(), P(), P("pos"), P("pos"))
    out_specs = (P(None, "gz", "pos", None), P(None, "pos", "gz", None))
    return jax.shard_map(body, mesh=mesh, in_specs=in_specs, out_specs=out_specs, check_vma=False)
```

time: 249 us -> 95.1 us (0.38)
  blocking collectives: 129 us -> 27.4 us
  local copies, waits for them, and re-layouts: 81.7 us -> 9.4 us
  Pallas kernels: 0 us -> 50 us
  other arithmetic: 20.1 us -> 1.97 us
  starting transfers between devices: 13.2 us -> 4.97 us
  waiting for transfers between devices: 3.36 us -> 0.01 us
    psum x3 -> x0, blocking collectives: 120 us -> none  [the longest x2 80.3 us: squares(): return lax.psum(column_sum(residual, residual), 'gz')]
    pallas_call x0 -> x4, Pallas kernels: none -> 50 us  [the longest x1 29 us: body(): call(field_kernel, [padded, padded, padded, (count, 8, LANES), (4, 8, LAN...]
    gather x5 -> x0, local copies, waits for them, and re-layouts: 44.5 us -> none  [the longest x2 16.3 us: band_stress(): jnp.take(flux_x.reshape(count_cols, depth, width_x * width_y), ordered, a...]
    mul x2 -> x0, local copies, waits for them, and re-layouts: 33 us -> none  [the longest x1 16.5 us: band_stress(): flux_x = 0.5 * (padded[:, :, 1:-1, 2:] - padded[:, :, 1:-1, :-2])]
    all_to_all x1, blocking collectives: 9.06 us -> 27.4 us  [body(): got = lax.all_to_all(payload, 'gz', split_axis=0, concat_axis=0, tiled=True)]
    ppermute x6 -> x3, starting transfers between devices: 13.2 us -> 4.97 us  [the longest x1 2.39 us: body(): low = lax.ppermute(own, 'gz', [(i, i + 1) for i in range(count - 1)])]
    unnamed x35 -> x26, local copies, waits for them, and re-layouts: 1.74 us -> 9.4 us
    reduce_sum x5 -> x0, other arithmetic: 5.86 us -> none  [the longest x3 4.91 us: column_sum(): return jnp.sum(first * second, axis=(1, 2, 3))]
  transfers between devices with their start and end apart: 6 -> 3, of which waited for: 1 -> 0; matrix products, arithmetic and copies ran while one was open for 5% -> 0% of each run, Pallas kernels for 0% -> 39%
where the time goes in v1:
time: 95.1 us; the launch traced here: 94.5 us
  Pallas kernels  50 us (53%)
  blocking collectives  27.4 us (29%)
  local copies, waits for them, and re-layouts  9.4 us (10%)
  starting transfers between devices  4.97 us (5%)
  other arithmetic  1.97 us (2%)
    pallas_call x1, Pallas kernels, body(): call(field_kernel, [padded, padded, padded, (count, 8, LANES), (4, 8, LAN...  29 us
    all_to_all x1, blocking collectives, body(): got = lax.all_to_all(payload, 'gz', split_axis=0, concat_axis=0, tiled=True)  27.4 us
    unnamed x26, local copies, waits for them, and re-layouts  9.4 us
    pallas_call x1, Pallas kernels, body(): call(face_kernel, [(count, 8, LANES)], [SMEM] + [VMEM] * 9, cost=estimate...  9.28 us
    pallas_call x1, Pallas kernels, body(): call(own_kernel, [(2 * count_regions, 8, LANES), padded, padded, packed],...  8.25 us
    pallas_call x1, Pallas kernels, body(): call(final_kernel, [(8, half, width_y), (2, cols, sectors, count)], [VMEM...  3.5 us
    ppermute x1, starting transfers between devices, body(): low = lax.ppermute(own, 'gz', [(i, i + 1) for i in range(count - 1)])  2.39 us
  transfers between devices with their start and end apart: 3, of which 0 were waited for; matrix products, arithmetic and copies ran while one was open for 0% of the time, Pallas kernels for 39%

profile of v1, /device:TPU:0, one launch (start us, length us, event | category | flops | bytes accessed | tf_op | source)
XLA Modules:
  0.0 94.5 jit_solution(16959801709955712185)
XLA Ops:
  0.6 0.0 copy-start.9
  0.6 0.0 copy-start.10
  0.7 1.0 %add_convert_fusion = f32[1,256,256]{2,1,0:T(8,128)S(1)} fusion(s32[1,256,256]{2,1,0:T(8,128)} %param.8), kind=kLoop, calls=%fused_computation.1 | loop fusion | flops 131072 | bytes 524288 | tf_op jit(solution)/shard_map/convert_element_type | solution.py:369
  1.6 1.0 %pad_maximum_fusion.x_ref = f32[2,256,256]{2,1,0:T(8,128)S(1)} fusion(f32[1,256,256]{2,1,0:T(8,128)S(1)} %add_convert_fusion, f32[1,256,256]{2,1,0:T(8,128)} %param.7), kind=kLoop, calls=%fused_computation | loop fusion | flops 131072 | bytes 1048576 | tf_op jit(solution)/shard_map/concatenate | solution.py:369
  2.6 0.0 copy-start.11
  2.6 2.4 %collective-permute-start = (f32[2,256,256]{2,1,0:T(8,128)S(1)}, f32[2,256,256]{2,1,0:T(8,128)S(1)}, u32[]{:S(2)}, u32[]{:S(2)}) collective-permute-start(f32[2,256,256]{2,1,0:T(8,128)S(1)} %pad_maximum_fusion.x_ref), channel_id=1, source_target_pairs={{0,1},{1,2},{2,3},{3,4},{4,5},{5,6},{6,7},{7,8},{8,9},{9,10},{10,1... | collective-permute-start | bytes 1572872 | tf_op jit(solution)/shard_map/ppermute | solution.py:370
  5.0 1.3 %collective-permute-start.1 = (f32[2,256,256]{2,1,0:T(8,128)S(1)}, f32[2,256,256]{2,1,0:T(8,128)S(1)}, u32[]{:S(2)}, u32[]{:S(2)}) collective-permute-start(f32[2,256,256]{2,1,0:T(8,128)S(1)} %pad_maximum_fusion.x_ref), channel_id=1, source_target_pairs={{1,0},{2,1},{3,2},{4,3},{5,4},{6,5},{7,6},{8,7},{9,8},{10,9},{11,1... | collective-permute-start | bytes 1572872 | tf_op jit(solution)/shard_map/ppermute | solution.py:371
  6.3 1.3 %collective-permute-start.2 = (f32[2,256,256]{2,1,0:T(8,128)S(1)}, f32[2,256,256]{2,1,0:T(8,128)S(1)}, u32[]{:S(2)}, u32[]{:S(2)}) collective-permute-start(f32[2,256,256]{2,1,0:T(8,128)S(1)} %pad_maximum_fusion.x_ref), channel_id=1, source_target_pairs={{2,0},{3,1},{4,2},{5,3},{6,4},{7,5},{8,6},{9,7},{10,8},{11,9},{12,... | collective-permute-start | bytes 1572872 | tf_op jit(solution)/shard_map/ppermute | solution.py:372
  7.6 0.0 copy-done.11
  7.7 8.2 %shard_map.86 = (f32[8,8,128]{2,1,0:T(8,128)}, f32[130,8,256]{2,1,0:T(8,128)}, f32[130,8,256]{2,1,0:T(8,128)}, f32[128,8,256]{2,1,0:T(8,128)}) custom-call(f32[4]{0:T(128)} %reluct_ref.1, f32[4]{0:T(128)} %levels_ref.1, s32[4,4]{1,0:T(4,128)} %seeds_ref.1, f32[2,256,256]{2,1,0:T(8,128)} %copy-done.11), custom_call_target="tpu_custom_call" | custom-call | flops 4000000 | bytes 12000000 | tf_op jit(solution)/shard_map/pallas_call | solution.py:374
  15.9 0.0 collective-permute-done.low_ref
  15.9 0.0 collective-permute-done.1.high_ref
  15.9 0.0 copy-done.9
  15.9 0.0 copy-done.10
  15.9 0.0 copy-start
  15.9 1.2 %copy-done = f32[130,8,256]{2,1,0:T(8,128)S(1)} copy-done((f32[130,8,256]{2,1,0:T(8,128)S(1)}, f32[130,8,256]{2,1,0:T(8,128)}, u32[]{:S(2)}) %copy-start) | copy-done | bytes 1064984
  17.2 0.0 copy-start.2
  17.2 1.2 %copy-done.2 = f32[130,8,256]{2,1,0:T(8,128)S(1)} copy-done((f32[130,8,256]{2,1,0:T(8,128)S(1)}, f32[130,8,256]{2,1,0:T(8,128)}, u32[]{:S(2)}) %copy-start.2) | copy-done | bytes 1064984
  18.4 0.0 copy-start.5
  18.4 1.2 %copy-done.5 = f32[128,8,256]{2,1,0:T(8,128)S(1)} copy-done((f32[128,8,256]{2,1,0:T(8,128)S(1)}, f32[128,8,256]{2,1,0:T(8,128)}, u32[]{:S(2)}) %copy-start.5) | copy-done | bytes 1048600
  19.6 0.0 copy-start.6
  19.6 0.8 copy-done.6
  20.4 29.0 %shard_map.87 = (f32[130,8,256]{2,1,0:T(8,128)S(1)}, f32[130,8,256]{2,1,0:T(8,128)S(1)}, f32[130,8,256]{2,1,0:T(8,128)S(1)}, f32[16,8,128]{2,1,0:T(8,128)S(1)}, f32[4,8,128]{2,1,0:T(8,128)S(1)}) custom-call(f32[8,8,128]{2,1,0:T(8,128)S(1)} %copy-done.6, f32[130,8,256]{2,1,0:T(8,128)S(1)} %copy-done, f32[130,8,256]{2,1,0:T(8,128)S(1)} %copy-done.2, ...), custom_call_target="tpu_custom_call" | custom-call | flops 10000000 | bytes 30000000 | tf_op jit(solution)/shard_map/pallas_call | solution.py:380
  49.3 0.0 copy-start.1
  49.4 1.0 %copy-done.1 = f32[130,8,256]{2,1,0:T(8,128)} copy-done((f32[130,8,256]{2,1,0:T(8,128)}, f32[130,8,256]{2,1,0:T(8,128)S(1)}, u32[]{:S(2)}) %copy-start.1) | copy-done | bytes 1064984
  50.3 0.0 copy-start.3
  50.3 1.0 %copy-done.3 = f32[130,8,256]{2,1,0:T(8,128)} copy-done((f32[130,8,256]{2,1,0:T(8,128)}, f32[130,8,256]{2,1,0:T(8,128)S(1)}, u32[]{:S(2)}) %copy-start.3) | copy-done | bytes 1064984
  51.3 0.0 copy-start.4
  51.3 1.0 %copy-done.4 = f32[130,8,256]{2,1,0:T(8,128)} copy-done((f32[130,8,256]{2,1,0:T(8,128)}, f32[130,8,256]{2,1,0:T(8,128)S(1)}, u32[]{:S(2)}) %copy-start.4) | copy-done | bytes 1064984
  52.3 0.0 copy-start.7
  52.3 0.6 copy-done.7
  52.9 0.0 copy-start.8
  52.9 0.6 copy-done.8
  53.5 0.0 collective-permute-done.2.far_ref
  53.5 0.0 copy-start.12
  53.5 0.8 copy-done.12
  54.3 9.3 %shard_map.88 = f32[16,8,128]{2,1,0:T(8,128)} custom-call(f32[1]{0:T(128)} %bitcast.bottom_ref, f32[8,8,128]{2,1,0:T(8,128)} %get-tuple-element.13.tab_ref, f32[130,8,256]{2,1,0:T(8,128)} %get-tuple-element.14.b_ref, f32[130,8,256]{2,1,0:T(8,128)} %get-tuple-element.15.rho_ref, f32[130,8,256]{2,1,0:T(8,128)} %copy-done.1, f32[130,8,256]{2,1,0:T(8,128)} %copy-done.3, ...), custom_call_target="tpu_custom_call" | custom-call | flops 4000000 | bytes 12000000 | tf_op jit(solution)/shard_map/pallas_call | solution.py:394
  63.6 27.4 %all_to_all.5.got_ref = f32[16,8,128]{2,1,0:T(8,128)} all-to-all(f32[16,8,128]{2,1,0:T(8,128)} %shard_map.88), channel_id=1, replica_groups=mesh['pos'=2,'gz'=16] {'gz'}, dimensions={0} | all-to-all | bytes 131072 | tf_op jit(solution)/shard_map/all_to_all | solution.py:400
  91.0 3.5 %shard_map.89 = (f32[8,128,256]{2,1,0:T(8,128)}, f32[2,4,2,16]{3,2,1,0:T(2,128)}) custom-call(f32[16,8,128]{2,1,0:T(8,128)} %all_to_all.5.got_ref, f32[130,8,256]{2,1,0:T(8,128)} %get-tuple-element.14.b_ref, f32[130,8,256]{2,1,0:T(8,128)} %copy-done.1), custom_call_target="tpu_custom_call" | custom-call | flops 2000000 | bytes 6000000 | tf_op jit(solution)/shard_map/pallas_call | solution.py:401
Async XLA Ops:
  0.6 15.3 %copy-start.9 = (s32[2048]{0:T(1024)S(1)}, s32[2048]{0:T(1024)}, u32[]{:S(2)}) copy-start(s32[2048]{0:T(1024)} %band_ref.1) | copy-start | bytes 24580
  0.6 15.3 %copy-start.10 = (s32[2048]{0:T(1024)S(1)}, s32[2048]{0:T(1024)}, u32[]{:S(2)}) copy-start(s32[2048]{0:T(1024)} %order_ref.1) | copy-start | bytes 24580
  2.6 5.0 %copy-start.11 = (f32[2,256,256]{2,1,0:T(8,128)}, f32[2,256,256]{2,1,0:T(8,128)S(1)}, u32[]{:S(2)}) copy-start(f32[2,256,256]{2,1,0:T(8,128)S(1)} %pad_maximum_fusion.x_ref) | copy-start | bytes 1572868
  2.6 13.3 %collective-permute-start = (f32[2,256,256]{2,1,0:T(8,128)S(1)}, f32[2,256,256]{2,1,0:T(8,128)S(1)}, u32[]{:S(2)}, u32[]{:S(2)}) collective-permute-start(f32[2,256,256]{2,1,0:T(8,128)S(1)} %pad_maximum_fusion.x_ref), channel_id=1, source_target_pairs={{0,1},{1,2},{2,3},{3,4},{4,5},{5,6},{6,7},{7,8},{8,9},{9,10},{10,1... | collective-permute-start | bytes 1572872 | tf_op jit(solution)/shard_map/ppermute | solution.py:370
  5.0 10.9 %collective-permute-start.1 = (f32[2,256,256]{2,1,0:T(8,128)S(1)}, f32[2,256,256]{2,1,0:T(8,128)S(1)}, u32[]{:S(2)}, u32[]{:S(2)}) collective-permute-start(f32[2,256,256]{2,1,0:T(8,128)S(1)} %pad_maximum_fusion.x_ref), channel_id=1, source_target_pairs={{1,0},{2,1},{3,2},{4,3},{5,4},{6,5},{7,6},{8,7},{9,8},{10,9},{11,1... | collective-permute-start | bytes 1572872 | tf_op jit(solution)/shard_map/ppermute | solution.py:371
  6.3 47.2 %collective-permute-start.2 = (f32[2,256,256]{2,1,0:T(8,128)S(1)}, f32[2,256,256]{2,1,0:T(8,128)S(1)}, u32[]{:S(2)}, u32[]{:S(2)}) collective-permute-start(f32[2,256,256]{2,1,0:T(8,128)S(1)} %pad_maximum_fusion.x_ref), channel_id=1, source_target_pairs={{2,0},{3,1},{4,2},{5,3},{6,4},{7,5},{8,6},{9,7},{10,8},{11,9},{12,... | collective-permute-start | bytes 1572872 | tf_op jit(solution)/shard_map/ppermute | solution.py:372
  15.9 1.2 %copy-start = (f32[130,8,256]{2,1,0:T(8,128)S(1)}, f32[130,8,256]{2,1,0:T(8,128)}, u32[]{:S(2)}) copy-start(f32[130,8,256]{2,1,0:T(8,128)} %get-tuple-element.14.b_ref) | copy-start | bytes 3194884
  17.2 1.2 %copy-start.2 = (f32[130,8,256]{2,1,0:T(8,128)S(1)}, f32[130,8,256]{2,1,0:T(8,128)}, u32[]{:S(2)}) copy-start(f32[130,8,256]{2,1,0:T(8,128)} %get-tuple-element.15.rho_ref) | copy-start | bytes 3194884
  18.4 1.2 %copy-start.5 = (f32[128,8,256]{2,1,0:T(8,128)S(1)}, f32[128,8,256]{2,1,0:T(8,128)}, u32[]{:S(2)}) copy-start(f32[128,8,256]{2,1,0:T(8,128)} %get-tuple-element.16.part_ref) | copy-start | bytes 3145732
  19.6 0.8 copy-start.6
  49.3 1.0 %copy-start.1 = (f32[130,8,256]{2,1,0:T(8,128)}, f32[130,8,256]{2,1,0:T(8,128)S(1)}, u32[]{:S(2)}) copy-start(f32[130,8,256]{2,1,0:T(8,128)S(1)} %get-tuple-element.17.w_ref) | copy-start | bytes 3194884
  50.3 1.0 %copy-start.3 = (f32[130,8,256]{2,1,0:T(8,128)}, f32[130,8,256]{2,1,0:T(8,128)S(1)}, u32[]{:S(2)}) copy-start(f32[130,8,256]{2,1,0:T(8,128)S(1)} %get-tuple-element.18.b1_ref) | copy-start | bytes 3194884
  51.3 1.0 %copy-start.4 = (f32[130,8,256]{2,1,0:T(8,128)}, f32[130,8,256]{2,1,0:T(8,128)S(1)}, u32[]{:S(2)}) copy-start(f32[130,8,256]{2,1,0:T(8,128)S(1)} %get-tuple-element.19.rho1_ref) | copy-start | bytes 3194884
  52.3 0.6 copy-start.7
  52.9 0.6 copy-start.8
  53.5 0.8 copy-start.12

commit v2 on v1

v2 whole, which is shorter than its diff:
```python
import functools

import jax
import jax.numpy as jnp
from jax import lax
from jax.experimental import pallas as pl
from jax.experimental.pallas import tpu as pltpu
from jax.sharding import PartitionSpec as P

PER_SEC = 64
LANES = 128
BLOCK = 32
M_BB, M_BW, M_WW, M_SIG, M_PP, M_PW, M_FPP, M_FPW, M_FWW = range(96, 105)

VMEM = pl.BlockSpec(memory_space=pltpu.VMEM)
SMEM = pl.BlockSpec(memory_space=pltpu.SMEM)
ANY = pl.BlockSpec(memory_space=pl.ANY)


def iota(shape, dim):
    return lax.broadcasted_iota(jnp.int32, shape, dim)


def build(x_ref, row, half, even, table):
    strength, reluct = table
    source = jnp.where(even, x_ref[0, pl.ds(row, 1), :], x_ref[0, pl.ds(row + half, 1), :])
    region = jnp.where(even, x_ref[1, pl.ds(row, 1), :], x_ref[1, pl.ds(row + half, 1), :])
    scale = strength[0]
    rho = jnp.zeros_like(source)
    for index in range(len(strength)):
        member = region == float(index + 1)
        rho = jnp.where(member, reluct[index], rho)
        if index:
            scale = jnp.where(member, strength[index], scale)
    return scale * source, rho


def load_table(tab_ref, width):
    count = tab_ref.shape[0] // 2
    rows = [jnp.concatenate([tab_ref[i]] * (width // LANES), axis=1) for i in range(2 * count)]
    return rows[:count], rows[count:]


def seams(ref, even):
    last = ref.shape[0] - 1
    edge = ref[last - 1]
    ref[0] = jnp.where(even, 0.0, pltpu.roll(edge, 1, 0))
    edge = ref[1]
    ref[last] = jnp.where(even, pltpu.roll(edge, 7, 0), 0.0)


def after(value, last_lane):
    return jnp.where(last_lane, 0.0, pltpu.roll(value, value.shape[1] - 1, 1))


def before(value, first_lane):
    return jnp.where(first_lane, 0.0, pltpu.roll(value, 1, 1))


def in_plane(value, rho, value_next, rho_next, flow_prev, first_lane, last_lane):
    flow = (rho + rho_next) * (value - value_next)
    along = (rho + after(rho, last_lane)) * (value - after(value, last_lane))
    back = jnp.where(first_lane, -rho * value, pltpu.roll(along, 1, 1))
    return (flow - flow_prev) + (along - back), flow


def own_kernel(reluct_ref, levels_ref, seeds_ref, x_ref, tab_ref, b_ref, rho_ref, part_ref):
    half, _, width = part_ref.shape
    count = reluct_ref.shape[0]
    cols = seeds_ref.shape[0]
    column = iota((8, LANES), 0) // 2
    for region in range(count):
        strength = jnp.zeros((8, LANES), jnp.float32)
        for c in range(cols):
            strength = jnp.where(column == c, levels_ref[seeds_ref[c, region]], strength)
        tab_ref[region] = strength
        tab_ref[count + region] = jnp.full((8, LANES), reluct_ref[region], jnp.float32)
    table = load_table(tab_ref, width)
    even = iota((8, width), 0) % 2 == 0
    lane = iota((8, width), 1)
    first_lane, last_lane = lane == 0, lane == width - 1

    def fill(block, carry):
        for step in range(8):
            row = block * 8 + step
            b_ref[row + 1], rho_ref[row + 1] = build(x_ref, row, half, even, table)
        return carry

    lax.fori_loop(0, half // 8, fill, 0)
    seams(b_ref, even)
    seams(rho_ref, even)

    def apply(block, carry):
        value, rho, flow = carry
        for step in range(16):
            row = block * 16 + step
            value_next, rho_next = b_ref[row + 2], rho_ref[row + 2]
            total, flow = in_plane(value, rho, value_next, rho_next, flow, first_lane, last_lane)
            part_ref[row] = value + total
            value, rho = value_next, rho_next
        return value, rho, flow

    value, rho = b_ref[1], rho_ref[1]
    flow = (rho_ref[0] + rho) * (b_ref[0] - value)
    lax.fori_loop(0, half // 16, apply, (value, rho, flow))


def lane_sum(value):
    return jnp.sum(value, axis=1, keepdims=True)


def halves_sum(value, even):
    return value + jnp.where(even, pltpu.roll(value, 7, 0), pltpu.roll(value, 1, 0))


def image_kernel(
    tab_ref, b_ref, rho_ref, part_ref, low_ref, high_ref, w_ref, b1_ref, rho1_ref, mom_ref
):
    half, _, width = part_ref.shape
    table = load_table(tab_ref, width)
    even = iota((8, width), 0) % 2 == 0
    zero = jnp.zeros((8, width), jnp.float32)

    def finish(block, carry):
        bb, bw, ww = carry
        for step in range(8):
            row = block * 8 + step
            b, rho = b_ref[row + 1], rho_ref[row + 1]
            b_low, rho_low = build(low_ref, row, half, even, table)
            b_high, rho_high = build(high_ref, row, half, even, table)
            b1_ref[row], rho1_ref[row] = b_high, rho_high
            w = 0.5 * (part_ref[row] + (rho + rho_low) * (b - b_low) + (rho + rho_high) * (b - b_high))
            w_ref[row] = w
            bb, bw, ww = bb + b * b, bw + b * w, ww + w * w
        return bb, bw, ww

    bb, bw, ww = lax.fori_loop(0, half // 8, finish, (zero, zero, zero))
    even_tile = even[:, :LANES]
    tile = jnp.zeros((8, LANES), jnp.float32)
    bb, bw, ww = (lane_sum(total) + tile for total in (bb, bw, ww))
    whole_bw, whole_ww = halves_sum(bw, even_tile), halves_sum(ww, even_tile)
    shift = jnp.where(whole_ww > 0.0, whole_bw / whole_ww, 0.0)
    mom_ref[0], mom_ref[1], mom_ref[2] = bb, bw, ww
    mom_ref[3] = jnp.minimum(jnp.maximum(shift, 0.0), 2.0)


def band_kernel(
    b_ref, w_ref, band_ref, order_ref, sums_ref, field_ref, band_smem, order_smem, sems
):
    half, _, width = w_ref.shape
    copies = [
        pltpu.make_async_copy(band_ref, band_smem, sems.at[0]),
        pltpu.make_async_copy(order_ref, order_smem, sems.at[1]),
    ]
    for copy in copies:
        copy.start()
    even = iota((8, width), 0) % 2 == 0
    lane = iota((8, width), 1)
    first_lane, last_lane = lane == 0, lane == width - 1
    normal_y = (lane.astype(jnp.float32) - 0.5 * (width - 1)) / (0.5 * width)
    upper = jnp.where(even, 0.0, 1.0)
    across = width // LANES
    lower_tiles = half * across

    def spread(row, low, high):
        b, w = b_ref[row + 1], w_ref[row]
        gx_b = after(b, last_lane) - before(b, first_lane)
        gx_w = after(w, last_lane) - before(w, first_lane)
        gy_b = b_ref[row + 2] - b_ref[row]
        gy_w = high - low
        normal_x = upper + (jnp.asarray(row).astype(jnp.float32) - (half - 0.5)) / half
        pairs = (
            (gx_b * gx_b - gy_b * gy_b, 2.0 * (gx_b * gy_b)),
            (2.0 * (gx_b * gx_w - gy_b * gy_w), 2.0 * (gx_b * gy_w + gx_w * gy_b)),
            (gx_w * gx_w - gy_w * gy_w, 2.0 * (gx_w * gy_w)),
        )
        for index, (diff, cross) in enumerate(pairs):
            force_x = normal_x * diff - normal_y * cross
            force_y = normal_x * cross + normal_y * diff
            lower = jnp.where(even, force_x, pltpu.roll(force_y, 1, 0))
            higher = jnp.where(even, pltpu.roll(force_x, 7, 0), force_y)
            for tile_index in range(across):
                part = slice(tile_index * LANES, (tile_index + 1) * LANES)
                at = row * across + tile_index
                field_ref[at, index] = lower[:, part]
                field_ref[lower_tiles + at, index] = higher[:, part]

    def forces(block, carry):
        for step in range(8):
            row = block * 8 + step
            spread(row, w_ref[row - 1], w_ref[row + 1])
        return carry

    edge = jnp.where(even, 0.0, pltpu.roll(w_ref[half - 1], 1, 0))
    for row in range(8):
        spread(row, w_ref[row - 1] if row else edge, w_ref[row + 1])
    lax.fori_loop(1, half // 8 - 1, forces, 0)
    edge = jnp.where(even, pltpu.roll(w_ref[0], 7, 0), 0.0)
    for row in range(half - 8, half):
        spread(row, w_ref[row - 1], w_ref[row + 1] if row + 1 < half else edge)
    for copy in copies:
        copy.wait()

    place = iota((8, LANES), 1)
    tile = jnp.zeros((8, LANES), jnp.float32)
    count = sums_ref.shape[0]
    sectors = band_smem.shape[0] // (PER_SEC * count)

    def owner(index, carry):
        out = tile
        for sector in range(sectors):
            base = (index * sectors + sector) * PER_SEC
            accs = [tile] * 3
            for step in range(PER_SEC):
                cell = band_smem[order_smem[base + step]]
                at = lax.shift_right_logical(cell, jnp.int32(7))
                here = place == (cell & (LANES - 1))
                for field in range(3):
                    accs[field] += jnp.where(here, field_ref[at, field], 0.0)
            for field in range(3):
                out = jnp.where(place == field * BLOCK + sector, lane_sum(accs[field]), out)
        sums_ref[index] = out
        return carry

    lax.fori_loop(0, count, owner, 0)


def face_kernel(bottom_ref, b_ref, rho_ref, w_ref, b1_ref, rho1_ref, w1_ref, sums_ref, mom_ref, out_ref):
    half, _, width = w_ref.shape
    even = iota((8, width), 0) % 2 == 0
    lane = iota((8, width), 1)
    first_lane, last_lane = lane == 0, lane == width - 1
    zero = jnp.zeros((8, width), jnp.float32)
    shift = jnp.concatenate([mom_ref[3]] * (width // LANES), axis=1)
    outside = jnp.where(first_lane, 1.0, 0.0) + bottom_ref[0]

    def row_sums(row, w_next, carry):
        w, p, rho, pp, pw, fpp, fpw, fww = carry
        rho_next = rho_ref[row + 2]
        p_next = b_ref[row + 2] - shift * w_next
        rho1, w1 = rho1_ref[row], w1_ref[row]
        p1 = b1_ref[row] - shift * w1
        pp, pw = pp + p * p, pw + p * w
        coef = 1.0 + rho * outside
        up, uw = coef * p, coef * w
        fpp, fpw, fww = fpp + up * p, fpw + up * w, fww + uw * w
        for other_rho, other_p, other_w in (
            (rho_next, p_next, w_next),
            (after(rho, last_lane), after(p, last_lane), after(w, last_lane)),
            (rho1, p1, w1),
        ):
            weight, dp, dw = rho + other_rho, p - other_p, w - other_w
            up, uw = weight * dp, weight * dw
            fpp, fpw, fww = fpp + up * dp, fpw + up * dw, fww + uw * dw
        return w_next, p_next, rho_next, pp, pw, fpp, fpw, fww

    def rows(block, carry):
        for step in range(8):
            row = block * 8 + step
            carry = row_sums(row, w_ref[row + 1], carry)
        return carry

    w, rho = w_ref[0], rho_ref[1]
    p = b_ref[1] - shift * w
    edge = jnp.where(even, rho, 0.0)
    carry = (w, p, rho, zero, zero, edge * p * p, edge * p * w, edge * w * w)
    carry = lax.fori_loop(0, half // 8 - 1, rows, carry)
    last = jnp.where(even, pltpu.roll(w, 7, 0), 0.0)
    for row in range(half - 8, half):
        carry = row_sums(row, w_ref[row + 1] if row + 1 < half else last, carry)
    pp, pw, fpp, fpw, fww = carry[-5:]
    lane_tile = iota((8, LANES), 1)
    scalars = {
        M_BB: mom_ref[0], M_BW: mom_ref[1], M_WW: mom_ref[2], M_SIG: 0.5 * mom_ref[3],
        M_PP: lane_sum(pp), M_PW: lane_sum(pw),
        M_FPP: 0.5 * lane_sum(fpp), M_FPW: 0.5 * lane_sum(fpw), M_FWW: 0.5 * lane_sum(fww),
    }
    tile = jnp.zeros((8, LANES), jnp.float32)
    for spot, value in scalars.items():
        tile = jnp.where(lane_tile == spot, value, tile)
    for index in range(out_ref.shape[0]):
        out_ref[index] = sums_ref[index] + tile


def final_kernel(got_ref, b_ref, w_ref, sol_ref, force_ref):
    half, _, width = w_ref.shape
    count = got_ref.shape[0]
    _, cols, sectors, _ = force_ref.shape
    even = iota((8, LANES), 0) % 2 == 0
    lane = iota((8, LANES), 1)

    def column(value, spot):
        return value[:, spot:spot + 1]

    whole = [halves_sum(got_ref[index], even) for index in range(count)]
    zeroth = functools.reduce(jnp.add, whole)
    norm = column(zeroth, M_BB)
    curve = column(zeroth, M_BW)
    step = norm / curve
    first = jnp.zeros((8, LANES), jnp.float32)
    second = first
    for value in whole:
        offset = step - column(value, M_SIG)
        scaled = offset * value
        first = first + scaled
        second = second + offset * scaled
    new = column(zeroth, M_PP) - 2.0 * column(first, M_PW) + column(second, M_WW)
    image_residual = column(zeroth, M_PW) - column(first, M_WW)
    energy = column(zeroth, M_FPP) - 2.0 * column(first, M_FPW) + column(second, M_FWW)
    ratio = new / norm
    step_two = new / (energy + 2.0 * ratio * image_residual + ratio * ratio * curve)
    alpha = step + step_two * (1.0 + ratio)
    gamma = -(step_two * step)

    wide_alpha = alpha + jnp.zeros((8, width), jnp.float32)
    wide_gamma = gamma + jnp.zeros((8, width), jnp.float32)

    def rows(block, carry):
        stack = []
        for step_index in range(8):
            row = block * 8 + step_index
            stack.append(wide_alpha * b_ref[row + 1] + wide_gamma * w_ref[row])
        turned = jnp.swapaxes(jnp.stack(stack), 0, 1)
        for sub in range(8):
            sol_ref[sub, pl.ds(block * 8, 8), :] = turned[sub]
        return carry

    lax.fori_loop(0, half // 8, rows, 0)

    sign = jnp.where(even, 0.125, -0.125)
    coef = sign * jnp.where(
        lane < BLOCK, alpha * alpha, jnp.where(lane < 2 * BLOCK, alpha * gamma, gamma * gamma)
    )
    tiles = [jnp.zeros((8, LANES), jnp.float32)] * sectors
    for index in range(count):
        value = coef * got_ref[index]
        value = value + pltpu.roll(value, LANES - BLOCK, 1) + pltpu.roll(value, LANES - 2 * BLOCK, 1)
        for sector in range(sectors):
            tiles[sector] = jnp.where(lane == index, column(value, sector), tiles[sector])
    for sector in range(sectors):
        for part in range(2):
            for c in range(cols):
                at = 2 * c + part
                force_ref[part, c, sector:sector + 1, :] = tiles[sector][at:at + 1, :count]


def call(kernel, outs, in_specs, out_specs=None, scratch=(), limit=16 * 2**20, cost=None):
    shapes = [jax.ShapeDtypeStruct(shape, jnp.float32) for shape in outs]
    return pl.pallas_call(
        kernel,
        out_shape=shapes,
        in_specs=in_specs,
        out_specs=[VMEM] * len(outs) if out_specs is None else out_specs,
        scratch_shapes=list(scratch),
        compiler_params=pltpu.CompilerParams(vmem_limit_bytes=limit),
        cost_estimate=cost,
    )


def estimate(micros):
    return pl.CostEstimate(flops=int(micros * 1e6), transcendentals=0, bytes_accessed=int(micros * 3e6))


def body(source, regions, reluctivity, levels, seeds, band_cells, sector_order):
    count = lax.axis_size("gz")
    _, width_x, width_y = source.shape
    cols = seeds.shape[0]
    count_regions = reluctivity.shape[0]
    half = width_x // 2
    band = band_cells.shape[0]
    sectors = band // (PER_SEC * count)
    packed, padded = (half, 8, width_y), (half + 2, 8, width_y)

    layer = lax.broadcasted_iota(jnp.int32, (2, width_x, width_y), 0)
    own = jnp.where(layer == 0, source, (regions + 1).astype(jnp.float32))
    low = lax.ppermute(own, "gz", [(i, i + 1) for i in range(count - 1)])
    high = lax.ppermute(own, "gz", [(i + 1, i) for i in range(count - 1)])

    table, b, rho, part = call(
        own_kernel,
        [(2 * count_regions, 8, LANES), padded, padded, packed],
        [SMEM, SMEM, SMEM, VMEM],
        cost=estimate(4),
    )(reluctivity, levels, seeds, own)
    w, b1, rho1, moments = call(
        image_kernel,
        [packed, packed, packed, (4, 8, LANES)],
        [VMEM] * 6,
        cost=estimate(2),
    )(table, b, rho, part, low, high)
    w1 = lax.ppermute(w, "gz", [(i + 1, i) for i in range(count - 1)])
    (sums,) = call(
        band_kernel,
        [(count, 8, LANES)],
        [VMEM] * 2 + [ANY] * 2,
        scratch=[
            pltpu.VMEM((width_x * (width_y // LANES), 3, 8, LANES), jnp.float32),
            pltpu.SMEM((band,), jnp.int32),
            pltpu.SMEM((band,), jnp.int32),
            pltpu.SemaphoreType.DMA((2,)),
        ],
        cost=estimate(7),
    )(b, w, band_cells, sector_order)
    bottom = (lax.axis_index("gz") == 0).astype(jnp.float32).reshape(1)
    (payload,) = call(
        face_kernel,
        [(count, 8, LANES)],
        [SMEM] + [VMEM] * 8,
        cost=estimate(3),
    )(bottom, b, rho, w, b1, rho1, w1, sums, moments)
    got = lax.all_to_all(payload, "gz", split_axis=0, concat_axis=0, tiled=True)
    solved, forces = call(
        final_kernel,
        [(8, half, width_y), (2, cols, sectors, count)],
        [VMEM] * 3,
        cost=estimate(2),
    )(got, b, w)
    return solved.reshape(cols, 1, width_x, width_y), forces


def solution(mesh):
    in_specs = (P("gz", "pos", None), P("gz", "pos", None), P(), P(), P(), P("pos"), P("pos"))
    out_specs = (P(None, "gz", "pos", None), P(None, "pos", "gz", None))
    return jax.shard_map(body, mesh=mesh, in_specs=in_specs, out_specs=out_specs, check_vma=False)
```

time: 95.1 us -> 58 us (0.61)
  Pallas kernels: 50 us -> 18.5 us
  local copies, waits for them, and re-layouts: 9.4 us -> 1.98 us
  waiting for transfers between devices: 0.01 us -> 4.48 us
  blocking collectives: 27.4 us -> 24.9 us
    pallas_call x2 -> x3, Pallas kernels: 38.2 us -> 13.4 us  [the longest x1 8.33 us: body(): call(band_kernel, [(count, 8, LANES)], [VMEM] * 2 + [ANY] * 2, scratch=[p...]
    unnamed x26 -> x18, local copies, waits for them, and re-layouts: 9.4 us -> 1.98 us
    pallas_call x1, Pallas kernels: 8.25 us -> 3.01 us  [body(): call(own_kernel, [(2 * count_regions, 8, LANES), padded, padded, packed],...]
    ppermute x1, waiting for transfers between devices: 0.01 us -> 2.92 us  [body(): w1 = lax.ppermute(w, 'gz', [(i + 1, i) for i in range(count - 1)])]
    all_to_all x1, blocking collectives: 27.4 us -> 24.9 us  [body(): got = lax.all_to_all(payload, 'gz', split_axis=0, concat_axis=0, tiled=True)]
    ppermute x1, waiting for transfers between devices: 0.01 us -> 1.56 us  [body(): high = lax.ppermute(own, 'gz', [(i + 1, i) for i in range(count - 1)])]
    pallas_call x1, Pallas kernels: 3.5 us -> 2.08 us  [body(): call(final_kernel, [(8, half, width_y), (2, cols, sectors, count)], [VMEM...]
    select_n x0 -> x1, other arithmetic: none -> 1.06 us  [body(): own = jnp.where(layer == 0, source, (regions + 1).astype(jnp.float32))]
  transfers between devices with their start and end apart: 3 -> 3, of which waited for: 0 -> 2; matrix products, arithmetic and copies ran while one was open for 0% -> 0% of each run, Pallas kernels for 39% -> 20%
where the time goes in v2:
time: 58 us; the launch traced here: 57.7 us
  blocking collectives  24.9 us (43%)
  Pallas kernels  18.5 us (32%)
  starting transfers between devices  4.96 us (9%)
  waiting for transfers between devices  4.48 us (8%)
  other arithmetic  2.04 us (4%)
  local copies, waits for them, and re-layouts  1.98 us (3%)
  between operations  0.78 us (1%)
    all_to_all x1, blocking collectives, body(): got = lax.all_to_all(payload, 'gz', split_axis=0, concat_axis=0, tiled=True)  24.9 us
    pallas_call x1, Pallas kernels, body(): call(band_kernel, [(count, 8, LANES)], [VMEM] * 2 + [ANY] * 2, scratch=[p...  8.33 us
    pallas_call x1, Pallas kernels, body(): call(face_kernel, [(count, 8, LANES)], [SMEM] + [VMEM] * 8, cost=estimate...  3.39 us
    pallas_call x1, Pallas kernels, body(): call(own_kernel, [(2 * count_regions, 8, LANES), padded, padded, packed],...  3.01 us
    ppermute x1, waiting for transfers between devices, body(): w1 = lax.ppermute(w, 'gz', [(i + 1, i) for i in range(count - 1)])  2.92 us
    ppermute x1, starting transfers between devices, body(): low = lax.ppermute(own, 'gz', [(i, i + 1) for i in range(count - 1)])  2.39 us
    pallas_call x1, Pallas kernels, body(): call(final_kernel, [(8, half, width_y), (2, cols, sectors, count)], [VMEM...  2.08 us
    unnamed x18, local copies, waits for them, and re-layouts  1.98 us
  transfers between devices with their start and end apart: 3, of which 2 were waited for; matrix products, arithmetic and copies ran while one was open for 0% of the time, Pallas kernels for 20%

profile of v2, /device:TPU:0, one launch (start us, length us, event | category | flops | bytes accessed | tf_op | source)
XLA Modules:
  0.0 57.7 jit_solution(3198451409521550655)
XLA Ops:
  0.6 0.0 copy-start.8
  0.6 0.0 copy-start.6
  0.7 0.0 copy-start.7
  0.7 1.0 %convert_bitcast_fusion = f32[256,256]{1,0:T(8,128)S(1)} fusion(s32[1,256,256]{2,1,0:T(8,128)} %param.8), kind=kLoop, calls=%fused_computation.1 | loop fusion | flops 131072 | bytes 524288 | tf_op jit(solution)/shard_map/jit(_where)/broadcast_in_dim | solution.py:375
  1.7 1.1 %broadcast_select_fusion.x_ref = f32[2,256,256]{2,1,0:T(8,128)S(1)} fusion(f32[256,256]{1,0:T(8,128)S(1)} %convert_bitcast_fusion, f32[256,256]{1,0:T(8,128)} %bitcast.7, pred[2]{0:T(512)(128)(4,1)S(1)} %iota_compare_fusion), kind=kLoop, calls=%fused_computation | loop fusion | flops 131072 | bytes 1048578 | tf_op jit(solution)/shard_map/jit(_where)/select_n | solution.py:375
  2.7 2.4 %collective-permute-start = (f32[2,256,256]{2,1,0:T(8,128)S(1)}, f32[2,256,256]{2,1,0:T(8,128)S(1)}, u32[]{:S(2)}, u32[]{:S(2)}) collective-permute-start(f32[2,256,256]{2,1,0:T(8,128)S(1)} %broadcast_select_fusion.x_ref), channel_id=1, source_target_pairs={{0,1},{1,2},{2,3},{3,4},{4,5},{5,6},{6,7},{7,8},{8,9},{9,10},{10,1... | collective-permute-start | bytes 1572872 | tf_op jit(solution)/shard_map/ppermute | solution.py:376
  5.1 1.3 %collective-permute-start.1 = (f32[2,256,256]{2,1,0:T(8,128)S(1)}, f32[2,256,256]{2,1,0:T(8,128)S(1)}, u32[]{:S(2)}, u32[]{:S(2)}) collective-permute-start(f32[2,256,256]{2,1,0:T(8,128)S(1)} %broadcast_select_fusion.x_ref), channel_id=1, source_target_pairs={{1,0},{2,1},{3,2},{4,3},{5,4},{6,5},{7,6},{8,7},{9,8},{10,9},{11,1... | collective-permute-start | bytes 1572872 | tf_op jit(solution)/shard_map/ppermute | solution.py:377
  6.4 0.0 copy-done.8
  6.4 0.0 copy-done.6
  6.4 0.0 copy-done.7
  6.4 3.0 %shard_map.86 = (f32[8,8,128]{2,1,0:T(8,128)S(1)}, f32[130,8,256]{2,1,0:T(8,128)S(1)}, f32[130,8,256]{2,1,0:T(8,128)S(1)}, f32[128,8,256]{2,1,0:T(8,128)S(1)}) custom-call(f32[4]{0:T(128)S(1)} %copy-done.7, f32[4]{0:T(128)S(1)} %copy-done.8, s32[4,4]{1,0:T(4,128)S(1)} %copy-done.6, f32[2,256,256]{2,1,0:T(8,128)S(1)} %broadcast_select_fusion.x_ref), custom_call_target="tpu_custom_call" | custom-call | flops 4000000 | bytes 12000000 | tf_op jit(solution)/shard_map/pallas_call | solution.py:379
  9.5 0.0 collective-permute-done.low_ref
  9.5 1.6 %collective-permute-done.1.high_ref = f32[2,256,256]{2,1,0:T(8,128)S(1)} collective-permute-done((f32[2,256,256]{2,1,0:T(8,128)S(1)}, f32[2,256,256]{2,1,0:T(8,128)S(1)}, u32[]{:S(2)}, u32[]{:S(2)}) %collective-permute-start.1) | collective-permute-done | bytes 524320 | tf_op jit(solution)/shard_map/ppermute | solution.py:377
  11.0 0.0 copy-start.4
  11.0 0.0 copy-start.5
  11.0 1.7 %shard_map.87 = (f32[128,8,256]{2,1,0:T(8,128)S(1)}, f32[128,8,256]{2,1,0:T(8,128)S(1)}, f32[128,8,256]{2,1,0:T(8,128)S(1)}, f32[4,8,128]{2,1,0:T(8,128)S(1)}) custom-call(f32[8,8,128]{2,1,0:T(8,128)S(1)} %get-tuple-element.14.tab_ref, f32[130,8,256]{2,1,0:T(8,128)S(1)} %get-tuple-element.12.b_ref, f32[130,8,256]{2,1,0:T(8,128)S(1)} %get-tuple-element.13.rho_ref, ...), custom_call_target="tpu_custom_call" | custom-call | flops 2000000 | bytes 6000000 | tf_op jit(solution)/shard_map/pallas_call | solution.py:385
  12.7 0.0 copy-start
  12.8 1.0 %copy-done = f32[128,8,256]{2,1,0:T(8,128)} copy-done((f32[128,8,256]{2,1,0:T(8,128)}, f32[128,8,256]{2,1,0:T(8,128)S(1)}, u32[]{:S(2)}) %copy-start) | copy-done | bytes 1048600
  13.7 0.0 copy-start.2
  13.7 1.0 %copy-done.2 = f32[128,8,256]{2,1,0:T(8,128)} copy-done((f32[128,8,256]{2,1,0:T(8,128)}, f32[128,8,256]{2,1,0:T(8,128)S(1)}, u32[]{:S(2)}) %copy-start.2) | copy-done | bytes 1048600
  14.7 1.3 %collective-permute-start.2 = (f32[128,8,256]{2,1,0:T(8,128)S(1)}, f32[128,8,256]{2,1,0:T(8,128)}, u32[]{:S(2)}, u32[]{:S(2)}) collective-permute-start(f32[128,8,256]{2,1,0:T(8,128)S(1)} %get-tuple-element.16.w_ref), channel_id=1, source_target_pairs={{1,0},{2,1},{3,2},{4,3},{5,4},{6,5},{7,6},{8,7},{9,8},{10,9},{11,1... | collective-permute-start | bytes 3145736 | tf_op jit(solution)/shard_map/ppermute | solution.py:391
  16.0 0.0 copy-done.4
  16.0 0.0 copy-done.5
  16.0 0.0 copy-start.1
  16.0 0.0 copy-start.3
  16.0 8.3 %shard_map.88.sums_ref = f32[16,8,128]{2,1,0:T(8,128)S(1)} custom-call(f32[130,8,256]{2,1,0:T(8,128)S(1)} %get-tuple-element.12.b_ref, f32[128,8,256]{2,1,0:T(8,128)S(1)} %get-tuple-element.16.w_ref, s32[2048]{0:T(1024)S(1)} %copy-done.4, s32[2048]{0:T(1024)S(1)} %copy-done.5), custom_call_target="tpu_custom_call" | custom-call | flops 7000000 | bytes 21000000 | tf_op jit(solution)/shard_map/pallas_call | solution.py:392
  24.4 2.9 %collective-permute-done.2.w1_ref = f32[128,8,256]{2,1,0:T(8,128)} collective-permute-done((f32[128,8,256]{2,1,0:T(8,128)S(1)}, f32[128,8,256]{2,1,0:T(8,128)}, u32[]{:S(2)}, u32[]{:S(2)}) %collective-permute-start.2) | collective-permute-done | bytes 1048608 | tf_op jit(solution)/shard_map/ppermute | solution.py:391
  27.3 0.0 copy-done.1
  27.3 0.0 copy-done.3
  27.3 3.4 %shard_map.89 = f32[16,8,128]{2,1,0:T(8,128)S(1)} custom-call(f32[1]{0:T(128)} %bitcast.bottom_ref, f32[130,8,256]{2,1,0:T(8,128)S(1)} %get-tuple-element.12.b_ref, f32[130,8,256]{2,1,0:T(8,128)S(1)} %get-tuple-element.13.rho_ref, f32[128,8,256]{2,1,0:T(8,128)S(1)} %get-tuple-element.16.w_ref, f32[128,8,256]{2,1,0:T(8,128)S(1)} %copy-done.1, ...), custom_call_target="tpu_custom_call" | custom-call | flops 3000000 | bytes 9000000 | tf_op jit(solution)/shard_map/pallas_call | solution.py:405
  30.7 24.9 %all_to_all.5.got_ref = f32[16,8,128]{2,1,0:T(8,128)S(1)} all-to-all(f32[16,8,128]{2,1,0:T(8,128)S(1)} %shard_map.89), channel_id=1, replica_groups=mesh['pos'=2,'gz'=16] {'gz'}, dimensions={0} | all-to-all | bytes 131072 | tf_op jit(solution)/shard_map/all_to_all | solution.py:411
  55.6 2.1 %shard_map.90 = (f32[8,128,256]{2,1,0:T(8,128)}, f32[2,4,2,16]{3,2,1,0:T(2,128)}) custom-call(f32[16,8,128]{2,1,0:T(8,128)S(1)} %all_to_all.5.got_ref, f32[130,8,256]{2,1,0:T(8,128)S(1)} %get-tuple-element.12.b_ref, f32[128,8,256]{2,1,0:T(8,128)S(1)} %get-tuple-element.16.w_ref), custom_call_target="tpu_custom_call" | custom-call | flops 2000000 | bytes 6000000 | tf_op jit(solution)/shard_map/pallas_call | solution.py:412
  (1 shorter events, 0.0 us)
Async XLA Ops:
  0.6 5.8 %copy-start.8 = (f32[4]{0:T(128)S(1)}, f32[4]{0:T(128)}, u32[]{:S(2)}) copy-start(f32[4]{0:T(128)} %levels_ref.1) | copy-start | bytes 52
  0.6 5.8 %copy-start.6 = (s32[4,4]{1,0:T(4,128)S(1)}, s32[4,4]{1,0:T(4,128)}, u32[]{:S(2)}) copy-start(s32[4,4]{1,0:T(4,128)} %seeds_ref.1) | copy-start | bytes 196
  0.7 5.8 %copy-start.7 = (f32[4]{0:T(128)S(1)}, f32[4]{0:T(128)}, u32[]{:S(2)}) copy-start(f32[4]{0:T(128)} %reluct_ref.1) | copy-start | bytes 52
  2.7 6.7 %collective-permute-start = (f32[2,256,256]{2,1,0:T(8,128)S(1)}, f32[2,256,256]{2,1,0:T(8,128)S(1)}, u32[]{:S(2)}, u32[]{:S(2)}) collective-permute-start(f32[2,256,256]{2,1,0:T(8,128)S(1)} %broadcast_select_fusion.x_ref), channel_id=1, source_target_pairs={{0,1},{1,2},{2,3},{3,4},{4,5},{5,6},{6,7},{7,8},{8,9},{9,10},{10,1... | collective-permute-start | bytes 1572872 | tf_op jit(solution)/shard_map/ppermute | solution.py:376
  5.1 5.9 %collective-permute-start.1 = (f32[2,256,256]{2,1,0:T(8,128)S(1)}, f32[2,256,256]{2,1,0:T(8,128)S(1)}, u32[]{:S(2)}, u32[]{:S(2)}) collective-permute-start(f32[2,256,256]{2,1,0:T(8,128)S(1)} %broadcast_select_fusion.x_ref), channel_id=1, source_target_pairs={{1,0},{2,1},{3,2},{4,3},{5,4},{6,5},{7,6},{8,7},{9,8},{10,9},{11,1... | collective-permute-start | bytes 1572872 | tf_op jit(solution)/shard_map/ppermute | solution.py:377
  11.0 5.0 %copy-start.4 = (s32[2048]{0:T(1024)S(1)}, s32[2048]{0:T(1024)}, u32[]{:S(2)}) copy-start(s32[2048]{0:T(1024)} %band_ref.1) | copy-start | bytes 24580
  11.0 5.0 %copy-start.5 = (s32[2048]{0:T(1024)S(1)}, s32[2048]{0:T(1024)}, u32[]{:S(2)}) copy-start(s32[2048]{0:T(1024)} %order_ref.1) | copy-start | bytes 24580
  12.7 1.0 %copy-start = (f32[128,8,256]{2,1,0:T(8,128)}, f32[128,8,256]{2,1,0:T(8,128)S(1)}, u32[]{:S(2)}) copy-start(f32[128,8,256]{2,1,0:T(8,128)S(1)} %get-tuple-element.17.b1_ref) | copy-start | bytes 3145732
  13.7 1.0 %copy-start.2 = (f32[128,8,256]{2,1,0:T(8,128)}, f32[128,8,256]{2,1,0:T(8,128)S(1)}, u32[]{:S(2)}) copy-start(f32[128,8,256]{2,1,0:T(8,128)S(1)} %get-tuple-element.18.rho1_ref) | copy-start | bytes 3145732
  14.7 12.6 %collective-permute-start.2 = (f32[128,8,256]{2,1,0:T(8,128)S(1)}, f32[128,8,256]{2,1,0:T(8,128)}, u32[]{:S(2)}, u32[]{:S(2)}) collective-permute-start(f32[128,8,256]{2,1,0:T(8,128)S(1)} %get-tuple-element.16.w_ref), channel_id=1, source_target_pairs={{1,0},{2,1},{3,2},{4,3},{5,4},{6,5},{7,6},{8,7},{9,8},{10,9},{11,1... | collective-permute-start | bytes 3145736 | tf_op jit(solution)/shard_map/ppermute | solution.py:391
  16.0 11.3 %copy-start.1 = (f32[128,8,256]{2,1,0:T(8,128)S(1)}, f32[128,8,256]{2,1,0:T(8,128)}, u32[]{:S(2)}) copy-start(f32[128,8,256]{2,1,0:T(8,128)} %copy-done) | copy-start | bytes 3145732
  16.0 11.3 %copy-start.3 = (f32[128,8,256]{2,1,0:T(8,128)S(1)}, f32[128,8,256]{2,1,0:T(8,128)}, u32[]{:S(2)}) copy-start(f32[128,8,256]{2,1,0:T(8,128)} %copy-done.2) | copy-start | bytes 3145732

commit v3 on v2

--- a/solution.py
+++ b/solution.py
@@ -10,21 +10,28 @@
 PER_SEC = 64
 LANES = 128
 BLOCK = 32
+TILE_ROWS = 24
 M_BB, M_BW, M_WW, M_SIG, M_PP, M_PW, M_FPP, M_FPW, M_FWW = range(96, 105)
 
 VMEM = pl.BlockSpec(memory_space=pltpu.VMEM)
 SMEM = pl.BlockSpec(memory_space=pltpu.SMEM)
 ANY = pl.BlockSpec(memory_space=pl.ANY)
+HBM = pl.BlockSpec(memory_space=pltpu.HBM)
 
 
 def iota(shape, dim):
     return lax.broadcasted_iota(jnp.int32, shape, dim)
 
 
-def build(x_ref, row, half, even, table):
+def build(x_refs, row, half, even, table):
     strength, reluct = table
-    source = jnp.where(even, x_ref[0, pl.ds(row, 1), :], x_ref[0, pl.ds(row + half, 1), :])
-    region = jnp.where(even, x_ref[1, pl.ds(row, 1), :], x_ref[1, pl.ds(row + half, 1), :])
+
+    def pick(part):
+        lower = sum(x_ref[part, pl.ds(row, 1), :] for x_ref in x_refs)
+        upper = sum(x_ref[part, pl.ds(row + half, 1), :] for x_ref in x_refs)
+        return jnp.where(even, lower, upper)
+
+    source, region = pick(0), pick(1)
     scale = strength[0]
     rho = jnp.zeros_like(source)
     for index in range(len(strength)):
@@ -64,7 +71,32 @@
     return (flow - flow_prev) + (along - back), flow
 
 
-def own_kernel(reluct_ref, levels_ref, seeds_ref, x_ref, tab_ref, b_ref, rho_ref, part_ref):
+def fetch(pairs, sems):
+    copies = [pltpu.make_async_copy(src, dst, sems.at[i]) for i, (src, dst) in enumerate(pairs)]
+    for copy in copies:
+        copy.start()
+    return copies
+
+
+def pack_kernel(source_ref, regions_ref, x_ref, region_buf, sems):
+    rows = x_ref.shape[1] // 4
+    spans = [pl.ds(part * rows, rows) for part in range(4)]
+    pairs = [(source_ref.at[0], x_ref.at[0])]
+    pairs += [(regions_ref.at[0, at], region_buf.at[at]) for at in spans]
+    copies = fetch(pairs, sems)
+    for at, copy in zip(spans, copies[1:]):
+        copy.wait()
+        x_ref[1, at, :] = (region_buf[at, :] + 1).astype(jnp.float32)
+    copies[0].wait()
+
+
+def own_kernel(
+    reluct_hbm, levels_hbm, seeds_hbm, x_ref, tab_ref, b_ref, rho_ref, part_ref,
+    reluct_ref, levels_ref, seeds_ref, sems,
+):
+    pairs = [(reluct_hbm, reluct_ref), (levels_hbm, levels_ref), (seeds_hbm, seeds_ref)]
+    for copy in fetch(pairs, sems):
+        copy.wait()
     half, _, width = part_ref.shape
     count = reluct_ref.shape[0]
     cols = seeds_ref.shape[0]
@@ -83,7 +115,7 @@
     def fill(block, carry):
         for step in range(8):
             row = block * 8 + step
-            b_ref[row + 1], rho_ref[row + 1] = build(x_ref, row, half, even, table)
+            b_ref[row + 1], rho_ref[row + 1] = build((x_ref,), row, half, even, table)
         return carry
 
     lax.fori_loop(0, half // 8, fill, 0)
@@ -105,6 +137,38 @@
     lax.fori_loop(0, half // 16, apply, (value, rho, flow))
 
 
+def upper_kernel(tab_ref, b_ref, rho_ref, high_ref, part_ref, b1_ref, rho1_ref):
+    half, _, width = part_ref.shape
+    table = load_table(tab_ref, width)
+    even = iota((8, width), 0) % 2 == 0
+    lane = iota((8, width), 1)
+    first_lane, last_lane = lane == 0, lane == width - 1
+
+    def fill(block, carry):
+        for step in range(8):
+            row = block * 8 + step
+            b1_ref[row + 1], rho1_ref[row + 1] = build((high_ref,), row, half, even, table)
+        return carry
+
+    lax.fori_loop(0, half // 8, fill, 0)
+    seams(b1_ref, even)
+    seams(rho1_ref, even)
+
+    def apply(block, carry):
+        value, rho, flow = carry
+        for step in range(16):
+            row = block * 16 + step
+            value_next, rho_next = b1_ref[row + 2], rho1_ref[row + 2]
+            total, flow = in_plane(value, rho, value_next, rho_next, flow, first_lane, last_lane)
+            part_ref[row] = value + total + (rho + rho_ref[row + 1]) * (value - b_ref[row + 1])
+            value, rho = value_next, rho_next
+        return value, rho, flow
+
+    value, rho = b1_ref[1], rho1_ref[1]
+    flow = (rho1_ref[0] + rho) * (b1_ref[0] - value)
+    lax.fori_loop(0, half // 16, apply, (value, rho, flow))
+
+
 def lane_sum(value):
     return jnp.sum(value, axis=1, keepdims=True)
 
@@ -114,7 +178,7 @@
 
 
 def image_kernel(
-    tab_ref, b_ref, rho_ref, part_ref, low_ref, high_ref, w_ref, b1_ref, rho1_ref, mom_ref
+    tab_ref, b_ref, rho_ref, part_ref, low_ref, high_ref, w_ref, mom_ref
 ):
     half, _, width = part_ref.shape
     table = load_table(tab_ref, width)
@@ -126,12 +190,12 @@
         for step in range(8):
             row = block * 8 + step
             b, rho = b_ref[row + 1], rho_ref[row + 1]
-            b_low, rho_low = build(low_ref, row, half, even, table)
-            b_high, rho_high = build(high_ref, row, half, even, table)
-            b1_ref[row], rho1_ref[row] = b_high, rho_high
+            b_low, rho_low = build((low_ref,), row, half, even, table)
+            b_high, rho_high = build((high_ref,), row, half, even, table)
             w = 0.5 * (part_ref[row] + (rho + rho_low) * (b - b_low) + (rho + rho_high) * (b - b_high))
             w_ref[row] = w
             bb, bw, ww = bb + b * b, bw + b * w, ww + w * w
+        mom_ref[4] = jnp.where(rho_low[:, :LANES] > 0.0, 0.0, 1.0)
         return bb, bw, ww
 
     bb, bw, ww = lax.fori_loop(0, half // 8, finish, (zero, zero, zero))
@@ -145,15 +209,10 @@
 
 
 def band_kernel(
-    b_ref, w_ref, band_ref, order_ref, sums_ref, field_ref, band_smem, order_smem, sems
+    b_ref, w_ref, band_hbm, order_hbm, sums_ref, field_ref, acc_ref, band_smem, order_smem, sems
 ):
     half, _, width = w_ref.shape
-    copies = [
-        pltpu.make_async_copy(band_ref, band_smem, sems.at[0]),
-        pltpu.make_async_copy(order_ref, order_smem, sems.at[1]),
-    ]
-    for copy in copies:
-        copy.start()
+    copies = fetch([(band_hbm, band_smem), (order_hbm, order_smem)], sems)
     even = iota((8, width), 0) % 2 == 0
     lane = iota((8, width), 1)
     first_lane, last_lane = lane == 0, lane == width - 1
@@ -182,8 +241,9 @@
             for tile_index in range(across):
                 part = slice(tile_index * LANES, (tile_index + 1) * LANES)
                 at = row * across + tile_index
-                field_ref[at, index] = lower[:, part]
-                field_ref[lower_tiles + at, index] = higher[:, part]
+                for base, value in ((0, lower), (lower_tiles, higher)):
+                    first = pl.multiple_of((base + at) * TILE_ROWS + 8 * index, 8)
+                    field_ref[pl.ds(first, 8), :] = value[:, part]
 
     def forces(block, carry):
         for step in range(8):
@@ -206,40 +266,51 @@
     count = sums_ref.shape[0]
     sectors = band_smem.shape[0] // (PER_SEC * count)
 
-    def owner(index, carry):
+    def gather(sector, carry):
+        accs = [tile] * 3
+        for step in range(PER_SEC):
+            cell = band_smem[order_smem[sector * PER_SEC + step]]
+            here = place == (cell & (LANES - 1))
+            start = lax.shift_right_logical(cell, jnp.int32(7)) * TILE_ROWS
+            for field in range(3):
+                first = pl.multiple_of(start + 8 * field, 8)
+                accs[field] += jnp.where(here, field_ref[pl.ds(first, 8), :], 0.0)
+        for field in range(3):
+            acc_ref[sector * 3 + field] = accs[field]
+        return carry
+
+    lax.fori_loop(0, count * sectors, gather, 0)
+    for index in range(count):
         out = tile
         for sector in range(sectors):
-            base = (index * sectors + sector) * PER_SEC
-            accs = [tile] * 3
-            for step in range(PER_SEC):
-                cell = band_smem[order_smem[base + step]]
-                at = lax.shift_right_logical(cell, jnp.int32(7))
-                here = place == (cell & (LANES - 1))
-                for field in range(3):
-                    accs[field] += jnp.where(here, field_ref[at, field], 0.0)
             for field in range(3):
-                out = jnp.where(place == field * BLOCK + sector, lane_sum(accs[field]), out)
+                total = lane_sum(acc_ref[(index * sectors + sector) * 3 + field])
+                out = jnp.where(place == field * BLOCK + sector, total, out)
         sums_ref[index] = out
-        return carry
-
-    lax.fori_loop(0, count, owner, 0)
-
-
-def face_kernel(bottom_ref, b_ref, rho_ref, w_ref, b1_ref, rho1_ref, w1_ref, sums_ref, mom_ref, out_ref):
+
+
+def face_kernel(
+    tab_ref, b_ref, rho_ref, w_ref, high_ref, upper_ref, far_ref, relay_ref, sums_ref, mom_ref,
+    out_ref,
+):
     half, _, width = w_ref.shape
+    table = load_table(tab_ref, width)
     even = iota((8, width), 0) % 2 == 0
     lane = iota((8, width), 1)
     first_lane, last_lane = lane == 0, lane == width - 1
     zero = jnp.zeros((8, width), jnp.float32)
     shift = jnp.concatenate([mom_ref[3]] * (width // LANES), axis=1)
-    outside = jnp.where(first_lane, 1.0, 0.0) + bottom_ref[0]
+    outside = jnp.where(first_lane, 1.0, 0.0) + jnp.concatenate([mom_ref[4]] * (width // LANES), axis=1)
 
     def row_sums(row, w_next, carry):
         w, p, rho, pp, pw, fpp, fpw, fww = carry
         rho_next = rho_ref[row + 2]
         p_next = b_ref[row + 2] - shift * w_next
-        rho1, w1 = rho1_ref[row], w1_ref[row]
-        p1 = b1_ref[row] - shift * w1
+        b1, rho1 = build((high_ref,), row, half, even, table)
+        b2, rho2 = build((far_ref, relay_ref), row, half, even, table)
+        w1 = 0.5 * (upper_ref[row] + (rho1 + rho2) * (b1 - b2))
+        w1 = jnp.where(rho1 > 0.0, w1, 0.0)
+        p1 = b1 - shift * w1
         pp, pw = pp + p * p, pw + p * w
         coef = 1.0 + rho * outside
         up, uw = coef * p, coef * w
@@ -265,7 +336,7 @@
     edge = jnp.where(even, rho, 0.0)
     carry = (w, p, rho, zero, zero, edge * p * p, edge * p * w, edge * w * w)
     carry = lax.fori_loop(0, half // 8 - 1, rows, carry)
-    last = jnp.where(even, pltpu.roll(w, 7, 0), 0.0)
+    last = jnp.where(even, pltpu.roll(w_ref[0], 7, 0), 0.0)
     for row in range(half - 8, half):
         carry = row_sums(row, w_ref[row + 1] if row + 1 < half else last, carry)
     pp, pw, fpp, fpw, fww = carry[-5:]
@@ -344,8 +415,11 @@
                 force_ref[part, c, sector:sector + 1, :] = tiles[sector][at:at + 1, :count]
 
 
-def call(kernel, outs, in_specs, out_specs=None, scratch=(), limit=16 * 2**20, cost=None):
-    shapes = [jax.ShapeDtypeStruct(shape, jnp.float32) for shape in outs]
+def call(kernel, outs, in_specs, out_specs=None, scratch=(), limit=4 * 2**20, cost=None):
+    shapes = [
+        out if isinstance(out, jax.ShapeDtypeStruct) else jax.ShapeDtypeStruct(out, jnp.float32)
+        for out in outs
+    ]
     return pl.pallas_call(
         kernel,
         out_shape=shapes,
@@ -357,6 +431,13 @@
     )
 
 
+ORDER = lax.optimization_barrier
+
+
+def in_hbm(value):
+    return pltpu.with_memory_space_constraint(value, pltpu.HBM)
+
+
 def estimate(micros):
     return pl.CostEstimate(flops=int(micros * 1e6), transcendentals=0, bytes_accessed=int(micros * 3e6))
 
@@ -371,43 +452,66 @@
     sectors = band // (PER_SEC * count)
     packed, padded = (half, 8, width_y), (half + 2, 8, width_y)
 
-    layer = lax.broadcasted_iota(jnp.int32, (2, width_x, width_y), 0)
-    own = jnp.where(layer == 0, source, (regions + 1).astype(jnp.float32))
-    low = lax.ppermute(own, "gz", [(i, i + 1) for i in range(count - 1)])
+
+    dma = pltpu.SemaphoreType.DMA
+
+    (own,) = call(
+        pack_kernel,
+        [(2, width_x, width_y)],
+        [HBM] * 2,
+        scratch=[pltpu.VMEM((width_x, width_y), jnp.int32), dma((5,))],
+    )(in_hbm(source), in_hbm(regions))
     high = lax.ppermute(own, "gz", [(i + 1, i) for i in range(count - 1)])
-
     table, b, rho, part = call(
         own_kernel,
         [(2 * count_regions, 8, LANES), padded, padded, packed],
-        [SMEM, SMEM, SMEM, VMEM],
-        cost=estimate(4),
-    )(reluctivity, levels, seeds, own)
-    w, b1, rho1, moments = call(
+        [HBM] * 3 + [VMEM],
+        scratch=[
+            pltpu.SMEM(reluctivity.shape, jnp.float32),
+            pltpu.SMEM(levels.shape, jnp.float32),
+            pltpu.SMEM(seeds.shape, jnp.int32),
+            dma((3,)),
+        ],
+        cost=estimate(3),
+    )(in_hbm(reluctivity), in_hbm(levels), in_hbm(seeds), own)
+    own_second, table = ORDER((own, table))
+    low = lax.ppermute(own_second, "gz", [(i, i + 1) for i in range(count - 1)])
+    (upper,) = call(
+        upper_kernel,
+        [packed],
+        [VMEM] * 4,
+        scratch=[pltpu.VMEM(padded, jnp.float32)] * 2,
+        cost=estimate(3),
+    )(table, b, rho, high)
+    upper, own_third, high_second = ORDER((upper, own_second, high))
+    far = lax.ppermute(own_third, "gz", [(i + 2, i) for i in range(1, count - 2, 2)])
+    relay = lax.ppermute(high_second, "gz", [(i + 1, i) for i in range(0, count - 1, 2)])
+    w, moments = call(
         image_kernel,
-        [packed, packed, packed, (4, 8, LANES)],
+        [packed, (5, 8, LANES)],
         [VMEM] * 6,
         cost=estimate(2),
     )(table, b, rho, part, low, high)
-    w1 = lax.ppermute(w, "gz", [(i + 1, i) for i in range(count - 1)])
     (sums,) = call(
         band_kernel,
         [(count, 8, LANES)],
-        [VMEM] * 2 + [ANY] * 2,
+        [VMEM] * 2 + [HBM] * 2,
         scratch=[
-            pltpu.VMEM((width_x * (width_y // LANES), 3, 8, LANES), jnp.float32),
+            pltpu.VMEM((width_x * (width_y // LANES) * TILE_ROWS, LANES), jnp.float32),
+            pltpu.VMEM((band // PER_SEC * 3, 8, LANES), jnp.float32),
             pltpu.SMEM((band,), jnp.int32),
             pltpu.SMEM((band,), jnp.int32),
-            pltpu.SemaphoreType.DMA((2,)),
+            dma((2,)),
         ],
-        cost=estimate(7),
-    )(b, w, band_cells, sector_order)
-    bottom = (lax.axis_index("gz") == 0).astype(jnp.float32).reshape(1)
+        limit=10 * 2**20,
+        cost=estimate(5),
+    )(b, w, in_hbm(band_cells), in_hbm(sector_order))
     (payload,) = call(
         face_kernel,
         [(count, 8, LANES)],
-        [SMEM] + [VMEM] * 8,
-        cost=estimate(3),
-    )(bottom, b, rho, w, b1, rho1, w1, sums, moments)
+        [VMEM] * 10,
+        cost=estimate(4),
+    )(table, b, rho, w, high, upper, far, relay, sums, moments)
     got = lax.all_to_all(payload, "gz", split_axis=0, concat_axis=0, tiled=True)
     solved, forces = call(
         final_kernel,

time: 58 us -> 47.7 us (0.82)
  blocking collectives: 24.9 us -> 18.9 us
  waiting for transfers between devices: 4.48 us -> 0.01 us
  Pallas kernels: 18.5 us -> 21.5 us
  other arithmetic: 2.04 us -> 0 us
  local copies, waits for them, and re-layouts: 1.98 us -> 0 us
  starting transfers between devices: 4.96 us -> 6.33 us
    all_to_all x1, blocking collectives: 24.9 us -> 18.9 us  [body(): got = lax.all_to_all(payload, 'gz', split_axis=0, concat_axis=0, tiled=True)]
    ppermute x2 -> x3, waiting for transfers between devices: 2.92 us -> 0.01 us  [the longest x1 0.01 us: body(): low = lax.ppermute(own_second, 'gz', [(i, i + 1) for i in range(count - 1)])]
    pallas_call x3 -> x5, Pallas kernels: 13.4 us -> 16.2 us  [the longest x1 7.46 us: body(): call(band_kernel, [(count, 8, LANES)], [VMEM] * 2 + [HBM] * 2, scratch=[p...]
    unnamed x18 -> x0, local copies, waits for them, and re-layouts: 1.98 us -> none
    ppermute x1, waiting for transfers between devices: 1.56 us -> 0.01 us  [body(): high = lax.ppermute(own, 'gz', [(i + 1, i) for i in range(count - 1)])]
    ppermute x2 -> x3, starting transfers between devices: 3.67 us -> 5.04 us  [the longest x1 3.06 us: body(): low = lax.ppermute(own_second, 'gz', [(i, i + 1) for i in range(count - 1)])]
    select_n x1 -> x0, other arithmetic: 1.06 us -> none  [body(): own = jnp.where(layer == 0, source, (regions + 1).astype(jnp.float32))]
    broadcast_in_dim x1 -> x0, other arithmetic: 0.98 us -> none  [body(): own = jnp.where(layer == 0, source, (regions + 1).astype(jnp.float32))]
  transfers between devices with their start and end apart: 3 -> 4, of which waited for: 2 -> 0; matrix products, arithmetic and copies ran while one was open for 0% -> 0% of each run, Pallas kernels for 20% -> 31%
where the time goes in v3:
time: 47.7 us; the launch traced here: 47.4 us
  Pallas kernels  21.5 us (45%)
  blocking collectives  18.9 us (40%)
  starting transfers between devices  6.33 us (13%)
  between operations  0.72 us (2%)
    all_to_all x1, blocking collectives, body(): got = lax.all_to_all(payload, 'gz', split_axis=0, concat_axis=0, tiled=True)  18.9 us
    pallas_call x1, Pallas kernels, body(): call(band_kernel, [(count, 8, LANES)], [VMEM] * 2 + [HBM] * 2, scratch=[p...  7.46 us
    pallas_call x1, Pallas kernels, body(): call(face_kernel, [(count, 8, LANES)], [VMEM] * 10, cost=estimate(4))  3.62 us
    pallas_call x1, Pallas kernels, body(): call(own_kernel, [(2 * count_regions, 8, LANES), padded, padded, packed],...  3.17 us
    ppermute x1, starting transfers between devices, body(): low = lax.ppermute(own_second, 'gz', [(i, i + 1) for i in range(count - 1)])  3.06 us
    pallas_call x1, Pallas kernels, body(): call(upper_kernel, [packed], [VMEM] * 4, scratch=[pltpu.VMEM(padded, jnp....  2.42 us
    pallas_call x1, Pallas kernels, body(): call(final_kernel, [(8, half, width_y), (2, cols, sectors, count)], [VMEM...  2.08 us
    pallas_call x1, Pallas kernels, body(): call(image_kernel, [packed, (5, 8, LANES)], [VMEM] * 6, cost=estimate(2))  1.69 us
  transfers between devices with their start and end apart: 4, of which 0 were waited for; matrix products, arithmetic and copies ran while one was open for 0% of the time, Pallas kernels for 31%

profile of v3, /device:TPU:0, one launch (start us, length us, event | category | flops | bytes accessed | tf_op | source)
XLA Modules:
  0.0 47.4 jit_solution(12604298842364539889)
XLA Ops:
  0.6 1.1 %shard_map.86.x_ref = f32[2,256,256]{2,1,0:T(8,128)S(1)} custom-call(f32[1,256,256]{2,1,0:T(8,128)} %source_ref.1, s32[1,256,256]{2,1,0:T(8,128)} %regions_ref.1), custom_call_target="tpu_custom_call" | custom-call | tf_op jit(solution)/shard_map/pallas_call | solution.py:458
  1.7 1.3 %collective-permute-start.1 = (f32[2,256,256]{2,1,0:T(8,128)S(1)}, f32[2,256,256]{2,1,0:T(8,128)S(1)}, u32[]{:S(2)}, u32[]{:S(2)}) collective-permute-start(f32[2,256,256]{2,1,0:T(8,128)S(1)} %shard_map.86.x_ref), channel_id=1, source_target_pairs={{1,0},{2,1},{3,2},{4,3},{5,4},{6,5},{7,6},{8,7},{9,8},{10,9},{11,1... | collective-permute-start | bytes 1572872 | tf_op jit(solution)/shard_map/ppermute | solution.py:464
  3.0 3.2 %shard_map.87 = (f32[8,8,128]{2,1,0:T(8,128)S(1)}, f32[130,8,256]{2,1,0:T(8,128)S(1)}, f32[130,8,256]{2,1,0:T(8,128)S(1)}, f32[128,8,256]{2,1,0:T(8,128)S(1)}) custom-call(f32[4]{0:T(128)} %reluct_hbm.1, f32[4]{0:T(128)} %levels_hbm.1, s32[4,4]{1,0:T(4,128)} %seeds_hbm.1, f32[2,256,256]{2,1,0:T(8,128)S(1)} %shard_map.86.x_ref), custom_call_target="tpu_custom_call" | custom-call | flops 3000000 | bytes 9000000 | tf_op jit(solution)/shard_map/pallas_call | solution.py:465
  6.2 3.1 %collective-permute-start = (f32[2,256,256]{2,1,0:T(8,128)S(1)}, f32[2,256,256]{2,1,0:T(8,128)S(1)}, u32[]{:S(2)}, u32[]{:S(2)}) collective-permute-start(f32[2,256,256]{2,1,0:T(8,128)S(1)} %shard_map.86.x_ref), channel_id=1, source_target_pairs={{0,1},{1,2},{2,3},{3,4},{4,5},{5,6},{6,7},{7,8},{8,9},{9,10},{10,1... | collective-permute-start | bytes 1572872 | tf_op jit(solution)/shard_map/ppermute | solution.py:478
  9.3 0.0 collective-permute-done.1.high_ref
  9.3 2.4 %shard_map.89.upper_ref = f32[128,8,256]{2,1,0:T(8,128)S(1)} custom-call(f32[8,8,128]{2,1,0:T(8,128)S(1)} %get-tuple-element.16.tab_ref, f32[130,8,256]{2,1,0:T(8,128)S(1)} %get-tuple-element.17.b_ref, f32[130,8,256]{2,1,0:T(8,128)S(1)} %get-tuple-element.18.rho_ref, f32[2,256,256]{2,1,0:T(8,128)S(1)} %collective-permute-done.1.high_ref), custom_call_target="tpu_custom_call" | custom-call | flops 3000000 | bytes 9000000 | tf_op jit(solution)/shard_map/pallas_call | solution.py:479
  11.7 0.7 %collective-permute-start.2 = (f32[2,256,256]{2,1,0:T(8,128)S(1)}, f32[2,256,256]{2,1,0:T(8,128)S(1)}, u32[]{:S(2)}, u32[]{:S(2)}) collective-permute-start(f32[2,256,256]{2,1,0:T(8,128)S(1)} %shard_map.86.x_ref), channel_id=1, source_target_pairs={{3,1},{5,3},{7,5},{9,7},{11,9},{13,11},{15,13},{19,17},{21,19},{23... | collective-permute-start | bytes 1572872 | tf_op jit(solution)/shard_map/ppermute | solution.py:487
  12.4 1.3 %collective-permute-start.3 = (f32[2,256,256]{2,1,0:T(8,128)S(1)}, f32[2,256,256]{2,1,0:T(8,128)S(1)}, u32[]{:S(2)}, u32[]{:S(2)}) collective-permute-start(f32[2,256,256]{2,1,0:T(8,128)S(1)} %collective-permute-done.1.high_ref), channel_id=1, source_target_pairs={{1,0},{3,2},{5,4},{7,6},{9,8},{11,10},{13,12},{15,14},{17,16},{19,... | collective-permute-start | bytes 1572872 | tf_op jit(solution)/shard_map/ppermute | solution.py:488
  13.7 0.0 collective-permute-done.low_ref
  13.7 1.7 %shard_map.88 = (f32[128,8,256]{2,1,0:T(8,128)S(1)}, f32[5,8,128]{2,1,0:T(8,128)S(1)}) custom-call(f32[8,8,128]{2,1,0:T(8,128)S(1)} %get-tuple-element.16.tab_ref, f32[130,8,256]{2,1,0:T(8,128)S(1)} %get-tuple-element.17.b_ref, f32[130,8,256]{2,1,0:T(8,128)S(1)} %get-tuple-element.18.rho_ref, f32[128,8,256]{2,1,0:T(8,128)S(1)} %get-tuple-element.19.part_ref, ...), custom_call_target="tpu_custom_call" | custom-call | flops 2000000 | bytes 6000000 | tf_op jit(solution)/shard_map/pallas_call | solution.py:489
  15.4 7.5 %shard_map.90.sums_ref = f32[16,8,128]{2,1,0:T(8,128)S(1)} custom-call(f32[130,8,256]{2,1,0:T(8,128)S(1)} %get-tuple-element.17.b_ref, f32[128,8,256]{2,1,0:T(8,128)S(1)} %get-tuple-element.21.w_ref, s32[2048]{0:T(1024)} %band_hbm.1, s32[2048]{0:T(1024)} %order_hbm.1), custom_call_target="tpu_custom_call" | custom-call | flops 5000000 | bytes 15000000 | tf_op jit(solution)/shard_map/pallas_call | solution.py:495
  22.8 0.0 collective-permute-done.2.far_ref
  22.9 0.0 collective-permute-done.3.relay_ref
  22.9 3.6 %shard_map.91 = f32[16,8,128]{2,1,0:T(8,128)S(1)} custom-call(f32[8,8,128]{2,1,0:T(8,128)S(1)} %get-tuple-element.16.tab_ref, f32[130,8,256]{2,1,0:T(8,128)S(1)} %get-tuple-element.17.b_ref, f32[130,8,256]{2,1,0:T(8,128)S(1)} %get-tuple-element.18.rho_ref, f32[128,8,256]{2,1,0:T(8,128)S(1)} %get-tuple-element.21.w_ref, ...), custom_call_target="tpu_custom_call" | custom-call | flops 4000000 | bytes 12000000 | tf_op jit(solution)/shard_map/pallas_call | solution.py:509
  26.5 18.9 %all_to_all.5.got_ref = f32[16,8,128]{2,1,0:T(8,128)S(1)} all-to-all(f32[16,8,128]{2,1,0:T(8,128)S(1)} %shard_map.91), channel_id=1, replica_groups=mesh['pos'=2,'gz'=16] {'gz'}, dimensions={0} | all-to-all | bytes 131072 | tf_op jit(solution)/shard_map/all_to_all | solution.py:515
  45.3 2.1 %shard_map.92 = (f32[8,128,256]{2,1,0:T(8,128)}, f32[2,4,2,16]{3,2,1,0:T(2,128)}) custom-call(f32[16,8,128]{2,1,0:T(8,128)S(1)} %all_to_all.5.got_ref, f32[130,8,256]{2,1,0:T(8,128)S(1)} %get-tuple-element.17.b_ref, f32[128,8,256]{2,1,0:T(8,128)S(1)} %get-tuple-element.21.w_ref), custom_call_target="tpu_custom_call" | custom-call | flops 2000000 | bytes 6000000 | tf_op jit(solution)/shard_map/pallas_call | solution.py:516
Async XLA Ops:
  1.7 7.6 %collective-permute-start.1 = (f32[2,256,256]{2,1,0:T(8,128)S(1)}, f32[2,256,256]{2,1,0:T(8,128)S(1)}, u32[]{:S(2)}, u32[]{:S(2)}) collective-permute-start(f32[2,256,256]{2,1,0:T(8,128)S(1)} %shard_map.86.x_ref), channel_id=1, source_target_pairs={{1,0},{2,1},{3,2},{4,3},{5,4},{6,5},{7,6},{8,7},{9,8},{10,9},{11,1... | collective-permute-start | bytes 1572872 | tf_op jit(solution)/shard_map/ppermute | solution.py:464
  6.2 7.5 %collective-permute-start = (f32[2,256,256]{2,1,0:T(8,128)S(1)}, f32[2,256,256]{2,1,0:T(8,128)S(1)}, u32[]{:S(2)}, u32[]{:S(2)}) collective-permute-start(f32[2,256,256]{2,1,0:T(8,128)S(1)} %shard_map.86.x_ref), channel_id=1, source_target_pairs={{0,1},{1,2},{2,3},{3,4},{4,5},{5,6},{6,7},{7,8},{8,9},{9,10},{10,1... | collective-permute-start | bytes 1572872 | tf_op jit(solution)/shard_map/ppermute | solution.py:478
  11.7 11.2 %collective-permute-start.2 = (f32[2,256,256]{2,1,0:T(8,128)S(1)}, f32[2,256,256]{2,1,0:T(8,128)S(1)}, u32[]{:S(2)}, u32[]{:S(2)}) collective-permute-start(f32[2,256,256]{2,1,0:T(8,128)S(1)} %shard_map.86.x_ref), channel_id=1, source_target_pairs={{3,1},{5,3},{7,5},{9,7},{11,9},{13,11},{15,13},{19,17},{21,19},{23... | collective-permute-start | bytes 1572872 | tf_op jit(solution)/shard_map/ppermute | solution.py:487
  12.4 10.5 %collective-permute-start.3 = (f32[2,256,256]{2,1,0:T(8,128)S(1)}, f32[2,256,256]{2,1,0:T(8,128)S(1)}, u32[]{:S(2)}, u32[]{:S(2)}) collective-permute-start(f32[2,256,256]{2,1,0:T(8,128)S(1)} %collective-permute-done.1.high_ref), channel_id=1, source_target_pairs={{1,0},{3,2},{5,4},{7,6},{9,8},{11,10},{13,12},{15,14},{17,16},{19,... | collective-permute-start | bytes 1572872 | tf_op jit(solution)/shard_map/ppermute | solution.py:488

commit v4 on v3

--- a/solution.py
+++ b/solution.py
@@ -9,6 +9,7 @@
 
 PER_SEC = 64
 LANES = 128
+LOG_LANES = 7
 BLOCK = 32
 TILE_ROWS = 24
 M_BB, M_BW, M_WW, M_SIG, M_PP, M_PW, M_FPP, M_FPW, M_FWW = range(96, 105)
@@ -91,12 +92,14 @@
 
 
 def own_kernel(
-    reluct_hbm, levels_hbm, seeds_hbm, x_ref, tab_ref, b_ref, rho_ref, part_ref,
-    reluct_ref, levels_ref, seeds_ref, sems,
+    reluct_hbm, levels_hbm, seeds_hbm, band_hbm, x_ref, tab_ref, b_ref, rho_ref, part_ref, place_ref,
+    reluct_ref, levels_ref, seeds_ref, band_ref, sems,
 ):
-    pairs = [(reluct_hbm, reluct_ref), (levels_hbm, levels_ref), (seeds_hbm, seeds_ref)]
+    pairs = [(reluct_hbm, reluct_ref), (levels_hbm, levels_ref), (seeds_hbm, seeds_ref), (band_hbm, band_ref)]
     for copy in fetch(pairs, sems):
         copy.wait()
+    cells = band_ref[...]
+    place_ref[...] = cells + lax.shift_right_logical(cells, jnp.int32(LOG_LANES)) * ((TILE_ROWS - 1) * LANES)
     half, _, width = part_ref.shape
     count = reluct_ref.shape[0]
     cols = seeds_ref.shape[0]
@@ -177,12 +180,16 @@
     return value + jnp.where(even, pltpu.roll(value, 7, 0), pltpu.roll(value, 1, 0))
 
 
-def image_kernel(
-    tab_ref, b_ref, rho_ref, part_ref, low_ref, high_ref, w_ref, mom_ref
+def field_kernel(
+    b_ref, rho_ref, part_ref, tab_ref, low_ref, b1_ref, rho1_ref, place_hbm, order_hbm,
+    w_ref, mom_ref, sums_ref, field_ref, acc_ref, place_smem, order_smem, sems,
 ):
     half, _, width = part_ref.shape
+    copies = fetch([(place_hbm, place_smem), (order_hbm, order_smem)], sems)
     table = load_table(tab_ref, width)
     even = iota((8, width), 0) % 2 == 0
+    lane = iota((8, width), 1)
+    first_lane, last_lane = lane == 0, lane == width - 1
     zero = jnp.zeros((8, width), jnp.float32)
 
     def finish(block, carry):
@@ -191,14 +198,15 @@
             row = block * 8 + step
             b, rho = b_ref[row + 1], rho_ref[row + 1]
             b_low, rho_low = build((low_ref,), row, half, even, table)
-            b_high, rho_high = build((high_ref,), row, half, even, table)
+            b_high, rho_high = b1_ref[row + 1], rho1_ref[row + 1]
             w = 0.5 * (part_ref[row] + (rho + rho_low) * (b - b_low) + (rho + rho_high) * (b - b_high))
-            w_ref[row] = w
+            w_ref[row + 1] = w
             bb, bw, ww = bb + b * b, bw + b * w, ww + w * w
         mom_ref[4] = jnp.where(rho_low[:, :LANES] > 0.0, 0.0, 1.0)
         return bb, bw, ww
 
     bb, bw, ww = lax.fori_loop(0, half // 8, finish, (zero, zero, zero))
+    seams(w_ref, even)
     even_tile = even[:, :LANES]
     tile = jnp.zeros((8, LANES), jnp.float32)
     bb, bw, ww = (lane_sum(total) + tile for total in (bb, bw, ww))
@@ -207,71 +215,52 @@
     mom_ref[0], mom_ref[1], mom_ref[2] = bb, bw, ww
     mom_ref[3] = jnp.minimum(jnp.maximum(shift, 0.0), 2.0)
 
-
-def band_kernel(
-    b_ref, w_ref, band_hbm, order_hbm, sums_ref, field_ref, acc_ref, band_smem, order_smem, sems
-):
-    half, _, width = w_ref.shape
-    copies = fetch([(band_hbm, band_smem), (order_hbm, order_smem)], sems)
-    even = iota((8, width), 0) % 2 == 0
-    lane = iota((8, width), 1)
-    first_lane, last_lane = lane == 0, lane == width - 1
     normal_y = (lane.astype(jnp.float32) - 0.5 * (width - 1)) / (0.5 * width)
     upper = jnp.where(even, 0.0, 1.0)
     across = width // LANES
     lower_tiles = half * across
 
-    def spread(row, low, high):
-        b, w = b_ref[row + 1], w_ref[row]
-        gx_b = after(b, last_lane) - before(b, first_lane)
-        gx_w = after(w, last_lane) - before(w, first_lane)
-        gy_b = b_ref[row + 2] - b_ref[row]
-        gy_w = high - low
-        normal_x = upper + (jnp.asarray(row).astype(jnp.float32) - (half - 0.5)) / half
-        pairs = (
-            (gx_b * gx_b - gy_b * gy_b, 2.0 * (gx_b * gy_b)),
-            (2.0 * (gx_b * gx_w - gy_b * gy_w), 2.0 * (gx_b * gy_w + gx_w * gy_b)),
-            (gx_w * gx_w - gy_w * gy_w, 2.0 * (gx_w * gy_w)),
-        )
-        for index, (diff, cross) in enumerate(pairs):
-            force_x = normal_x * diff - normal_y * cross
-            force_y = normal_x * cross + normal_y * diff
-            lower = jnp.where(even, force_x, pltpu.roll(force_y, 1, 0))
-            higher = jnp.where(even, pltpu.roll(force_x, 7, 0), force_y)
-            for tile_index in range(across):
-                part = slice(tile_index * LANES, (tile_index + 1) * LANES)
-                at = row * across + tile_index
-                for base, value in ((0, lower), (lower_tiles, higher)):
-                    first = pl.multiple_of((base + at) * TILE_ROWS + 8 * index, 8)
-                    field_ref[pl.ds(first, 8), :] = value[:, part]
-
     def forces(block, carry):
         for step in range(8):
             row = block * 8 + step
-            spread(row, w_ref[row - 1], w_ref[row + 1])
+            b, w = b_ref[row + 1], w_ref[row + 1]
+            gx_b = after(b, last_lane) - before(b, first_lane)
+            gx_w = after(w, last_lane) - before(w, first_lane)
+            gy_b = b_ref[row + 2] - b_ref[row]
+            gy_w = w_ref[row + 2] - w_ref[row]
+            normal_x = upper + (row.astype(jnp.float32) - (half - 0.5)) / half
+            pairs = (
+                (0.5 * (gx_b * gx_b - gy_b * gy_b), gx_b * gy_b),
+                (gx_b * gx_w - gy_b * gy_w, gx_b * gy_w + gx_w * gy_b),
+                (0.5 * (gx_w * gx_w - gy_w * gy_w), gx_w * gy_w),
+            )
+            for index, (diff, cross) in enumerate(pairs):
+                force_x = normal_x * diff - normal_y * cross
+                force_y = normal_x * cross + normal_y * diff
+                lower = jnp.where(even, force_x, pltpu.roll(force_y, 1, 0))
+                higher = jnp.where(even, pltpu.roll(force_x, 7, 0), force_y)
+                for tile_index in range(across):
+                    part = slice(tile_index * LANES, (tile_index + 1) * LANES)
+                    at = row * across + tile_index
+                    for base, value in ((0, lower), (lower_tiles, higher)):
+                        first = pl.multiple_of((base + at) * TILE_ROWS + 8 * index, 8)
+                        field_ref[pl.ds(first, 8), :] = value[:, part]
         return carry
 
-    edge = jnp.where(even, 0.0, pltpu.roll(w_ref[half - 1], 1, 0))
-    for row in range(8):
-        spread(row, w_ref[row - 1] if row else edge, w_ref[row + 1])
-    lax.fori_loop(1, half // 8 - 1, forces, 0)
-    edge = jnp.where(even, pltpu.roll(w_ref[0], 7, 0), 0.0)
-    for row in range(half - 8, half):
-        spread(row, w_ref[row - 1], w_ref[row + 1] if row + 1 < half else edge)
+    lax.fori_loop(0, half // 8, forces, 0)
     for copy in copies:
         copy.wait()
 
     place = iota((8, LANES), 1)
-    tile = jnp.zeros((8, LANES), jnp.float32)
     count = sums_ref.shape[0]
-    sectors = band_smem.shape[0] // (PER_SEC * count)
+    sectors = order_smem.shape[0] // (PER_SEC * count)
 
     def gather(sector, carry):
         accs = [tile] * 3
         for step in range(PER_SEC):
-            cell = band_smem[order_smem[sector * PER_SEC + step]]
-            here = place == (cell & (LANES - 1))
-            start = lax.shift_right_logical(cell, jnp.int32(7)) * TILE_ROWS
+            spot = place_smem[order_smem[sector * PER_SEC + step]]
+            here = ((place ^ spot) & (LANES - 1)) == 0
+            start = lax.shift_right_logical(spot, jnp.int32(LOG_LANES))
             for field in range(3):
                 first = pl.multiple_of(start + 8 * field, 8)
                 accs[field] += jnp.where(here, field_ref[pl.ds(first, 8), :], 0.0)
@@ -290,10 +279,9 @@
 
 
 def face_kernel(
-    tab_ref, b_ref, rho_ref, w_ref, high_ref, upper_ref, far_ref, relay_ref, sums_ref, mom_ref,
-    out_ref,
+    b_ref, rho_ref, w_ref, b1_ref, rho1_ref, upper_ref, tab_ref, far_ref, relay_ref, sums_ref, mom_ref, out_ref
 ):
-    half, _, width = w_ref.shape
+    half, _, width = upper_ref.shape
     table = load_table(tab_ref, width)
     even = iota((8, width), 0) % 2 == 0
     lane = iota((8, width), 1)
@@ -302,43 +290,37 @@
     shift = jnp.concatenate([mom_ref[3]] * (width // LANES), axis=1)
     outside = jnp.where(first_lane, 1.0, 0.0) + jnp.concatenate([mom_ref[4]] * (width // LANES), axis=1)
 
-    def row_sums(row, w_next, carry):
+    def rows(block, carry):
         w, p, rho, pp, pw, fpp, fpw, fww = carry
-        rho_next = rho_ref[row + 2]
-        p_next = b_ref[row + 2] - shift * w_next
-        b1, rho1 = build((high_ref,), row, half, even, table)
-        b2, rho2 = build((far_ref, relay_ref), row, half, even, table)
-        w1 = 0.5 * (upper_ref[row] + (rho1 + rho2) * (b1 - b2))
-        w1 = jnp.where(rho1 > 0.0, w1, 0.0)
-        p1 = b1 - shift * w1
-        pp, pw = pp + p * p, pw + p * w
-        coef = 1.0 + rho * outside
-        up, uw = coef * p, coef * w
-        fpp, fpw, fww = fpp + up * p, fpw + up * w, fww + uw * w
-        for other_rho, other_p, other_w in (
-            (rho_next, p_next, w_next),
-            (after(rho, last_lane), after(p, last_lane), after(w, last_lane)),
-            (rho1, p1, w1),
-        ):
-            weight, dp, dw = rho + other_rho, p - other_p, w - other_w
-            up, uw = weight * dp, weight * dw
-            fpp, fpw, fww = fpp + up * dp, fpw + up * dw, fww + uw * dw
-        return w_next, p_next, rho_next, pp, pw, fpp, fpw, fww
-
-    def rows(block, carry):
         for step in range(8):
             row = block * 8 + step
-            carry = row_sums(row, w_ref[row + 1], carry)
-        return carry
-
-    w, rho = w_ref[0], rho_ref[1]
+            w_next, rho_next = w_ref[row + 2], rho_ref[row + 2]
+            p_next = b_ref[row + 2] - shift * w_next
+            b1, rho1 = b1_ref[row + 1], rho1_ref[row + 1]
+            b2, rho2 = build((far_ref, relay_ref), row, half, even, table)
+            w1 = 0.5 * (upper_ref[row] + (rho1 + rho2) * (b1 - b2))
+            w1 = jnp.where(rho1 > 0.0, w1, 0.0)
+            p1 = b1 - shift * w1
+            pp, pw = pp + p * p, pw + p * w
+            coef = 1.0 + rho * outside
+            up, uw = coef * p, coef * w
+            fpp, fpw, fww = fpp + up * p, fpw + up * w, fww + uw * w
+            for other_rho, other_p, other_w in (
+                (rho_next, p_next, w_next),
+                (after(rho, last_lane), after(p, last_lane), after(w, last_lane)),
+                (rho1, p1, w1),
+            ):
+                weight, dp, dw = rho + other_rho, p - other_p, w - other_w
+                up, uw = weight * dp, weight * dw
+                fpp, fpw, fww = fpp + up * dp, fpw + up * dw, fww + uw * dw
+            w, p, rho = w_next, p_next, rho_next
+        return w, p, rho, pp, pw, fpp, fpw, fww
+
+    w, rho = w_ref[1], rho_ref[1]
     p = b_ref[1] - shift * w
     edge = jnp.where(even, rho, 0.0)
     carry = (w, p, rho, zero, zero, edge * p * p, edge * p * w, edge * w * w)
-    carry = lax.fori_loop(0, half // 8 - 1, rows, carry)
-    last = jnp.where(even, pltpu.roll(w_ref[0], 7, 0), 0.0)
-    for row in range(half - 8, half):
-        carry = row_sums(row, w_ref[row + 1] if row + 1 < half else last, carry)
+    carry = lax.fori_loop(0, half // 8, rows, carry)
     pp, pw, fpp, fpw, fww = carry[-5:]
     lane_tile = iota((8, LANES), 1)
     scalars = {
@@ -353,8 +335,8 @@
         out_ref[index] = sums_ref[index] + tile
 
 
-def final_kernel(got_ref, b_ref, w_ref, sol_ref, force_ref):
-    half, _, width = w_ref.shape
+def final_kernel(got_ref, b_ref, w_ref, sol_hbm, force_ref, sol_ref, sems):
+    half, width = b_ref.shape[0] - 2, b_ref.shape[2]
     count = got_ref.shape[0]
     _, cols, sectors, _ = force_ref.shape
     even = iota((8, LANES), 0) % 2 == 0
@@ -390,15 +372,22 @@
         stack = []
         for step_index in range(8):
             row = block * 8 + step_index
-            stack.append(wide_alpha * b_ref[row + 1] + wide_gamma * w_ref[row])
+            stack.append(wide_alpha * b_ref[row + 1] + wide_gamma * w_ref[row + 1])
         turned = jnp.swapaxes(jnp.stack(stack), 0, 1)
         for sub in range(8):
-            sol_ref[sub, pl.ds(block * 8, 8), :] = turned[sub]
+            sol_ref[sub, pl.ds(pl.multiple_of(block * 8, 8), 8), :] = turned[sub]
         return carry
 
-    lax.fori_loop(0, half // 8, rows, 0)
-
-    sign = jnp.where(even, 0.125, -0.125)
+    chunks = sems.shape[0]
+    span = half // chunks
+    copies = []
+    for chunk in range(chunks):
+        lax.fori_loop(chunk * span // 8, (chunk + 1) * span // 8, rows, 0)
+        at = pl.ds(chunk * span, span)
+        copies.append(pltpu.make_async_copy(sol_ref.at[:, at], sol_hbm.at[:, at], sems.at[chunk]))
+        copies[-1].start()
+
+    sign = jnp.where(even, 0.25, -0.25)
     coef = sign * jnp.where(
         lane < BLOCK, alpha * alpha, jnp.where(lane < 2 * BLOCK, alpha * gamma, gamma * gamma)
     )
@@ -413,11 +402,13 @@
             for c in range(cols):
                 at = 2 * c + part
                 force_ref[part, c, sector:sector + 1, :] = tiles[sector][at:at + 1, :count]
+    for copy in copies:
+        copy.wait()
 
 
 def call(kernel, outs, in_specs, out_specs=None, scratch=(), limit=4 * 2**20, cost=None):
     shapes = [
-        out if isinstance(out, jax.ShapeDtypeStruct) else jax.ShapeDtypeStruct(out, jnp.float32)
+        jax.ShapeDtypeStruct(out, jnp.float32) if isinstance(out, tuple) else out
         for out in outs
     ]
     return pl.pallas_call(
@@ -462,40 +453,34 @@
         scratch=[pltpu.VMEM((width_x, width_y), jnp.int32), dma((5,))],
     )(in_hbm(source), in_hbm(regions))
     high = lax.ppermute(own, "gz", [(i + 1, i) for i in range(count - 1)])
-    table, b, rho, part = call(
+    table, b, rho, part, places = call(
         own_kernel,
-        [(2 * count_regions, 8, LANES), padded, padded, packed],
-        [HBM] * 3 + [VMEM],
+        [(2 * count_regions, 8, LANES), padded, padded, packed, jax.ShapeDtypeStruct((band // LANES, LANES), jnp.int32)],
+        [HBM] * 4 + [VMEM],
         scratch=[
             pltpu.SMEM(reluctivity.shape, jnp.float32),
             pltpu.SMEM(levels.shape, jnp.float32),
             pltpu.SMEM(seeds.shape, jnp.int32),
-            dma((3,)),
+            pltpu.VMEM((band // LANES, LANES), jnp.int32),
+            dma((4,)),
         ],
         cost=estimate(3),
-    )(in_hbm(reluctivity), in_hbm(levels), in_hbm(seeds), own)
+    )(in_hbm(reluctivity), in_hbm(levels), in_hbm(seeds), in_hbm(band_cells.reshape(-1, LANES)), own)
     own_second, table = ORDER((own, table))
     low = lax.ppermute(own_second, "gz", [(i, i + 1) for i in range(count - 1)])
-    (upper,) = call(
+    upper, b1, rho1 = call(
         upper_kernel,
-        [packed],
+        [packed, padded, padded],
         [VMEM] * 4,
-        scratch=[pltpu.VMEM(padded, jnp.float32)] * 2,
         cost=estimate(3),
     )(table, b, rho, high)
     upper, own_third, high_second = ORDER((upper, own_second, high))
     far = lax.ppermute(own_third, "gz", [(i + 2, i) for i in range(1, count - 2, 2)])
     relay = lax.ppermute(high_second, "gz", [(i + 1, i) for i in range(0, count - 1, 2)])
-    w, moments = call(
-        image_kernel,
-        [packed, (5, 8, LANES)],
-        [VMEM] * 6,
-        cost=estimate(2),
-    )(table, b, rho, part, low, high)
-    (sums,) = call(
-        band_kernel,
-        [(count, 8, LANES)],
-        [VMEM] * 2 + [HBM] * 2,
+    w, moments, sums = call(
+        field_kernel,
+        [padded, (5, 8, LANES), (count, 8, LANES)],
+        [VMEM] * 7 + [ANY, HBM],
         scratch=[
             pltpu.VMEM((width_x * (width_y // LANES) * TILE_ROWS, LANES), jnp.float32),
             pltpu.VMEM((band // PER_SEC * 3, 8, LANES), jnp.float32),
@@ -504,19 +489,21 @@
             dma((2,)),
         ],
         limit=10 * 2**20,
-        cost=estimate(5),
-    )(b, w, in_hbm(band_cells), in_hbm(sector_order))
+        cost=estimate(7),
+    )(b, rho, part, table, low, b1, rho1, places.reshape(-1), in_hbm(sector_order))
     (payload,) = call(
         face_kernel,
         [(count, 8, LANES)],
-        [VMEM] * 10,
+        [VMEM] * 11,
         cost=estimate(4),
-    )(table, b, rho, w, high, upper, far, relay, sums, moments)
+    )(b, rho, w, b1, rho1, upper, table, far, relay, sums, moments)
     got = lax.all_to_all(payload, "gz", split_axis=0, concat_axis=0, tiled=True)
     solved, forces = call(
         final_kernel,
         [(8, half, width_y), (2, cols, sectors, count)],
         [VMEM] * 3,
+        [HBM, VMEM],
+        scratch=[pltpu.VMEM((8, half, width_y), jnp.float32), dma((4,))],
         cost=estimate(2),
     )(got, b, w)
     return solved.reshape(cols, 1, width_x, width_y), forces

time: 47.7 us -> 46.5 us (0.975)
  Pallas kernels: 21.5 us -> 20.2 us
    pallas_call x5 -> x4, Pallas kernels: 18.4 us -> 16.9 us  [the longest x1 8.05 us: body(): call(field_kernel, [padded, (5, 8, LANES), (count, 8, LANES)], [VMEM] * 7...]
  transfers between devices with their start and end apart: 4 -> 4, of which waited for: 0 -> 0; matrix products, arithmetic and copies ran while one was open for 0% -> 0% of each run, Pallas kernels for 31% -> 30%
where the time goes in v4:
time: 46.5 us; the launch traced here: 46.2 us
  Pallas kernels  20.2 us (43%)
  blocking collectives  18.9 us (41%)
  starting transfers between devices  6.34 us (14%)
  between operations  0.72 us (2%)
    all_to_all x1, blocking collectives, body(): got = lax.all_to_all(payload, 'gz', split_axis=0, concat_axis=0, tiled=True)  18.9 us
    pallas_call x1, Pallas kernels, body(): call(field_kernel, [padded, (5, 8, LANES), (count, 8, LANES)], [VMEM] * 7...  8.05 us
    pallas_call x1, Pallas kernels, body(): call(face_kernel, [(count, 8, LANES)], [VMEM] * 11, cost=estimate(4))  3.23 us
    pallas_call x1, Pallas kernels, body(): call(own_kernel, [(2 * count_regions, 8, LANES), padded, padded, packed,...  3.18 us
    ppermute x1, starting transfers between devices, body(): low = lax.ppermute(own_second, 'gz', [(i, i + 1) for i in range(count - 1)])  3.06 us
    pallas_call x1, Pallas kernels, body(): call(upper_kernel, [packed, padded, padded], [VMEM] * 4, cost=estimate(3))  2.43 us
    pallas_call x1, Pallas kernels, body(): call(final_kernel, [(8, half, width_y), (2, cols, sectors, count)], [VMEM...  2.29 us
    ppermute x1, starting transfers between devices, body(): high = lax.ppermute(own, 'gz', [(i + 1, i) for i in range(count - 1)])  1.29 us
  transfers between devices with their start and end apart: 4, of which 0 were waited for; matrix products, arithmetic and copies ran while one was open for 0% of the time, Pallas kernels for 30%

profile of v4, /device:TPU:0, one launch (start us, length us, event | category | flops | bytes accessed | tf_op | source)
XLA Modules:
  0.0 46.2 jit_solution(1134914135191762533)
XLA Ops:
  0.6 1.1 %shard_map.86.x_ref = f32[2,256,256]{2,1,0:T(8,128)S(1)} custom-call(f32[1,256,256]{2,1,0:T(8,128)} %source_ref.1, s32[1,256,256]{2,1,0:T(8,128)} %regions_ref.1), custom_call_target="tpu_custom_call" | custom-call | tf_op jit(solution)/shard_map/pallas_call | solution.py:449
  1.7 1.3 %collective-permute-start.1 = (f32[2,256,256]{2,1,0:T(8,128)S(1)}, f32[2,256,256]{2,1,0:T(8,128)S(1)}, u32[]{:S(2)}, u32[]{:S(2)}) collective-permute-start(f32[2,256,256]{2,1,0:T(8,128)S(1)} %shard_map.86.x_ref), channel_id=1, source_target_pairs={{1,0},{2,1},{3,2},{4,3},{5,4},{6,5},{7,6},{8,7},{9,8},{10,9},{11,1... | collective-permute-start | bytes 1572872 | tf_op jit(solution)/shard_map/ppermute | solution.py:455
  3.0 3.2 %shard_map.87 = (f32[8,8,128]{2,1,0:T(8,128)S(1)}, f32[130,8,256]{2,1,0:T(8,128)S(1)}, f32[130,8,256]{2,1,0:T(8,128)S(1)}, f32[128,8,256]{2,1,0:T(8,128)S(1)}, s32[16,128]{1,0:T(8,128)S(1)}) custom-call(f32[4]{0:T(128)} %reluct_hbm.1, f32[4]{0:T(128)} %levels_hbm.1, s32[4,4]{1,0:T(4,128)} %seeds_hbm.1, s32[16,128]{1,0:T(8,128)} %bitcast.6, ...), custom_call_target="tpu_custom_call" | custom-call | flops 3000000 | bytes 9000000 | tf_op jit(solution)/shard_map/pallas_call | solution.py:456
  6.2 3.1 %collective-permute-start = (f32[2,256,256]{2,1,0:T(8,128)S(1)}, f32[2,256,256]{2,1,0:T(8,128)S(1)}, u32[]{:S(2)}, u32[]{:S(2)}) collective-permute-start(f32[2,256,256]{2,1,0:T(8,128)S(1)} %shard_map.86.x_ref), channel_id=1, source_target_pairs={{0,1},{1,2},{2,3},{3,4},{4,5},{5,6},{6,7},{7,8},{8,9},{9,10},{10,1... | collective-permute-start | bytes 1572872 | tf_op jit(solution)/shard_map/ppermute | solution.py:470
  9.3 0.0 collective-permute-done.1.high_ref
  9.3 2.4 %shard_map.88 = (f32[128,8,256]{2,1,0:T(8,128)S(1)}, f32[130,8,256]{2,1,0:T(8,128)S(1)}, f32[130,8,256]{2,1,0:T(8,128)S(1)}) custom-call(f32[8,8,128]{2,1,0:T(8,128)S(1)} %get-tuple-element.24.tab_ref, f32[130,8,256]{2,1,0:T(8,128)S(1)} %get-tuple-element.20.b_ref, f32[130,8,256]{2,1,0:T(8,128)S(1)} %get-tuple-element.21.rho_ref, ...), custom_call_target="tpu_custom_call" | custom-call | flops 3000000 | bytes 9000000 | tf_op jit(solution)/shard_map/pallas_call | solution.py:471
  11.7 0.7 %collective-permute-start.2 = (f32[2,256,256]{2,1,0:T(8,128)S(1)}, f32[2,256,256]{2,1,0:T(8,128)S(1)}, u32[]{:S(2)}, u32[]{:S(2)}) collective-permute-start(f32[2,256,256]{2,1,0:T(8,128)S(1)} %shard_map.86.x_ref), channel_id=1, source_target_pairs={{3,1},{5,3},{7,5},{9,7},{11,9},{13,11},{15,13},{19,17},{21,19},{23... | collective-permute-start | bytes 1572872 | tf_op jit(solution)/shard_map/ppermute | solution.py:478
  12.4 1.3 %collective-permute-start.3 = (f32[2,256,256]{2,1,0:T(8,128)S(1)}, f32[2,256,256]{2,1,0:T(8,128)S(1)}, u32[]{:S(2)}, u32[]{:S(2)}) collective-permute-start(f32[2,256,256]{2,1,0:T(8,128)S(1)} %collective-permute-done.1.high_ref), channel_id=1, source_target_pairs={{1,0},{3,2},{5,4},{7,6},{9,8},{11,10},{13,12},{15,14},{17,16},{19,... | collective-permute-start | bytes 1572872 | tf_op jit(solution)/shard_map/ppermute | solution.py:479
  13.7 0.0 collective-permute-done.low_ref
  13.7 8.1 %shard_map.89 = (f32[130,8,256]{2,1,0:T(8,128)S(1)}, f32[5,8,128]{2,1,0:T(8,128)S(1)}, f32[16,8,128]{2,1,0:T(8,128)S(1)}) custom-call(f32[130,8,256]{2,1,0:T(8,128)S(1)} %get-tuple-element.20.b_ref, f32[130,8,256]{2,1,0:T(8,128)S(1)} %get-tuple-element.21.rho_ref, f32[128,8,256]{2,1,0:T(8,128)S(1)} %get-tuple-element.22.part_ref, ...), custom_call_target="tpu_custom_call" | custom-call | flops 7000000 | bytes 21000000 | tf_op jit(solution)/shard_map/pallas_call | solution.py:480
  21.8 0.0 collective-permute-done.2.far_ref
  21.8 0.0 collective-permute-done.3.relay_ref
  21.8 3.2 %shard_map.90 = f32[16,8,128]{2,1,0:T(8,128)S(1)} custom-call(f32[130,8,256]{2,1,0:T(8,128)S(1)} %get-tuple-element.20.b_ref, f32[130,8,256]{2,1,0:T(8,128)S(1)} %get-tuple-element.21.rho_ref, f32[130,8,256]{2,1,0:T(8,128)S(1)} %get-tuple-element.29.w_ref, f32[130,8,256]{2,1,0:T(8,128)S(1)} %get-tuple-element.26.b1_ref, ...), custom_call_target="tpu_custom_call" | custom-call | flops 4000000 | bytes 12000000 | tf_op jit(solution)/shard_map/pallas_call | solution.py:494
  25.0 18.9 %all_to_all.5.got_ref = f32[16,8,128]{2,1,0:T(8,128)S(1)} all-to-all(f32[16,8,128]{2,1,0:T(8,128)S(1)} %shard_map.90), channel_id=1, replica_groups=mesh['pos'=2,'gz'=16] {'gz'}, dimensions={0} | all-to-all | bytes 131072 | tf_op jit(solution)/shard_map/all_to_all | solution.py:500
  43.9 2.3 %shard_map.91 = (f32[8,128,256]{2,1,0:T(8,128)}, f32[2,4,2,16]{3,2,1,0:T(2,128)}) custom-call(f32[16,8,128]{2,1,0:T(8,128)S(1)} %all_to_all.5.got_ref, f32[130,8,256]{2,1,0:T(8,128)S(1)} %get-tuple-element.20.b_ref, f32[130,8,256]{2,1,0:T(8,128)S(1)} %get-tuple-element.29.w_ref), custom_call_target="tpu_custom_call" | custom-call | flops 2000000 | bytes 6000000 | tf_op jit(solution)/shard_map/pallas_call | solution.py:501
Async XLA Ops:
  1.7 7.6 %collective-permute-start.1 = (f32[2,256,256]{2,1,0:T(8,128)S(1)}, f32[2,256,256]{2,1,0:T(8,128)S(1)}, u32[]{:S(2)}, u32[]{:S(2)}) collective-permute-start(f32[2,256,256]{2,1,0:T(8,128)S(1)} %shard_map.86.x_ref), channel_id=1, source_target_pairs={{1,0},{2,1},{3,2},{4,3},{5,4},{6,5},{7,6},{8,7},{9,8},{10,9},{11,1... | collective-permute-start | bytes 1572872 | tf_op jit(solution)/shard_map/ppermute | solution.py:455
  6.2 7.5 %collective-permute-start = (f32[2,256,256]{2,1,0:T(8,128)S(1)}, f32[2,256,256]{2,1,0:T(8,128)S(1)}, u32[]{:S(2)}, u32[]{:S(2)}) collective-permute-start(f32[2,256,256]{2,1,0:T(8,128)S(1)} %shard_map.86.x_ref), channel_id=1, source_target_pairs={{0,1},{1,2},{2,3},{3,4},{4,5},{5,6},{6,7},{7,8},{8,9},{9,10},{10,1... | collective-permute-start | bytes 1572872 | tf_op jit(solution)/shard_map/ppermute | solution.py:470
  11.7 10.1 %collective-permute-start.2 = (f32[2,256,256]{2,1,0:T(8,128)S(1)}, f32[2,256,256]{2,1,0:T(8,128)S(1)}, u32[]{:S(2)}, u32[]{:S(2)}) collective-permute-start(f32[2,256,256]{2,1,0:T(8,128)S(1)} %shard_map.86.x_ref), channel_id=1, source_target_pairs={{3,1},{5,3},{7,5},{9,7},{11,9},{13,11},{15,13},{19,17},{21,19},{23... | collective-permute-start | bytes 1572872 | tf_op jit(solution)/shard_map/ppermute | solution.py:478
  12.4 9.4 %collective-permute-start.3 = (f32[2,256,256]{2,1,0:T(8,128)S(1)}, f32[2,256,256]{2,1,0:T(8,128)S(1)}, u32[]{:S(2)}, u32[]{:S(2)}) collective-permute-start(f32[2,256,256]{2,1,0:T(8,128)S(1)} %collective-permute-done.1.high_ref), channel_id=1, source_target_pairs={{1,0},{3,2},{5,4},{7,6},{9,8},{11,10},{13,12},{15,14},{17,16},{19,... | collective-permute-start | bytes 1572872 | tf_op jit(solution)/shard_map/ppermute | solution.py:479

commit v5 on v4

--- a/solution.py
+++ b/solution.py
@@ -92,14 +92,12 @@
 
 
 def own_kernel(
-    reluct_hbm, levels_hbm, seeds_hbm, band_hbm, x_ref, tab_ref, b_ref, rho_ref, part_ref, place_ref,
-    reluct_ref, levels_ref, seeds_ref, band_ref, sems,
+    reluct_hbm, levels_hbm, seeds_hbm, x_ref, tab_ref, b_ref, rho_ref, part_ref,
+    reluct_ref, levels_ref, seeds_ref, sems,
 ):
-    pairs = [(reluct_hbm, reluct_ref), (levels_hbm, levels_ref), (seeds_hbm, seeds_ref), (band_hbm, band_ref)]
+    pairs = [(reluct_hbm, reluct_ref), (levels_hbm, levels_ref), (seeds_hbm, seeds_ref)]
     for copy in fetch(pairs, sems):
         copy.wait()
-    cells = band_ref[...]
-    place_ref[...] = cells + lax.shift_right_logical(cells, jnp.int32(LOG_LANES)) * ((TILE_ROWS - 1) * LANES)
     half, _, width = part_ref.shape
     count = reluct_ref.shape[0]
     cols = seeds_ref.shape[0]
@@ -140,7 +138,32 @@
     lax.fori_loop(0, half // 16, apply, (value, rho, flow))
 
 
-def upper_kernel(tab_ref, b_ref, rho_ref, high_ref, part_ref, b1_ref, rho1_ref):
+def locate(band_ref, order_ref, start_ref, lane_ref):
+    cells = band_ref[...]
+    rows = cells.shape[0]
+    halves = jnp.concatenate([lax.shift_right_logical(cells, jnp.int32(8)), cells & 255], axis=0)
+    halves = halves.astype(jnp.float32)
+    column, row = iota((LANES, LANES), 0), iota((rows, LANES), 0)
+
+    def chunk(index, carry):
+        order = order_ref[pl.ds(index, 1), :]
+        pick = jnp.where(column == (order & (LANES - 1)), 1.0, 0.0)
+        got = jnp.dot(halves, pick, preferred_element_type=jnp.float32)
+        here = row == lax.shift_right_logical(order, jnp.int32(LOG_LANES))
+        both = jnp.where(here, got[:rows] * 256.0 + got[rows:], 0.0)
+        cell = jnp.sum(both, axis=0, keepdims=True).astype(jnp.int32)
+        start_ref[pl.ds(index, 1), :] = lax.shift_right_logical(cell, jnp.int32(LOG_LANES)) * TILE_ROWS
+        lane_ref[pl.ds(index, 1), :] = cell & (LANES - 1)
+        return carry
+
+    lax.fori_loop(0, order_ref.shape[0], chunk, 0, unroll=True if order_ref.shape[0] <= 16 else 8)
+
+
+def upper_kernel(
+    tab_ref, b_ref, rho_ref, high_ref, band_hbm, order_hbm, part_ref, b1_ref, rho1_ref, start_ref, lane_ref,
+    band_ref, order_ref, sems,
+):
+    copies = fetch([(band_hbm, band_ref), (order_hbm, order_ref)], sems)
     half, _, width = part_ref.shape
     table = load_table(tab_ref, width)
     even = iota((8, width), 0) % 2 == 0
@@ -170,6 +193,9 @@
     value, rho = b1_ref[1], rho1_ref[1]
     flow = (rho1_ref[0] + rho) * (b1_ref[0] - value)
     lax.fori_loop(0, half // 16, apply, (value, rho, flow))
+    for copy in copies:
+        copy.wait()
+    locate(band_ref, order_ref, start_ref, lane_ref)
 
 
 def lane_sum(value):
@@ -181,11 +207,11 @@
 
 
 def field_kernel(
-    b_ref, rho_ref, part_ref, tab_ref, low_ref, b1_ref, rho1_ref, place_hbm, order_hbm,
-    w_ref, mom_ref, sums_ref, field_ref, acc_ref, place_smem, order_smem, sems,
+    b_ref, rho_ref, part_ref, tab_ref, low_ref, b1_ref, rho1_ref, start_any, lane_any,
+    w_ref, mom_ref, sums_ref, field_ref, acc_ref, start_smem, lane_smem, sems,
 ):
     half, _, width = part_ref.shape
-    copies = fetch([(place_hbm, place_smem), (order_hbm, order_smem)], sems)
+    copies = fetch([(start_any, start_smem), (lane_any, lane_smem)], sems)
     table = load_table(tab_ref, width)
     even = iota((8, width), 0) % 2 == 0
     lane = iota((8, width), 1)
@@ -221,8 +247,8 @@
     lower_tiles = half * across
 
     def forces(block, carry):
-        for step in range(8):
-            row = block * 8 + step
+        for step in range(16):
+            row = block * 16 + step
             b, w = b_ref[row + 1], w_ref[row + 1]
             gx_b = after(b, last_lane) - before(b, first_lane)
             gx_w = after(w, last_lane) - before(w, first_lane)
@@ -247,20 +273,19 @@
                         field_ref[pl.ds(first, 8), :] = value[:, part]
         return carry
 
-    lax.fori_loop(0, half // 8, forces, 0)
+    lax.fori_loop(0, half // 16, forces, 0)
     for copy in copies:
         copy.wait()
 
     place = iota((8, LANES), 1)
     count = sums_ref.shape[0]
-    sectors = order_smem.shape[0] // (PER_SEC * count)
+    sectors = start_smem.shape[0] // (PER_SEC * count)
 
     def gather(sector, carry):
         accs = [tile] * 3
         for step in range(PER_SEC):
-            spot = place_smem[order_smem[sector * PER_SEC + step]]
-            here = ((place ^ spot) & (LANES - 1)) == 0
-            start = lax.shift_right_logical(spot, jnp.int32(LOG_LANES))
+            start = start_smem[sector * PER_SEC + step]
+            here = place == lane_smem[sector * PER_SEC + step]
             for field in range(3):
                 first = pl.multiple_of(start + 8 * field, 8)
                 accs[field] += jnp.where(here, field_ref[pl.ds(first, 8), :], 0.0)
@@ -292,8 +317,8 @@
 
     def rows(block, carry):
         w, p, rho, pp, pw, fpp, fpw, fww = carry
-        for step in range(8):
-            row = block * 8 + step
+        for step in range(16):
+            row = block * 16 + step
             w_next, rho_next = w_ref[row + 2], rho_ref[row + 2]
             p_next = b_ref[row + 2] - shift * w_next
             b1, rho1 = b1_ref[row + 1], rho1_ref[row + 1]
@@ -320,7 +345,7 @@
     p = b_ref[1] - shift * w
     edge = jnp.where(even, rho, 0.0)
     carry = (w, p, rho, zero, zero, edge * p * p, edge * p * w, edge * w * w)
-    carry = lax.fori_loop(0, half // 8, rows, carry)
+    carry = lax.fori_loop(0, half // 16, rows, carry)
     pp, pw, fpp, fpw, fww = carry[-5:]
     lane_tile = iota((8, LANES), 1)
     scalars = {
@@ -335,7 +360,7 @@
         out_ref[index] = sums_ref[index] + tile
 
 
-def final_kernel(got_ref, b_ref, w_ref, sol_hbm, force_ref, sol_ref, sems):
+def final_kernel(got_ref, b_ref, w_ref, sol_ref, force_ref):
     half, width = b_ref.shape[0] - 2, b_ref.shape[2]
     count = got_ref.shape[0]
     _, cols, sectors, _ = force_ref.shape
@@ -378,14 +403,7 @@
             sol_ref[sub, pl.ds(pl.multiple_of(block * 8, 8), 8), :] = turned[sub]
         return carry
 
-    chunks = sems.shape[0]
-    span = half // chunks
-    copies = []
-    for chunk in range(chunks):
-        lax.fori_loop(chunk * span // 8, (chunk + 1) * span // 8, rows, 0)
-        at = pl.ds(chunk * span, span)
-        copies.append(pltpu.make_async_copy(sol_ref.at[:, at], sol_hbm.at[:, at], sems.at[chunk]))
-        copies[-1].start()
+    lax.fori_loop(0, half // 8, rows, 0)
 
     sign = jnp.where(even, 0.25, -0.25)
     coef = sign * jnp.where(
@@ -402,8 +420,6 @@
             for c in range(cols):
                 at = 2 * c + part
                 force_ref[part, c, sector:sector + 1, :] = tiles[sector][at:at + 1, :count]
-    for copy in copies:
-        copy.wait()
 
 
 def call(kernel, outs, in_specs, out_specs=None, scratch=(), limit=4 * 2**20, cost=None):
@@ -453,34 +469,35 @@
         scratch=[pltpu.VMEM((width_x, width_y), jnp.int32), dma((5,))],
     )(in_hbm(source), in_hbm(regions))
     high = lax.ppermute(own, "gz", [(i + 1, i) for i in range(count - 1)])
-    table, b, rho, part, places = call(
+    table, b, rho, part = call(
         own_kernel,
-        [(2 * count_regions, 8, LANES), padded, padded, packed, jax.ShapeDtypeStruct((band // LANES, LANES), jnp.int32)],
-        [HBM] * 4 + [VMEM],
+        [(2 * count_regions, 8, LANES), padded, padded, packed],
+        [HBM] * 3 + [VMEM],
         scratch=[
             pltpu.SMEM(reluctivity.shape, jnp.float32),
             pltpu.SMEM(levels.shape, jnp.float32),
             pltpu.SMEM(seeds.shape, jnp.int32),
-            pltpu.VMEM((band // LANES, LANES), jnp.int32),
-            dma((4,)),
+            dma((3,)),
         ],
         cost=estimate(3),
-    )(in_hbm(reluctivity), in_hbm(levels), in_hbm(seeds), in_hbm(band_cells.reshape(-1, LANES)), own)
+    )(in_hbm(reluctivity), in_hbm(levels), in_hbm(seeds), own)
     own_second, table = ORDER((own, table))
     low = lax.ppermute(own_second, "gz", [(i, i + 1) for i in range(count - 1)])
-    upper, b1, rho1 = call(
+    lists = (band // LANES, LANES)
+    upper, b1, rho1, starts, lanes = call(
         upper_kernel,
-        [packed, padded, padded],
-        [VMEM] * 4,
+        [packed, padded, padded] + [jax.ShapeDtypeStruct(lists, jnp.int32)] * 2,
+        [VMEM] * 4 + [HBM] * 2,
+        scratch=[pltpu.VMEM(lists, jnp.int32), pltpu.VMEM(lists, jnp.int32), dma((2,))],
         cost=estimate(3),
-    )(table, b, rho, high)
+    )(table, b, rho, high, in_hbm(band_cells.reshape(lists)), in_hbm(sector_order.reshape(lists)))
     upper, own_third, high_second = ORDER((upper, own_second, high))
+    relay = lax.ppermute(high_second, "gz", [(i + 1, i) for i in range(0, count - 1, 2)])
     far = lax.ppermute(own_third, "gz", [(i + 2, i) for i in range(1, count - 2, 2)])
-    relay = lax.ppermute(high_second, "gz", [(i + 1, i) for i in range(0, count - 1, 2)])
     w, moments, sums = call(
         field_kernel,
         [padded, (5, 8, LANES), (count, 8, LANES)],
-        [VMEM] * 7 + [ANY, HBM],
+        [VMEM] * 7 + [ANY] * 2,
         scratch=[
             pltpu.VMEM((width_x * (width_y // LANES) * TILE_ROWS, LANES), jnp.float32),
             pltpu.VMEM((band // PER_SEC * 3, 8, LANES), jnp.float32),
@@ -490,7 +507,7 @@
         ],
         limit=10 * 2**20,
         cost=estimate(7),
-    )(b, rho, part, table, low, b1, rho1, places.reshape(-1), in_hbm(sector_order))
+    )(b, rho, part, table, low, b1, rho1, starts.reshape(-1), lanes.reshape(-1))
     (payload,) = call(
         face_kernel,
         [(count, 8, LANES)],
@@ -502,8 +519,6 @@
         final_kernel,
         [(8, half, width_y), (2, cols, sectors, count)],
         [VMEM] * 3,
-        [HBM, VMEM],
-        scratch=[pltpu.VMEM((8, half, width_y), jnp.float32), dma((4,))],
         cost=estimate(2),
     )(got, b, w)
     return solved.reshape(cols, 1, width_x, width_y), forces

time: 46.5 us -> 44.9 us (0.966)
  Pallas kernels: 20.2 us -> 18.6 us
    pallas_call x1, Pallas kernels: 8.05 us -> 6.51 us  [body(): call(field_kernel, [padded, (5, 8, LANES), (count, 8, LANES)], [VMEM] * 7...]
  transfers between devices with their start and end apart: 4 -> 4, of which waited for: 0 -> 0; matrix products, arithmetic and copies ran while one was open for 0% -> 0% of each run, Pallas kernels for 30% -> 28%
where the time goes in v5:
time: 44.9 us; the launch traced here: 44.6 us
  blocking collectives  18.9 us (42%)
  Pallas kernels  18.6 us (41%)
  starting transfers between devices  6.34 us (14%)
  between operations  0.73 us (2%)
    all_to_all x1, blocking collectives, body(): got = lax.all_to_all(payload, 'gz', split_axis=0, concat_axis=0, tiled=True)  18.9 us
    pallas_call x1, Pallas kernels, body(): call(field_kernel, [padded, (5, 8, LANES), (count, 8, LANES)], [VMEM] * 7...  6.51 us
    pallas_call x1, Pallas kernels, body(): call(own_kernel, [(2 * count_regions, 8, LANES), padded, padded, packed],...  3.17 us
    pallas_call x1, Pallas kernels, body(): call(face_kernel, [(count, 8, LANES)], [VMEM] * 11, cost=estimate(4))  3.08 us
    ppermute x1, starting transfers between devices, body(): low = lax.ppermute(own_second, 'gz', [(i, i + 1) for i in range(count - 1)])  3.06 us
    pallas_call x1, Pallas kernels, body(): call(upper_kernel, [packed, padded, padded] + [jax.ShapeDtypeStruct(lists...  2.72 us
    pallas_call x1, Pallas kernels, body(): call(final_kernel, [(8, half, width_y), (2, cols, sectors, count)], [VMEM...  2.08 us
    ppermute x1, starting transfers between devices, body(): lax.ppermute(high_second, 'gz', [(i + 1, i) for i in range(0, count - 1,...  1.29 us
  transfers between devices with their start and end apart: 4, of which 0 were waited for; matrix products, arithmetic and copies ran while one was open for 0% of the time, Pallas kernels for 28%

profile of v5, /device:TPU:0, one launch (start us, length us, event | category | flops | bytes accessed | tf_op | source)
XLA Modules:
  0.0 44.6 jit_solution(2426092413885164489)
XLA Ops:
  0.6 1.1 %shard_map.86.x_ref = f32[2,256,256]{2,1,0:T(8,128)S(1)} custom-call(f32[1,256,256]{2,1,0:T(8,128)} %source_ref.1, s32[1,256,256]{2,1,0:T(8,128)} %regions_ref.1), custom_call_target="tpu_custom_call" | custom-call | tf_op jit(solution)/shard_map/pallas_call | solution.py:465
  1.7 1.3 %collective-permute-start.1 = (f32[2,256,256]{2,1,0:T(8,128)S(1)}, f32[2,256,256]{2,1,0:T(8,128)S(1)}, u32[]{:S(2)}, u32[]{:S(2)}) collective-permute-start(f32[2,256,256]{2,1,0:T(8,128)S(1)} %shard_map.86.x_ref), channel_id=1, source_target_pairs={{1,0},{2,1},{3,2},{4,3},{5,4},{6,5},{7,6},{8,7},{9,8},{10,9},{11,1... | collective-permute-start | bytes 1572872 | tf_op jit(solution)/shard_map/ppermute | solution.py:471
  3.0 3.2 %shard_map.87 = (f32[8,8,128]{2,1,0:T(8,128)S(1)}, f32[130,8,256]{2,1,0:T(8,128)S(1)}, f32[130,8,256]{2,1,0:T(8,128)S(1)}, f32[128,8,256]{2,1,0:T(8,128)S(1)}) custom-call(f32[4]{0:T(128)} %reluct_hbm.1, f32[4]{0:T(128)} %levels_hbm.1, s32[4,4]{1,0:T(4,128)} %seeds_hbm.1, f32[2,256,256]{2,1,0:T(8,128)S(1)} %shard_map.86.x_ref), custom_call_target="tpu_custom_call" | custom-call | flops 3000000 | bytes 9000000 | tf_op jit(solution)/shard_map/pallas_call | solution.py:472
  6.2 3.1 %collective-permute-start = (f32[2,256,256]{2,1,0:T(8,128)S(1)}, f32[2,256,256]{2,1,0:T(8,128)S(1)}, u32[]{:S(2)}, u32[]{:S(2)}) collective-permute-start(f32[2,256,256]{2,1,0:T(8,128)S(1)} %shard_map.86.x_ref), channel_id=1, source_target_pairs={{0,1},{1,2},{2,3},{3,4},{4,5},{5,6},{6,7},{7,8},{8,9},{9,10},{10,1... | collective-permute-start | bytes 1572872 | tf_op jit(solution)/shard_map/ppermute | solution.py:485
  9.3 0.0 collective-permute-done.1.high_ref
  9.3 2.7 %shard_map.88 = (f32[128,8,256]{2,1,0:T(8,128)S(1)}, f32[130,8,256]{2,1,0:T(8,128)S(1)}, f32[130,8,256]{2,1,0:T(8,128)S(1)}, s32[16,128]{1,0:T(8,128)S(1)}, s32[16,128]{1,0:T(8,128)S(1)}) custom-call(f32[8,8,128]{2,1,0:T(8,128)S(1)} %get-tuple-element.25.tab_ref, f32[130,8,256]{2,1,0:T(8,128)S(1)} %get-tuple-element.21.b_ref, ...), custom_call_target="tpu_custom_call" | custom-call | flops 3000000 | bytes 9000000 | tf_op jit(solution)/shard_map/pallas_call | solution.py:487
  12.0 0.7 %collective-permute-start.2 = (f32[2,256,256]{2,1,0:T(8,128)S(1)}, f32[2,256,256]{2,1,0:T(8,128)S(1)}, u32[]{:S(2)}, u32[]{:S(2)}) collective-permute-start(f32[2,256,256]{2,1,0:T(8,128)S(1)} %shard_map.86.x_ref), channel_id=1, source_target_pairs={{3,1},{5,3},{7,5},{9,7},{11,9},{13,11},{15,13},{19,17},{21,19},{23... | collective-permute-start | bytes 1572872 | tf_op jit(solution)/shard_map/ppermute | solution.py:496
  12.7 1.3 %collective-permute-start.3 = (f32[2,256,256]{2,1,0:T(8,128)S(1)}, f32[2,256,256]{2,1,0:T(8,128)S(1)}, u32[]{:S(2)}, u32[]{:S(2)}) collective-permute-start(f32[2,256,256]{2,1,0:T(8,128)S(1)} %collective-permute-done.1.high_ref), channel_id=1, source_target_pairs={{1,0},{3,2},{5,4},{7,6},{9,8},{11,10},{13,12},{15,14},{17,16},{19,... | collective-permute-start | bytes 1572872 | tf_op jit(solution)/shard_map/ppermute | solution.py:495
  14.0 0.0 collective-permute-done.low_ref
  14.0 6.5 %shard_map.89 = (f32[130,8,256]{2,1,0:T(8,128)S(1)}, f32[5,8,128]{2,1,0:T(8,128)S(1)}, f32[16,8,128]{2,1,0:T(8,128)S(1)}) custom-call(f32[130,8,256]{2,1,0:T(8,128)S(1)} %get-tuple-element.21.b_ref, f32[130,8,256]{2,1,0:T(8,128)S(1)} %get-tuple-element.22.rho_ref, f32[128,8,256]{2,1,0:T(8,128)S(1)} %get-tuple-element.23.part_ref, ...), custom_call_target="tpu_custom_call" | custom-call | flops 7000000 | bytes 21000000 | tf_op jit(solution)/shard_map/pallas_call | solution.py:497
  20.5 0.0 collective-permute-done.2.far_ref
  20.5 0.0 collective-permute-done.3.relay_ref
  20.6 3.1 %shard_map.90 = f32[16,8,128]{2,1,0:T(8,128)S(1)} custom-call(f32[130,8,256]{2,1,0:T(8,128)S(1)} %get-tuple-element.21.b_ref, f32[130,8,256]{2,1,0:T(8,128)S(1)} %get-tuple-element.22.rho_ref, f32[130,8,256]{2,1,0:T(8,128)S(1)} %get-tuple-element.31.w_ref, f32[130,8,256]{2,1,0:T(8,128)S(1)} %get-tuple-element.27.b1_ref, ...), custom_call_target="tpu_custom_call" | custom-call | flops 4000000 | bytes 12000000 | tf_op jit(solution)/shard_map/pallas_call | solution.py:511
  23.6 18.9 %all_to_all.5.got_ref = f32[16,8,128]{2,1,0:T(8,128)S(1)} all-to-all(f32[16,8,128]{2,1,0:T(8,128)S(1)} %shard_map.90), channel_id=1, replica_groups=mesh['pos'=2,'gz'=16] {'gz'}, dimensions={0} | all-to-all | bytes 131072 | tf_op jit(solution)/shard_map/all_to_all | solution.py:517
  42.5 2.1 %shard_map.91 = (f32[8,128,256]{2,1,0:T(8,128)}, f32[2,4,2,16]{3,2,1,0:T(2,128)}) custom-call(f32[16,8,128]{2,1,0:T(8,128)S(1)} %all_to_all.5.got_ref, f32[130,8,256]{2,1,0:T(8,128)S(1)} %get-tuple-element.21.b_ref, f32[130,8,256]{2,1,0:T(8,128)S(1)} %get-tuple-element.31.w_ref), custom_call_target="tpu_custom_call" | custom-call | flops 2000000 | bytes 6000000 | tf_op jit(solution)/shard_map/pallas_call | solution.py:518
Async XLA Ops:
  1.7 7.6 %collective-permute-start.1 = (f32[2,256,256]{2,1,0:T(8,128)S(1)}, f32[2,256,256]{2,1,0:T(8,128)S(1)}, u32[]{:S(2)}, u32[]{:S(2)}) collective-permute-start(f32[2,256,256]{2,1,0:T(8,128)S(1)} %shard_map.86.x_ref), channel_id=1, source_target_pairs={{1,0},{2,1},{3,2},{4,3},{5,4},{6,5},{7,6},{8,7},{9,8},{10,9},{11,1... | collective-permute-start | bytes 1572872 | tf_op jit(solution)/shard_map/ppermute | solution.py:471
  6.2 7.8 %collective-permute-start = (f32[2,256,256]{2,1,0:T(8,128)S(1)}, f32[2,256,256]{2,1,0:T(8,128)S(1)}, u32[]{:S(2)}, u32[]{:S(2)}) collective-permute-start(f32[2,256,256]{2,1,0:T(8,128)S(1)} %shard_map.86.x_ref), channel_id=1, source_target_pairs={{0,1},{1,2},{2,3},{3,4},{4,5},{5,6},{6,7},{7,8},{8,9},{9,10},{10,1... | collective-permute-start | bytes 1572872 | tf_op jit(solution)/shard_map/ppermute | solution.py:485
  12.0 8.5 %collective-permute-start.2 = (f32[2,256,256]{2,1,0:T(8,128)S(1)}, f32[2,256,256]{2,1,0:T(8,128)S(1)}, u32[]{:S(2)}, u32[]{:S(2)}) collective-permute-start(f32[2,256,256]{2,1,0:T(8,128)S(1)} %shard_map.86.x_ref), channel_id=1, source_target_pairs={{3,1},{5,3},{7,5},{9,7},{11,9},{13,11},{15,13},{19,17},{21,19},{23... | collective-permute-start | bytes 1572872 | tf_op jit(solution)/shard_map/ppermute | solution.py:496
  12.7 7.8 %collective-permute-start.3 = (f32[2,256,256]{2,1,0:T(8,128)S(1)}, f32[2,256,256]{2,1,0:T(8,128)S(1)}, u32[]{:S(2)}, u32[]{:S(2)}) collective-permute-start(f32[2,256,256]{2,1,0:T(8,128)S(1)} %collective-permute-done.1.high_ref), channel_id=1, source_target_pairs={{1,0},{3,2},{5,4},{7,6},{9,8},{11,10},{13,12},{15,14},{17,16},{19,... | collective-permute-start | bytes 1572872 | tf_op jit(solution)/shard_map/ppermute | solution.py:495

commit v6 on v5

--- a/solution.py
+++ b/solution.py
@@ -10,9 +10,9 @@
 PER_SEC = 64
 LANES = 128
 LOG_LANES = 7
-BLOCK = 32
+SLOTS = 16
+M_BB, M_BW, M_WW, M_SIG, M_PP, M_PW, M_FPP, M_FPW, M_FWW = range(7, 16)
 TILE_ROWS = 24
-M_BB, M_BW, M_WW, M_SIG, M_PP, M_PW, M_FPP, M_FPW, M_FWW = range(96, 105)
 
 VMEM = pl.BlockSpec(memory_space=pltpu.VMEM)
 SMEM = pl.BlockSpec(memory_space=pltpu.SMEM)
@@ -299,7 +299,7 @@
         for sector in range(sectors):
             for field in range(3):
                 total = lane_sum(acc_ref[(index * sectors + sector) * 3 + field])
-                out = jnp.where(place == field * BLOCK + sector, total, out)
+                out = jnp.where(place == field * sectors + sector, total, out)
         sums_ref[index] = out
 
 
@@ -349,7 +349,7 @@
     pp, pw, fpp, fpw, fww = carry[-5:]
     lane_tile = iota((8, LANES), 1)
     scalars = {
-        M_BB: mom_ref[0], M_BW: mom_ref[1], M_WW: mom_ref[2], M_SIG: 0.5 * mom_ref[3],
+        M_BB: mom_ref[0], M_BW: mom_ref[1], M_WW: mom_ref[2], M_SIG: mom_ref[3],
         M_PP: lane_sum(pp), M_PW: lane_sum(pw),
         M_FPP: 0.5 * lane_sum(fpp), M_FPW: 0.5 * lane_sum(fpw), M_FWW: 0.5 * lane_sum(fww),
     }
@@ -357,7 +357,8 @@
     for spot, value in scalars.items():
         tile = jnp.where(lane_tile == spot, value, tile)
     for index in range(out_ref.shape[0]):
-        out_ref[index] = sums_ref[index] + tile
+        spread = pltpu.roll(sums_ref[index] + tile, SLOTS, 1, stride=SLOTS, stride_axis=0)
+        out_ref[index:index + 1, :] = jnp.sum(spread, axis=0, keepdims=True)
 
 
 def final_kernel(got_ref, b_ref, w_ref, sol_ref, force_ref):
@@ -366,32 +367,35 @@
     _, cols, sectors, _ = force_ref.shape
     even = iota((8, LANES), 0) % 2 == 0
     lane = iota((8, LANES), 1)
+    slot = (lane - SLOTS * (iota((8, LANES), 0) + 1)) & (LANES - 1)
 
     def column(value, spot):
-        return value[:, spot:spot + 1]
-
-    whole = [halves_sum(got_ref[index], even) for index in range(count)]
-    zeroth = functools.reduce(jnp.add, whole)
-    norm = column(zeroth, M_BB)
-    curve = column(zeroth, M_BW)
+        return lane_sum(jnp.where(slot == spot, value, 0.0))
+
+    def whole(value, spot):
+        return halves_sum(column(value, spot) + jnp.zeros((8, LANES), jnp.float32), even)
+
+    got = [got_ref[index:index + 1, :] for index in range(count)]
+    zeroth = functools.reduce(jnp.add, got)
+    norm, curve = whole(zeroth, M_BB), whole(zeroth, M_BW)
     step = norm / curve
     first = jnp.zeros((8, LANES), jnp.float32)
     second = first
-    for value in whole:
+    for value in got:
         offset = step - column(value, M_SIG)
         scaled = offset * value
         first = first + scaled
         second = second + offset * scaled
-    new = column(zeroth, M_PP) - 2.0 * column(first, M_PW) + column(second, M_WW)
-    image_residual = column(zeroth, M_PW) - column(first, M_WW)
-    energy = column(zeroth, M_FPP) - 2.0 * column(first, M_FPW) + column(second, M_FWW)
+    new = whole(zeroth, M_PP) - 2.0 * whole(first, M_PW) + whole(second, M_WW)
+    image_residual = whole(zeroth, M_PW) - whole(first, M_WW)
+    energy = whole(zeroth, M_FPP) - 2.0 * whole(first, M_FPW) + whole(second, M_FWW)
     ratio = new / norm
     step_two = new / (energy + 2.0 * ratio * image_residual + ratio * ratio * curve)
     alpha = step + step_two * (1.0 + ratio)
     gamma = -(step_two * step)
 
-    wide_alpha = alpha + jnp.zeros((8, width), jnp.float32)
-    wide_gamma = gamma + jnp.zeros((8, width), jnp.float32)
+    wide_alpha = jnp.concatenate([alpha] * (width // LANES), axis=1)
+    wide_gamma = jnp.concatenate([gamma] * (width // LANES), axis=1)
 
     def rows(block, carry):
         stack = []
@@ -407,14 +411,14 @@
 
     sign = jnp.where(even, 0.25, -0.25)
     coef = sign * jnp.where(
-        lane < BLOCK, alpha * alpha, jnp.where(lane < 2 * BLOCK, alpha * gamma, gamma * gamma)
+        slot < sectors, alpha * alpha, jnp.where(slot < 2 * sectors, alpha * gamma, gamma * gamma)
     )
+    used = jnp.where(slot < 3 * sectors, coef, 0.0)
+    coefs = [jnp.where(slot % sectors == sector, used, 0.0) for sector in range(sectors)]
     tiles = [jnp.zeros((8, LANES), jnp.float32)] * sectors
-    for index in range(count):
-        value = coef * got_ref[index]
-        value = value + pltpu.roll(value, LANES - BLOCK, 1) + pltpu.roll(value, LANES - 2 * BLOCK, 1)
+    for index, value in enumerate(got):
         for sector in range(sectors):
-            tiles[sector] = jnp.where(lane == index, column(value, sector), tiles[sector])
+            tiles[sector] = jnp.where(lane == index, lane_sum(coefs[sector] * value), tiles[sector])
     for sector in range(sectors):
         for part in range(2):
             for c in range(cols):
@@ -457,6 +461,7 @@
     half = width_x // 2
     band = band_cells.shape[0]
     sectors = band // (PER_SEC * count)
+    assert 3 * sectors <= M_BB
     packed, padded = (half, 8, width_y), (half + 2, 8, width_y)
 
 
@@ -510,7 +515,7 @@
     )(b, rho, part, table, low, b1, rho1, starts.reshape(-1), lanes.reshape(-1))
     (payload,) = call(
         face_kernel,
-        [(count, 8, LANES)],
+        [(count, LANES)],
         [VMEM] * 11,
         cost=estimate(4),
     )(b, rho, w, b1, rho1, upper, table, far, relay, sums, moments)

time: 44.9 us -> 43.9 us (0.978)
  blocking collectives: 18.9 us -> 18.4 us
    pallas_call x1, Pallas kernels: 2.08 us -> 1.54 us  [body(): call(final_kernel, [(8, half, width_y), (2, cols, sectors, count)], [VMEM...]
    all_to_all x1, blocking collectives: 18.9 us -> 18.4 us  [body(): got = lax.all_to_all(payload, 'gz', split_axis=0, concat_axis=0, tiled=True)]
where the time goes in v6:
time: 43.9 us; the launch traced here: 43.6 us
  blocking collectives  18.4 us (42%)
  Pallas kernels  18.2 us (41%)
  starting transfers between devices  6.34 us (14%)
  between operations  0.73 us (2%)
    all_to_all x1, blocking collectives, body(): got = lax.all_to_all(payload, 'gz', split_axis=0, concat_axis=0, tiled=True)  18.4 us
    pallas_call x1, Pallas kernels, body(): call(field_kernel, [padded, (5, 8, LANES), (count, 8, LANES)], [VMEM] * 7...  6.51 us
    pallas_call x1, Pallas kernels, body(): call(own_kernel, [(2 * count_regions, 8, LANES), padded, padded, packed],...  3.17 us
    pallas_call x1, Pallas kernels, body(): call(face_kernel, [(count, LANES)], [VMEM] * 11, cost=estimate(4))  3.16 us
    ppermute x1, starting transfers between devices, body(): low = lax.ppermute(own_second, 'gz', [(i, i + 1) for i in range(count - 1)])  3.06 us
    pallas_call x1, Pallas kernels, body(): call(upper_kernel, [packed, padded, padded] + [jax.ShapeDtypeStruct(lists...  2.72 us
    pallas_call x1, Pallas kernels, body(): call(final_kernel, [(8, half, width_y), (2, cols, sectors, count)], [VMEM...  1.54 us
    ppermute x1, starting transfers between devices, body(): lax.ppermute(high_second, 'gz', [(i + 1, i) for i in range(0, count - 1,...  1.29 us
  transfers between devices with their start and end apart: 4, of which 0 were waited for; matrix products, arithmetic and copies ran while one was open for 0% of the time, Pallas kernels for 28%

profile of v6, /device:TPU:0, one launch (start us, length us, event | category | flops | bytes accessed | tf_op | source)
XLA Modules:
  0.0 43.6 jit_solution(17769996879251802182)
XLA Ops:
  0.6 1.1 %shard_map.86.x_ref = f32[2,256,256]{2,1,0:T(8,128)S(1)} custom-call(f32[1,256,256]{2,1,0:T(8,128)} %source_ref.1, s32[1,256,256]{2,1,0:T(8,128)} %regions_ref.1), custom_call_target="tpu_custom_call" | custom-call | tf_op jit(solution)/shard_map/pallas_call | solution.py:470
  1.7 1.3 %collective-permute-start.1 = (f32[2,256,256]{2,1,0:T(8,128)S(1)}, f32[2,256,256]{2,1,0:T(8,128)S(1)}, u32[]{:S(2)}, u32[]{:S(2)}) collective-permute-start(f32[2,256,256]{2,1,0:T(8,128)S(1)} %shard_map.86.x_ref), channel_id=1, source_target_pairs={{1,0},{2,1},{3,2},{4,3},{5,4},{6,5},{7,6},{8,7},{9,8},{10,9},{11,1... | collective-permute-start | bytes 1572872 | tf_op jit(solution)/shard_map/ppermute | solution.py:476
  3.0 3.2 %shard_map.87 = (f32[8,8,128]{2,1,0:T(8,128)S(1)}, f32[130,8,256]{2,1,0:T(8,128)S(1)}, f32[130,8,256]{2,1,0:T(8,128)S(1)}, f32[128,8,256]{2,1,0:T(8,128)S(1)}) custom-call(f32[4]{0:T(128)} %reluct_hbm.1, f32[4]{0:T(128)} %levels_hbm.1, s32[4,4]{1,0:T(4,128)} %seeds_hbm.1, f32[2,256,256]{2,1,0:T(8,128)S(1)} %shard_map.86.x_ref), custom_call_target="tpu_custom_call" | custom-call | flops 3000000 | bytes 9000000 | tf_op jit(solution)/shard_map/pallas_call | solution.py:477
  6.2 3.1 %collective-permute-start = (f32[2,256,256]{2,1,0:T(8,128)S(1)}, f32[2,256,256]{2,1,0:T(8,128)S(1)}, u32[]{:S(2)}, u32[]{:S(2)}) collective-permute-start(f32[2,256,256]{2,1,0:T(8,128)S(1)} %shard_map.86.x_ref), channel_id=1, source_target_pairs={{0,1},{1,2},{2,3},{3,4},{4,5},{5,6},{6,7},{7,8},{8,9},{9,10},{10,1... | collective-permute-start | bytes 1572872 | tf_op jit(solution)/shard_map/ppermute | solution.py:490
  9.3 0.0 collective-permute-done.1.high_ref
  9.3 2.7 %shard_map.88 = (f32[128,8,256]{2,1,0:T(8,128)S(1)}, f32[130,8,256]{2,1,0:T(8,128)S(1)}, f32[130,8,256]{2,1,0:T(8,128)S(1)}, s32[16,128]{1,0:T(8,128)S(1)}, s32[16,128]{1,0:T(8,128)S(1)}) custom-call(f32[8,8,128]{2,1,0:T(8,128)S(1)} %get-tuple-element.25.tab_ref, f32[130,8,256]{2,1,0:T(8,128)S(1)} %get-tuple-element.21.b_ref, ...), custom_call_target="tpu_custom_call" | custom-call | flops 3000000 | bytes 9000000 | tf_op jit(solution)/shard_map/pallas_call | solution.py:492
  12.0 0.7 %collective-permute-start.2 = (f32[2,256,256]{2,1,0:T(8,128)S(1)}, f32[2,256,256]{2,1,0:T(8,128)S(1)}, u32[]{:S(2)}, u32[]{:S(2)}) collective-permute-start(f32[2,256,256]{2,1,0:T(8,128)S(1)} %shard_map.86.x_ref), channel_id=1, source_target_pairs={{3,1},{5,3},{7,5},{9,7},{11,9},{13,11},{15,13},{19,17},{21,19},{23... | collective-permute-start | bytes 1572872 | tf_op jit(solution)/shard_map/ppermute | solution.py:501
  12.7 1.3 %collective-permute-start.3 = (f32[2,256,256]{2,1,0:T(8,128)S(1)}, f32[2,256,256]{2,1,0:T(8,128)S(1)}, u32[]{:S(2)}, u32[]{:S(2)}) collective-permute-start(f32[2,256,256]{2,1,0:T(8,128)S(1)} %collective-permute-done.1.high_ref), channel_id=1, source_target_pairs={{1,0},{3,2},{5,4},{7,6},{9,8},{11,10},{13,12},{15,14},{17,16},{19,... | collective-permute-start | bytes 1572872 | tf_op jit(solution)/shard_map/ppermute | solution.py:500
  14.0 0.0 collective-permute-done.low_ref
  14.0 6.5 %shard_map.89 = (f32[130,8,256]{2,1,0:T(8,128)S(1)}, f32[5,8,128]{2,1,0:T(8,128)S(1)}, f32[16,8,128]{2,1,0:T(8,128)S(1)}) custom-call(f32[130,8,256]{2,1,0:T(8,128)S(1)} %get-tuple-element.21.b_ref, f32[130,8,256]{2,1,0:T(8,128)S(1)} %get-tuple-element.22.rho_ref, f32[128,8,256]{2,1,0:T(8,128)S(1)} %get-tuple-element.23.part_ref, ...), custom_call_target="tpu_custom_call" | custom-call | flops 7000000 | bytes 21000000 | tf_op jit(solution)/shard_map/pallas_call | solution.py:502
  20.5 0.0 collective-permute-done.2.far_ref
  20.5 0.0 collective-permute-done.3.relay_ref
  20.6 3.2 %shard_map.90 = f32[16,128]{1,0:T(8,128)S(1)} custom-call(f32[130,8,256]{2,1,0:T(8,128)S(1)} %get-tuple-element.21.b_ref, f32[130,8,256]{2,1,0:T(8,128)S(1)} %get-tuple-element.22.rho_ref, f32[130,8,256]{2,1,0:T(8,128)S(1)} %get-tuple-element.31.w_ref, f32[130,8,256]{2,1,0:T(8,128)S(1)} %get-tuple-element.27.b1_ref, ...), custom_call_target="tpu_custom_call" | custom-call | flops 4000000 | bytes 12000000 | tf_op jit(solution)/shard_map/pallas_call | solution.py:516
  23.7 18.4 %all_to_all.11 = f32[16,1,128]{2,1,0:T(1,128)S(1)} all-to-all(f32[16,1,128]{2,1,0:T(1,128)S(1)} %bitcast.12), channel_id=1, replica_groups=mesh['pos'=2,'gz'=16] {'gz'}, dimensions={0} | all-to-all | bytes 16384 | tf_op jit(solution)/shard_map/all_to_all | solution.py:522
  42.1 1.5 %shard_map.91 = (f32[8,128,256]{2,1,0:T(8,128)}, f32[2,4,2,16]{3,2,1,0:T(2,128)}) custom-call(f32[16,128]{1,0:T(8,128)S(1)} %bitcast.11, f32[130,8,256]{2,1,0:T(8,128)S(1)} %get-tuple-element.21.b_ref, f32[130,8,256]{2,1,0:T(8,128)S(1)} %get-tuple-element.31.w_ref), custom_call_target="tpu_custom_call" | custom-call | flops 2000000 | bytes 6000000 | tf_op jit(solution)/shard_map/pallas_call | solution.py:523
Async XLA Ops:
  1.7 7.6 %collective-permute-start.1 = (f32[2,256,256]{2,1,0:T(8,128)S(1)}, f32[2,256,256]{2,1,0:T(8,128)S(1)}, u32[]{:S(2)}, u32[]{:S(2)}) collective-permute-start(f32[2,256,256]{2,1,0:T(8,128)S(1)} %shard_map.86.x_ref), channel_id=1, source_target_pairs={{1,0},{2,1},{3,2},{4,3},{5,4},{6,5},{7,6},{8,7},{9,8},{10,9},{11,1... | collective-permute-start | bytes 1572872 | tf_op jit(solution)/shard_map/ppermute | solution.py:476
  6.2 7.8 %collective-permute-start = (f32[2,256,256]{2,1,0:T(8,128)S(1)}, f32[2,256,256]{2,1,0:T(8,128)S(1)}, u32[]{:S(2)}, u32[]{:S(2)}) collective-permute-start(f32[2,256,256]{2,1,0:T(8,128)S(1)} %shard_map.86.x_ref), channel_id=1, source_target_pairs={{0,1},{1,2},{2,3},{3,4},{4,5},{5,6},{6,7},{7,8},{8,9},{9,10},{10,1... | collective-permute-start | bytes 1572872 | tf_op jit(solution)/shard_map/ppermute | solution.py:490
  12.0 8.5 %collective-permute-start.2 = (f32[2,256,256]{2,1,0:T(8,128)S(1)}, f32[2,256,256]{2,1,0:T(8,128)S(1)}, u32[]{:S(2)}, u32[]{:S(2)}) collective-permute-start(f32[2,256,256]{2,1,0:T(8,128)S(1)} %shard_map.86.x_ref), channel_id=1, source_target_pairs={{3,1},{5,3},{7,5},{9,7},{11,9},{13,11},{15,13},{19,17},{21,19},{23... | collective-permute-start | bytes 1572872 | tf_op jit(solution)/shard_map/ppermute | solution.py:501
  12.7 7.8 %collective-permute-start.3 = (f32[2,256,256]{2,1,0:T(8,128)S(1)}, f32[2,256,256]{2,1,0:T(8,128)S(1)}, u32[]{:S(2)}, u32[]{:S(2)}) collective-permute-start(f32[2,256,256]{2,1,0:T(8,128)S(1)} %collective-permute-done.1.high_ref), channel_id=1, source_target_pairs={{1,0},{3,2},{5,4},{7,6},{9,8},{11,10},{13,12},{15,14},{17,16},{19,... | collective-permute-start | bytes 1572872 | tf_op jit(solution)/shard_map/ppermute | solution.py:500

commit v7 on v6

--- a/solution.py
+++ b/solution.py
@@ -72,6 +72,41 @@
     return (flow - flow_prev) + (along - back), flow
 
 
+def sweep(x_ref, b_ref, rho_ref, even, table, emit):
+    half, width = b_ref.shape[0] - 2, b_ref.shape[2]
+    lane = iota((8, width), 1)
+    first_lane, last_lane = lane == 0, lane == width - 1
+
+    def put(row, pair):
+        b_ref[row + 1], rho_ref[row + 1] = pair
+        return pair
+
+    start = put(0, build((x_ref,), 0, half, even, table))
+    last = build((x_ref,), half - 1, half, even, table)
+    below = put(-1, tuple(jnp.where(even, 0.0, pltpu.roll(value, 1, 0)) for value in last))
+    above = tuple(jnp.where(even, pltpu.roll(value, 7, 0), 0.0) for value in start)
+
+    def apply(block, carry):
+        value, rho, flow = carry
+        for step in range(16):
+            row = block * 16 + step
+            if step < 15:
+                value_next, rho_next = put(row + 1, build((x_ref,), row + 1, half, even, table))
+            else:
+                end = row + 1 == half
+                built = build((x_ref,), jnp.where(end, 0, row + 1), half, even, table)
+                value_next, rho_next = put(
+                    row + 1, tuple(jnp.where(end, edge, inner) for edge, inner in zip(above, built))
+                )
+            total, flow = in_plane(value, rho, value_next, rho_next, flow, first_lane, last_lane)
+            emit(row, value, rho, total)
+            value, rho = value_next, rho_next
+        return value, rho, flow
+
+    flow = (below[1] + start[1]) * (below[0] - start[0])
+    lax.fori_loop(0, half // 16, apply, (*start, flow))
+
+
 def fetch(pairs, sems):
     copies = [pltpu.make_async_copy(src, dst, sems.at[i]) for i, (src, dst) in enumerate(pairs)]
     for copy in copies:
@@ -79,63 +114,88 @@
     return copies
 
 
-def pack_kernel(source_ref, regions_ref, x_ref, region_buf, sems):
+def pack_kernel(
+    source_ref, regions_ref, reluct_hbm, levels_hbm, seeds_hbm, x_ref, tab_ref,
+    region_buf, reluct_ref, levels_ref, seeds_ref, sems,
+):
     rows = x_ref.shape[1] // 4
     spans = [pl.ds(part * rows, rows) for part in range(4)]
-    pairs = [(source_ref.at[0], x_ref.at[0])]
+    pairs = [(reluct_hbm, reluct_ref), (levels_hbm, levels_ref), (seeds_hbm, seeds_ref)]
+    pairs += [(source_ref.at[0], x_ref.at[0])]
     pairs += [(regions_ref.at[0, at], region_buf.at[at]) for at in spans]
     copies = fetch(pairs, sems)
-    for at, copy in zip(spans, copies[1:]):
+    for copy in copies[:3]:
         copy.wait()
-        x_ref[1, at, :] = (region_buf[at, :] + 1).astype(jnp.float32)
-    copies[0].wait()
-
-
-def own_kernel(
-    reluct_hbm, levels_hbm, seeds_hbm, x_ref, tab_ref, b_ref, rho_ref, part_ref,
-    reluct_ref, levels_ref, seeds_ref, sems,
-):
-    pairs = [(reluct_hbm, reluct_ref), (levels_hbm, levels_ref), (seeds_hbm, seeds_ref)]
-    for copy in fetch(pairs, sems):
-        copy.wait()
-    half, _, width = part_ref.shape
     count = reluct_ref.shape[0]
-    cols = seeds_ref.shape[0]
     column = iota((8, LANES), 0) // 2
     for region in range(count):
         strength = jnp.zeros((8, LANES), jnp.float32)
-        for c in range(cols):
+        for c in range(seeds_ref.shape[0]):
             strength = jnp.where(column == c, levels_ref[seeds_ref[c, region]], strength)
         tab_ref[region] = strength
         tab_ref[count + region] = jnp.full((8, LANES), reluct_ref[region], jnp.float32)
-    table = load_table(tab_ref, width)
+    for at, copy in zip(spans, copies[4:]):
+        copy.wait()
+        x_ref[1, at, :] = (region_buf[at, :] + 1).astype(jnp.float32)
+    copies[3].wait()
+
+
+def forces_of(row, half, even, lane):
+    width = lane.shape[1]
+    normal_y = (lane.astype(jnp.float32) - 0.5 * (width - 1)) / (0.5 * width)
+    upper = jnp.where(even, 0.0, 1.0)
+    normal_x = upper + (row.astype(jnp.float32) - (half - 0.5)) / half
+    return lambda diff, cross: (normal_x * diff - normal_y * cross, normal_x * cross + normal_y * diff)
+
+
+def put_tiles(ref, row, half, rows, shift, even, force_x, force_y):
+    across = force_x.shape[1] // LANES
+    lower = jnp.where(even, force_x, pltpu.roll(force_y, 1, 0))
+    higher = jnp.where(even, pltpu.roll(force_x, 7, 0), force_y)
+    for tile_index in range(across):
+        part = slice(tile_index * LANES, (tile_index + 1) * LANES)
+        for base, value in ((0, lower), (half * across, higher)):
+            first = pl.multiple_of((base + row * across + tile_index) * rows + shift, 8)
+            ref[pl.ds(first, 8), :] = value[:, part]
+
+
+def own_kernel(
+    tab_ref, x_ref, band_hbm, order_hbm, b_ref, rho_ref, part_ref, tile_ref, start_ref, lane_ref,
+    band_ref, order_ref, sems,
+):
+    copies = fetch([(band_hbm, band_ref), (order_hbm, order_ref)], sems)
+    half, _, width = part_ref.shape
     even = iota((8, width), 0) % 2 == 0
     lane = iota((8, width), 1)
     first_lane, last_lane = lane == 0, lane == width - 1
 
-    def fill(block, carry):
-        for step in range(8):
-            row = block * 8 + step
-            b_ref[row + 1], rho_ref[row + 1] = build((x_ref,), row, half, even, table)
-        return carry
-
-    lax.fori_loop(0, half // 8, fill, 0)
-    seams(b_ref, even)
-    seams(rho_ref, even)
-
-    def apply(block, carry):
-        value, rho, flow = carry
+    def emit(row, value, rho, total):
+        part_ref[row] = value + total
+
+    sweep(x_ref, b_ref, rho_ref, even, load_table(tab_ref, width), emit)
+
+    def forces(block, carry):
         for step in range(16):
             row = block * 16 + step
-            value_next, rho_next = b_ref[row + 2], rho_ref[row + 2]
-            total, flow = in_plane(value, rho, value_next, rho_next, flow, first_lane, last_lane)
-            part_ref[row] = value + total
-            value, rho = value_next, rho_next
-        return value, rho, flow
-
-    value, rho = b_ref[1], rho_ref[1]
-    flow = (rho_ref[0] + rho) * (b_ref[0] - value)
-    lax.fori_loop(0, half // 16, apply, (value, rho, flow))
+            b = b_ref[row + 1]
+            gx = after(b, last_lane) - before(b, first_lane)
+            gy = b_ref[row + 2] - b_ref[row]
+            components = forces_of(row, half, even, lane)(0.5 * (gx * gx - gy * gy), gx * gy)
+            put_tiles(tile_ref, row, half, TILE_ROWS, 0, even, *components)
+        return carry
+
+    lax.fori_loop(0, half // 16, forces, 0)
+    for copy in copies:
+        copy.wait()
+    locate(band_ref, order_ref, start_ref, lane_ref)
+
+
+def lane_sum(value):
+    return jnp.sum(value, axis=1, keepdims=True)
+
+
+def halves_sum(value, even):
+    return value + jnp.where(even, pltpu.roll(value, 7, 0), pltpu.roll(value, 1, 0))
 
 
 def locate(band_ref, order_ref, start_ref, lane_ref):
@@ -159,55 +219,18 @@
     lax.fori_loop(0, order_ref.shape[0], chunk, 0, unroll=True if order_ref.shape[0] <= 16 else 8)
 
 
-def upper_kernel(
-    tab_ref, b_ref, rho_ref, high_ref, band_hbm, order_hbm, part_ref, b1_ref, rho1_ref, start_ref, lane_ref,
-    band_ref, order_ref, sems,
-):
-    copies = fetch([(band_hbm, band_ref), (order_hbm, order_ref)], sems)
-    half, _, width = part_ref.shape
-    table = load_table(tab_ref, width)
+def upper_kernel(tab_ref, b_ref, rho_ref, high_ref, part_ref, b1_ref, rho1_ref):
+    width = part_ref.shape[2]
     even = iota((8, width), 0) % 2 == 0
-    lane = iota((8, width), 1)
-    first_lane, last_lane = lane == 0, lane == width - 1
-
-    def fill(block, carry):
-        for step in range(8):
-            row = block * 8 + step
-            b1_ref[row + 1], rho1_ref[row + 1] = build((high_ref,), row, half, even, table)
-        return carry
-
-    lax.fori_loop(0, half // 8, fill, 0)
-    seams(b1_ref, even)
-    seams(rho1_ref, even)
-
-    def apply(block, carry):
-        value, rho, flow = carry
-        for step in range(16):
-            row = block * 16 + step
-            value_next, rho_next = b1_ref[row + 2], rho1_ref[row + 2]
-            total, flow = in_plane(value, rho, value_next, rho_next, flow, first_lane, last_lane)
-            part_ref[row] = value + total + (rho + rho_ref[row + 1]) * (value - b_ref[row + 1])
-            value, rho = value_next, rho_next
-        return value, rho, flow
-
-    value, rho = b1_ref[1], rho1_ref[1]
-    flow = (rho1_ref[0] + rho) * (b1_ref[0] - value)
-    lax.fori_loop(0, half // 16, apply, (value, rho, flow))
-    for copy in copies:
-        copy.wait()
-    locate(band_ref, order_ref, start_ref, lane_ref)
-
-
-def lane_sum(value):
-    return jnp.sum(value, axis=1, keepdims=True)
-
-
-def halves_sum(value, even):
-    return value + jnp.where(even, pltpu.roll(value, 7, 0), pltpu.roll(value, 1, 0))
+
+    def emit(row, value, rho, total):
+        part_ref[row] = value + total + (rho + rho_ref[row + 1]) * (value - b_ref[row + 1])
+
+    sweep(high_ref, b1_ref, rho1_ref, even, load_table(tab_ref, width), emit)
 
 
 def field_kernel(
-    b_ref, rho_ref, part_ref, tab_ref, low_ref, b1_ref, rho1_ref, start_any, lane_any,
+    b_ref, rho_ref, part_ref, tab_ref, low_ref, b1_ref, rho1_ref, _aliased, start_any, lane_any,
     w_ref, mom_ref, sums_ref, field_ref, acc_ref, start_smem, lane_smem, sems,
 ):
     half, _, width = part_ref.shape
@@ -241,11 +264,6 @@
     mom_ref[0], mom_ref[1], mom_ref[2] = bb, bw, ww
     mom_ref[3] = jnp.minimum(jnp.maximum(shift, 0.0), 2.0)
 
-    normal_y = (lane.astype(jnp.float32) - 0.5 * (width - 1)) / (0.5 * width)
-    upper = jnp.where(even, 0.0, 1.0)
-    across = width // LANES
-    lower_tiles = half * across
-
     def forces(block, carry):
         for step in range(16):
             row = block * 16 + step
@@ -254,23 +272,11 @@
             gx_w = after(w, last_lane) - before(w, first_lane)
             gy_b = b_ref[row + 2] - b_ref[row]
             gy_w = w_ref[row + 2] - w_ref[row]
-            normal_x = upper + (row.astype(jnp.float32) - (half - 0.5)) / half
-            pairs = (
-                (0.5 * (gx_b * gx_b - gy_b * gy_b), gx_b * gy_b),
-                (gx_b * gx_w - gy_b * gy_w, gx_b * gy_w + gx_w * gy_b),
-                (0.5 * (gx_w * gx_w - gy_w * gy_w), gx_w * gy_w),
-            )
-            for index, (diff, cross) in enumerate(pairs):
-                force_x = normal_x * diff - normal_y * cross
-                force_y = normal_x * cross + normal_y * diff
-                lower = jnp.where(even, force_x, pltpu.roll(force_y, 1, 0))
-                higher = jnp.where(even, pltpu.roll(force_x, 7, 0), force_y)
-                for tile_index in range(across):
-                    part = slice(tile_index * LANES, (tile_index + 1) * LANES)
-                    at = row * across + tile_index
-                    for base, value in ((0, lower), (lower_tiles, higher)):
-                        first = pl.multiple_of((base + at) * TILE_ROWS + 8 * index, 8)
-                        field_ref[pl.ds(first, 8), :] = value[:, part]
+            components = forces_of(row, half, even, lane)
+            mixed = components(gx_b * gx_w - gy_b * gy_w, gx_b * gy_w + gx_w * gy_b)
+            square = components(0.5 * (gx_w * gx_w - gy_w * gy_w), gx_w * gy_w)
+            put_tiles(field_ref, row, half, TILE_ROWS, 8, even, *mixed)
+            put_tiles(field_ref, row, half, TILE_ROWS, 16, even, *square)
         return carry
 
     lax.fori_loop(0, half // 16, forces, 0)
@@ -286,9 +292,10 @@
         for step in range(PER_SEC):
             start = start_smem[sector * PER_SEC + step]
             here = place == lane_smem[sector * PER_SEC + step]
-            for field in range(3):
-                first = pl.multiple_of(start + 8 * field, 8)
-                accs[field] += jnp.where(here, field_ref[pl.ds(first, 8), :], 0.0)
+            for field, (ref, first) in enumerate(
+                ((field_ref, start), (field_ref, start + 8), (field_ref, start + 16))
+            ):
+                accs[field] += jnp.where(here, ref[pl.ds(pl.multiple_of(first, 8), 8), :], 0.0)
         for field in range(3):
             acc_ref[sector * 3 + field] = accs[field]
         return carry
@@ -426,7 +433,7 @@
                 force_ref[part, c, sector:sector + 1, :] = tiles[sector][at:at + 1, :count]
 
 
-def call(kernel, outs, in_specs, out_specs=None, scratch=(), limit=4 * 2**20, cost=None):
+def call(kernel, outs, in_specs, out_specs=None, scratch=(), limit=4 * 2**20, cost=None, alias=None):
     shapes = [
         jax.ShapeDtypeStruct(out, jnp.float32) if isinstance(out, tuple) else out
         for out in outs
@@ -439,6 +446,7 @@
         scratch_shapes=list(scratch),
         compiler_params=pltpu.CompilerParams(vmem_limit_bytes=limit),
         cost_estimate=cost,
+        input_output_aliases=alias or {},
     )
 
 
@@ -467,44 +475,45 @@
 
     dma = pltpu.SemaphoreType.DMA
 
-    (own,) = call(
+    own, table = call(
         pack_kernel,
-        [(2, width_x, width_y)],
-        [HBM] * 2,
-        scratch=[pltpu.VMEM((width_x, width_y), jnp.int32), dma((5,))],
-    )(in_hbm(source), in_hbm(regions))
-    high = lax.ppermute(own, "gz", [(i + 1, i) for i in range(count - 1)])
-    table, b, rho, part = call(
-        own_kernel,
-        [(2 * count_regions, 8, LANES), padded, padded, packed],
-        [HBM] * 3 + [VMEM],
+        [(2, width_x, width_y), (2 * count_regions, 8, LANES)],
+        [HBM] * 5,
         scratch=[
+            pltpu.VMEM((width_x, width_y), jnp.int32),
             pltpu.SMEM(reluctivity.shape, jnp.float32),
             pltpu.SMEM(levels.shape, jnp.float32),
             pltpu.SMEM(seeds.shape, jnp.int32),
-            dma((3,)),
+            dma((8,)),
         ],
-        cost=estimate(3),
-    )(in_hbm(reluctivity), in_hbm(levels), in_hbm(seeds), own)
-    own_second, table = ORDER((own, table))
-    low = lax.ppermute(own_second, "gz", [(i, i + 1) for i in range(count - 1)])
+    )(in_hbm(source), in_hbm(regions), in_hbm(reluctivity), in_hbm(levels), in_hbm(seeds))
+    high = lax.ppermute(own, "gz", [(i + 1, i) for i in range(count - 1)])
     lists = (band // LANES, LANES)
-    upper, b1, rho1, starts, lanes = call(
-        upper_kernel,
-        [packed, padded, padded] + [jax.ShapeDtypeStruct(lists, jnp.int32)] * 2,
-        [VMEM] * 4 + [HBM] * 2,
+    tile_rows = width_x * (width_y // LANES) * TILE_ROWS
+    b, rho, part, own_tiles, starts, lanes = call(
+        own_kernel,
+        [padded, padded, packed, (tile_rows, LANES)] + [jax.ShapeDtypeStruct(lists, jnp.int32)] * 2,
+        [VMEM] * 2 + [HBM] * 2,
         scratch=[pltpu.VMEM(lists, jnp.int32), pltpu.VMEM(lists, jnp.int32), dma((2,))],
         cost=estimate(3),
-    )(table, b, rho, high, in_hbm(band_cells.reshape(lists)), in_hbm(sector_order.reshape(lists)))
+    )(table, own, in_hbm(band_cells.reshape(lists)), in_hbm(sector_order.reshape(lists)))
+    own_second, b = ORDER((own, b))
+    low = lax.ppermute(own_second, "gz", [(i, i + 1) for i in range(count - 1)])
+    upper, b1, rho1 = call(
+        upper_kernel,
+        [packed, padded, padded],
+        [VMEM] * 4,
+        cost=estimate(3),
+    )(table, b, rho, high)
     upper, own_third, high_second = ORDER((upper, own_second, high))
     relay = lax.ppermute(high_second, "gz", [(i + 1, i) for i in range(0, count - 1, 2)])
     far = lax.ppermute(own_third, "gz", [(i + 2, i) for i in range(1, count - 2, 2)])
-    w, moments, sums = call(
+    w, moments, sums, _ = call(
         field_kernel,
-        [padded, (5, 8, LANES), (count, 8, LANES)],
-        [VMEM] * 7 + [ANY] * 2,
+        [padded, (5, 8, LANES), (count, 8, LANES), (tile_rows, LANES)],
+        [VMEM] * 8 + [ANY] * 2,
+        alias={7: 3},
         scratch=[
-            pltpu.VMEM((width_x * (width_y // LANES) * TILE_ROWS, LANES), jnp.float32),
             pltpu.VMEM((band // PER_SEC * 3, 8, LANES), jnp.float32),
             pltpu.SMEM((band,), jnp.int32),
             pltpu.SMEM((band,), jnp.int32),
@@ -512,7 +521,7 @@
         ],
         limit=10 * 2**20,
         cost=estimate(7),
-    )(b, rho, part, table, low, b1, rho1, starts.reshape(-1), lanes.reshape(-1))
+    )(b, rho, part, table, low, b1, rho1, own_tiles, starts.reshape(-1), lanes.reshape(-1))
     (payload,) = call(
         face_kernel,
         [(count, LANES)],

time: 43.9 us -> 43.1 us (0.982)
  Pallas kernels: 18.2 us -> 17.1 us
    pallas_call x4, Pallas kernels: 13.5 us -> 12.4 us  [the longest x1 6.13 us: body(): call(field_kernel, [padded, (5, 8, LANES), (count, 8, LANES), (tile_rows,...]
  transfers between devices with their start and end apart: 4 -> 4, of which waited for: 0 -> 0; matrix products, arithmetic and copies ran while one was open for 0% -> 0% of each run, Pallas kernels for 28% -> 26%
where the time goes in v7:
time: 43.1 us; the launch traced here: 42.8 us
  blocking collectives  18.7 us (43%)
  Pallas kernels  17.1 us (40%)
  starting transfers between devices  6.34 us (15%)
  between operations  0.73 us (2%)
    all_to_all x1, blocking collectives, body(): got = lax.all_to_all(payload, 'gz', split_axis=0, concat_axis=0, tiled=True)  18.7 us
    pallas_call x1, Pallas kernels, body(): call(field_kernel, [padded, (5, 8, LANES), (count, 8, LANES), (tile_rows,...  6.13 us
    pallas_call x1, Pallas kernels, body(): call(own_kernel, [padded, padded, packed, (tile_rows, LANES)] + [jax.Shap...  3.33 us
    pallas_call x1, Pallas kernels, body(): call(face_kernel, [(count, LANES)], [VMEM] * 11, cost=estimate(4))  3.19 us
    ppermute x1, starting transfers between devices, body(): low = lax.ppermute(own_second, 'gz', [(i, i + 1) for i in range(count - 1)])  3.06 us
    pallas_call x1, Pallas kernels, body(): call(upper_kernel, [packed, padded, padded], [VMEM] * 4, cost=estimate(3))  1.8 us
    pallas_call x1, Pallas kernels, body(): call(final_kernel, [(8, half, width_y), (2, cols, sectors, count)], [VMEM...  1.54 us
    ppermute x1, starting transfers between devices, body(): lax.ppermute(high_second, 'gz', [(i + 1, i) for i in range(0, count - 1,...  1.29 us
  transfers between devices with their start and end apart: 4, of which 0 were waited for; matrix products, arithmetic and copies ran while one was open for 0% of the time, Pallas kernels for 26%

profile of v7, /device:TPU:0, one launch (start us, length us, event | category | flops | bytes accessed | tf_op | source)
XLA Modules:
  0.0 42.8 jit_solution(15696510219705313648)
XLA Ops:
  0.6 1.1 %shard_map.86 = (f32[2,256,256]{2,1,0:T(8,128)S(1)}, f32[8,8,128]{2,1,0:T(8,128)S(1)}) custom-call(f32[1,256,256]{2,1,0:T(8,128)} %source_ref.1, s32[1,256,256]{2,1,0:T(8,128)} %regions_ref.1, f32[4]{0:T(128)} %reluct_hbm.1, f32[4]{0:T(128)} %levels_hbm.1, s32[4,4]{1,0:T(4,128)} %seeds_hbm.1), custom_call_target="tpu_custom_call" | custom-call | tf_op jit(solution)/shard_map/pallas_call | solution.py:478
  1.7 1.3 %collective-permute-start.1 = (f32[2,256,256]{2,1,0:T(8,128)S(1)}, f32[2,256,256]{2,1,0:T(8,128)S(1)}, u32[]{:S(2)}, u32[]{:S(2)}) collective-permute-start(f32[2,256,256]{2,1,0:T(8,128)S(1)} %get-tuple-element.38.x_ref), channel_id=1, source_target_pairs={{1,0},{2,1},{3,2},{4,3},{5,4},{6,5},{7,6},{8,7},{9,8},{10,9},{11,1... | collective-permute-start | bytes 1572872 | tf_op jit(solution)/shard_map/ppermute | solution.py:490
  3.0 3.3 %shard_map.87 = (f32[130,8,256]{2,1,0:T(8,128)S(1)}, f32[130,8,256]{2,1,0:T(8,128)S(1)}, f32[128,8,256]{2,1,0:T(8,128)S(1)}, f32[12288,128]{1,0:T(8,128)S(1)}, s...) custom-call(f32[8,8,128]{2,1,0:T(8,128)S(1)} %get-tuple-element.24.tab_ref, f32[2,256,256]{2,1,0:T(8,128)S(1)} %get-tuple-element.38.x_ref, ...), custom_call_target="tpu_custom_call" | custom-call | flops 3000000 | bytes 9000000 | tf_op jit(solution)/shard_map/pallas_call | solution.py:493
  6.4 3.1 %collective-permute-start = (f32[2,256,256]{2,1,0:T(8,128)S(1)}, f32[2,256,256]{2,1,0:T(8,128)S(1)}, u32[]{:S(2)}, u32[]{:S(2)}) collective-permute-start(f32[2,256,256]{2,1,0:T(8,128)S(1)} %get-tuple-element.38.x_ref), channel_id=1, source_target_pairs={{0,1},{1,2},{2,3},{3,4},{4,5},{5,6},{6,7},{7,8},{8,9},{9,10},{10,1... | collective-permute-start | bytes 1572872 | tf_op jit(solution)/shard_map/ppermute | solution.py:501
  9.4 0.0 collective-permute-done.1.high_ref
  9.4 1.8 %shard_map.88 = (f32[128,8,256]{2,1,0:T(8,128)S(1)}, f32[130,8,256]{2,1,0:T(8,128)S(1)}, f32[130,8,256]{2,1,0:T(8,128)S(1)}) custom-call(f32[8,8,128]{2,1,0:T(8,128)S(1)} %get-tuple-element.24.tab_ref, f32[130,8,256]{2,1,0:T(8,128)S(1)} %get-tuple-element.26.b_ref, f32[130,8,256]{2,1,0:T(8,128)S(1)} %get-tuple-element.27.rho_ref, ...), custom_call_target="tpu_custom_call" | custom-call | flops 3000000 | bytes 9000000 | tf_op jit(solution)/shard_map/pallas_call | solution.py:502
  11.3 0.7 %collective-permute-start.2 = (f32[2,256,256]{2,1,0:T(8,128)S(1)}, f32[2,256,256]{2,1,0:T(8,128)S(1)}, u32[]{:S(2)}, u32[]{:S(2)}) collective-permute-start(f32[2,256,256]{2,1,0:T(8,128)S(1)} %get-tuple-element.38.x_ref), channel_id=1, source_target_pairs={{3,1},{5,3},{7,5},{9,7},{11,9},{13,11},{15,13},{19,17},{21,19},{23... | collective-permute-start | bytes 1572872 | tf_op jit(solution)/shard_map/ppermute | solution.py:510
  12.0 1.3 %collective-permute-start.3 = (f32[2,256,256]{2,1,0:T(8,128)S(1)}, f32[2,256,256]{2,1,0:T(8,128)S(1)}, u32[]{:S(2)}, u32[]{:S(2)}) collective-permute-start(f32[2,256,256]{2,1,0:T(8,128)S(1)} %collective-permute-done.1.high_ref), channel_id=1, source_target_pairs={{1,0},{3,2},{5,4},{7,6},{9,8},{11,10},{13,12},{15,14},{17,16},{19,... | collective-permute-start | bytes 1572872 | tf_op jit(solution)/shard_map/ppermute | solution.py:509
  13.3 0.0 collective-permute-done.low_ref
  13.3 6.1 %shard_map.89 = (f32[130,8,256]{2,1,0:T(8,128)S(1)}, f32[5,8,128]{2,1,0:T(8,128)S(1)}, f32[16,8,128]{2,1,0:T(8,128)S(1)}, f32[12288,128]{1,0:T(8,128)S(1)}) custom-call(f32[130,8,256]{2,1,0:T(8,128)S(1)} %get-tuple-element.26.b_ref, f32[130,8,256]{2,1,0:T(8,128)S(1)} %get-tuple-element.27.rho_ref, ...), custom_call_target="tpu_custom_call", output_to_operand_aliasing={{3}: (7, {})} | custom-call | flops 7000000 | bytes 21000000 | tf_op jit(solution)/shard_map/pallas_call | solution.py:511
  19.4 0.0 collective-permute-done.2.far_ref
  19.4 0.0 collective-permute-done.3.relay_ref
  19.4 3.2 %shard_map.90 = f32[16,128]{1,0:T(8,128)S(1)} custom-call(f32[130,8,256]{2,1,0:T(8,128)S(1)} %get-tuple-element.26.b_ref, f32[130,8,256]{2,1,0:T(8,128)S(1)} %get-tuple-element.27.rho_ref, f32[130,8,256]{2,1,0:T(8,128)S(1)} %get-tuple-element.35.w_ref, f32[130,8,256]{2,1,0:T(8,128)S(1)} %get-tuple-element.30.b1_ref, ...), custom_call_target="tpu_custom_call" | custom-call | flops 4000000 | bytes 12000000 | tf_op jit(solution)/shard_map/pallas_call | solution.py:525
  22.6 18.7 %all_to_all.11 = f32[16,1,128]{2,1,0:T(1,128)S(1)} all-to-all(f32[16,1,128]{2,1,0:T(1,128)S(1)} %bitcast.12), channel_id=1, replica_groups=mesh['pos'=2,'gz'=16] {'gz'}, dimensions={0} | all-to-all | bytes 16384 | tf_op jit(solution)/shard_map/all_to_all | solution.py:531
  41.3 1.5 %shard_map.91 = (f32[8,128,256]{2,1,0:T(8,128)}, f32[2,4,2,16]{3,2,1,0:T(2,128)}) custom-call(f32[16,128]{1,0:T(8,128)S(1)} %bitcast.11, f32[130,8,256]{2,1,0:T(8,128)S(1)} %get-tuple-element.26.b_ref, f32[130,8,256]{2,1,0:T(8,128)S(1)} %get-tuple-element.35.w_ref), custom_call_target="tpu_custom_call" | custom-call | flops 2000000 | bytes 6000000 | tf_op jit(solution)/shard_map/pallas_call | solution.py:532
Async XLA Ops:
  1.7 7.7 %collective-permute-start.1 = (f32[2,256,256]{2,1,0:T(8,128)S(1)}, f32[2,256,256]{2,1,0:T(8,128)S(1)}, u32[]{:S(2)}, u32[]{:S(2)}) collective-permute-start(f32[2,256,256]{2,1,0:T(8,128)S(1)} %get-tuple-element.38.x_ref), channel_id=1, source_target_pairs={{1,0},{2,1},{3,2},{4,3},{5,4},{6,5},{7,6},{8,7},{9,8},{10,9},{11,1... | collective-permute-start | bytes 1572872 | tf_op jit(solution)/shard_map/ppermute | solution.py:490
  6.4 6.9 %collective-permute-start = (f32[2,256,256]{2,1,0:T(8,128)S(1)}, f32[2,256,256]{2,1,0:T(8,128)S(1)}, u32[]{:S(2)}, u32[]{:S(2)}) collective-permute-start(f32[2,256,256]{2,1,0:T(8,128)S(1)} %get-tuple-element.38.x_ref), channel_id=1, source_target_pairs={{0,1},{1,2},{2,3},{3,4},{4,5},{5,6},{6,7},{7,8},{8,9},{9,10},{10,1... | collective-permute-start | bytes 1572872 | tf_op jit(solution)/shard_map/ppermute | solution.py:501
  11.3 8.2 %collective-permute-start.2 = (f32[2,256,256]{2,1,0:T(8,128)S(1)}, f32[2,256,256]{2,1,0:T(8,128)S(1)}, u32[]{:S(2)}, u32[]{:S(2)}) collective-permute-start(f32[2,256,256]{2,1,0:T(8,128)S(1)} %get-tuple-element.38.x_ref), channel_id=1, source_target_pairs={{3,1},{5,3},{7,5},{9,7},{11,9},{13,11},{15,13},{19,17},{21,19},{23... | collective-permute-start | bytes 1572872 | tf_op jit(solution)/shard_map/ppermute | solution.py:510
  12.0 7.5 %collective-permute-start.3 = (f32[2,256,256]{2,1,0:T(8,128)S(1)}, f32[2,256,256]{2,1,0:T(8,128)S(1)}, u32[]{:S(2)}, u32[]{:S(2)}) collective-permute-start(f32[2,256,256]{2,1,0:T(8,128)S(1)} %collective-permute-done.1.high_ref), channel_id=1, source_target_pairs={{1,0},{3,2},{5,4},{7,6},{9,8},{11,10},{13,12},{15,14},{17,16},{19,... | collective-permute-start | bytes 1572872 | tf_op jit(solution)/shard_map/ppermute | solution.py:509

commit v8 on v7

--- a/solution.py
+++ b/solution.py
@@ -67,9 +67,10 @@
 
 def in_plane(value, rho, value_next, rho_next, flow_prev, first_lane, last_lane):
     flow = (rho + rho_next) * (value - value_next)
-    along = (rho + after(rho, last_lane)) * (value - after(value, last_lane))
+    weight = rho + after(rho, last_lane)
+    along = weight * (value - after(value, last_lane))
     back = jnp.where(first_lane, -rho * value, pltpu.roll(along, 1, 1))
-    return (flow - flow_prev) + (along - back), flow
+    return (flow - flow_prev) + (along - back), flow, weight
 
 
 def sweep(x_ref, b_ref, rho_ref, even, table, emit):
@@ -98,8 +99,8 @@
                 value_next, rho_next = put(
                     row + 1, tuple(jnp.where(end, edge, inner) for edge, inner in zip(above, built))
                 )
-            total, flow = in_plane(value, rho, value_next, rho_next, flow, first_lane, last_lane)
-            emit(row, value, rho, total)
+            total, flow, weight = in_plane(value, rho, value_next, rho_next, flow, first_lane, last_lane)
+            emit(row, value, rho, total, weight)
             value, rho = value_next, rho_next
         return value, rho, flow
 
@@ -160,7 +161,7 @@
 
 
 def own_kernel(
-    tab_ref, x_ref, band_hbm, order_hbm, b_ref, rho_ref, part_ref, tile_ref, start_ref, lane_ref,
+    tab_ref, x_ref, band_hbm, order_hbm, b_ref, rho_ref, part_ref, weight_ref, gx_ref, tile_ref, start_ref, lane_ref,
     band_ref, order_ref, sems,
 ):
     copies = fetch([(band_hbm, band_ref), (order_hbm, order_ref)], sems)
@@ -169,8 +170,9 @@
     lane = iota((8, width), 1)
     first_lane, last_lane = lane == 0, lane == width - 1
 
-    def emit(row, value, rho, total):
+    def emit(row, value, rho, total, weight):
         part_ref[row] = value + total
+        weight_ref[row] = weight
 
     sweep(x_ref, b_ref, rho_ref, even, load_table(tab_ref, width), emit)
 
@@ -179,6 +181,7 @@
             row = block * 16 + step
             b = b_ref[row + 1]
             gx = after(b, last_lane) - before(b, first_lane)
+            gx_ref[row] = gx
             gy = b_ref[row + 2] - b_ref[row]
             components = forces_of(row, half, even, lane)(0.5 * (gx * gx - gy * gy), gx * gy)
             put_tiles(tile_ref, row, half, TILE_ROWS, 0, even, *components)
@@ -223,14 +226,15 @@
     width = part_ref.shape[2]
     even = iota((8, width), 0) % 2 == 0
 
-    def emit(row, value, rho, total):
-        part_ref[row] = value + total + (rho + rho_ref[row + 1]) * (value - b_ref[row + 1])
+    def emit(row, value, rho, total, weight):
+        total = value + total + (rho + rho_ref[row + 1]) * (value - b_ref[row + 1])
+        part_ref[row] = jnp.where(rho > 0.0, total, 0.0)
 
     sweep(high_ref, b1_ref, rho1_ref, even, load_table(tab_ref, width), emit)
 
 
 def field_kernel(
-    b_ref, rho_ref, part_ref, tab_ref, low_ref, b1_ref, rho1_ref, _aliased, start_any, lane_any,
+    b_ref, rho_ref, part_ref, tab_ref, low_ref, b1_ref, rho1_ref, _aliased, start_any, lane_any, gx_ref,
     w_ref, mom_ref, sums_ref, field_ref, acc_ref, start_smem, lane_smem, sems,
 ):
     half, _, width = part_ref.shape
@@ -265,10 +269,10 @@
     mom_ref[3] = jnp.minimum(jnp.maximum(shift, 0.0), 2.0)
 
     def forces(block, carry):
-        for step in range(16):
-            row = block * 16 + step
-            b, w = b_ref[row + 1], w_ref[row + 1]
-            gx_b = after(b, last_lane) - before(b, first_lane)
+        for step in range(32):
+            row = block * 32 + step
+            w = w_ref[row + 1]
+            gx_b = gx_ref[row]
             gx_w = after(w, last_lane) - before(w, first_lane)
             gy_b = b_ref[row + 2] - b_ref[row]
             gy_w = w_ref[row + 2] - w_ref[row]
@@ -279,7 +283,7 @@
             put_tiles(field_ref, row, half, TILE_ROWS, 16, even, *square)
         return carry
 
-    lax.fori_loop(0, half // 16, forces, 0)
+    lax.fori_loop(0, half // 32, forces, 0)
     for copy in copies:
         copy.wait()
 
@@ -311,7 +315,7 @@
 
 
 def face_kernel(
-    b_ref, rho_ref, w_ref, b1_ref, rho1_ref, upper_ref, tab_ref, far_ref, relay_ref, sums_ref, mom_ref, out_ref
+    b_ref, rho_ref, weight_ref, w_ref, b1_ref, rho1_ref, upper_ref, tab_ref, far_ref, relay_ref, sums_ref, mom_ref, out_ref
 ):
     half, _, width = upper_ref.shape
     table = load_table(tab_ref, width)
@@ -331,18 +335,17 @@
             b1, rho1 = b1_ref[row + 1], rho1_ref[row + 1]
             b2, rho2 = build((far_ref, relay_ref), row, half, even, table)
             w1 = 0.5 * (upper_ref[row] + (rho1 + rho2) * (b1 - b2))
-            w1 = jnp.where(rho1 > 0.0, w1, 0.0)
             p1 = b1 - shift * w1
             pp, pw = pp + p * p, pw + p * w
             coef = 1.0 + rho * outside
             up, uw = coef * p, coef * w
             fpp, fpw, fww = fpp + up * p, fpw + up * w, fww + uw * w
-            for other_rho, other_p, other_w in (
-                (rho_next, p_next, w_next),
-                (after(rho, last_lane), after(p, last_lane), after(w, last_lane)),
-                (rho1, p1, w1),
+            for weight, other_p, other_w in (
+                (rho + rho_next, p_next, w_next),
+                (weight_ref[row], after(p, last_lane), after(w, last_lane)),
+                (rho + rho1, p1, w1),
             ):
-                weight, dp, dw = rho + other_rho, p - other_p, w - other_w
+                dp, dw = p - other_p, w - other_w
                 up, uw = weight * dp, weight * dw
                 fpp, fpw, fww = fpp + up * dp, fpw + up * dw, fww + uw * dw
             w, p, rho = w_next, p_next, rho_next
@@ -490,9 +493,9 @@
     high = lax.ppermute(own, "gz", [(i + 1, i) for i in range(count - 1)])
     lists = (band // LANES, LANES)
     tile_rows = width_x * (width_y // LANES) * TILE_ROWS
-    b, rho, part, own_tiles, starts, lanes = call(
+    b, rho, part, weights, gx, own_tiles, starts, lanes = call(
         own_kernel,
-        [padded, padded, packed, (tile_rows, LANES)] + [jax.ShapeDtypeStruct(lists, jnp.int32)] * 2,
+        [padded, padded, packed, packed, packed, (tile_rows, LANES)] + [jax.ShapeDtypeStruct(lists, jnp.int32)] * 2,
         [VMEM] * 2 + [HBM] * 2,
         scratch=[pltpu.VMEM(lists, jnp.int32), pltpu.VMEM(lists, jnp.int32), dma((2,))],
         cost=estimate(3),
@@ -511,7 +514,7 @@
     w, moments, sums, _ = call(
         field_kernel,
         [padded, (5, 8, LANES), (count, 8, LANES), (tile_rows, LANES)],
-        [VMEM] * 8 + [ANY] * 2,
+        [VMEM] * 8 + [ANY] * 2 + [VMEM],
         alias={7: 3},
         scratch=[
             pltpu.VMEM((band // PER_SEC * 3, 8, LANES), jnp.float32),
@@ -521,13 +524,13 @@
         ],
         limit=10 * 2**20,
         cost=estimate(7),
-    )(b, rho, part, table, low, b1, rho1, own_tiles, starts.reshape(-1), lanes.reshape(-1))
+    )(b, rho, part, table, low, b1, rho1, own_tiles, starts.reshape(-1), lanes.reshape(-1), gx)
     (payload,) = call(
         face_kernel,
         [(count, LANES)],
-        [VMEM] * 11,
+        [VMEM] * 12,
         cost=estimate(4),
-    )(b, rho, w, b1, rho1, upper, table, far, relay, sums, moments)
+    )(b, rho, weights, w, b1, rho1, upper, table, far, relay, sums, moments)
     got = lax.all_to_all(payload, "gz", split_axis=0, concat_axis=0, tiled=True)
     solved, forces = call(
         final_kernel,

time: 43.1 us -> 42.6 us (0.988)
  Pallas kernels: 17.1 us -> 16.4 us
    pallas_call x1, Pallas kernels: 6.13 us -> 5.69 us  [body(): call(field_kernel, [padded, (5, 8, LANES), (count, 8, LANES), (tile_rows,...]
  transfers between devices with their start and end apart: 4 -> 4, of which waited for: 0 -> 1; matrix products, arithmetic and copies ran while one was open for 0% -> 0% of each run, Pallas kernels for 26% -> 26%
where the time goes in v8:
time: 42.6 us; the launch traced here: 42.4 us
  blocking collectives  18.5 us (43%)
  Pallas kernels  16.4 us (38%)
  starting transfers between devices  6.34 us (15%)
  between operations  0.72 us (2%)
    all_to_all x1, blocking collectives, body(): got = lax.all_to_all(payload, 'gz', split_axis=0, concat_axis=0, tiled=True)  18.5 us
    pallas_call x1, Pallas kernels, body(): call(field_kernel, [padded, (5, 8, LANES), (count, 8, LANES), (tile_rows,...  5.69 us
    pallas_call x1, Pallas kernels, body(): call(own_kernel, [padded, padded, packed, packed, packed, (tile_rows, LAN...  3.33 us
    ppermute x1, starting transfers between devices, body(): low = lax.ppermute(own_second, 'gz', [(i, i + 1) for i in range(count - 1)])  3.06 us
    pallas_call x1, Pallas kernels, body(): call(face_kernel, [(count, LANES)], [VMEM] * 12, cost=estimate(4))  2.96 us
    pallas_call x1, Pallas kernels, body(): call(upper_kernel, [packed, padded, padded], [VMEM] * 4, cost=estimate(3))  1.8 us
    pallas_call x1, Pallas kernels, body(): call(final_kernel, [(8, half, width_y), (2, cols, sectors, count)], [VMEM...  1.54 us
    ppermute x1, starting transfers between devices, body(): lax.ppermute(high_second, 'gz', [(i + 1, i) for i in range(0, count - 1,...  1.29 us
  transfers between devices with their start and end apart: 4, of which 1 were waited for; matrix products, arithmetic and copies ran while one was open for 0% of the time, Pallas kernels for 26%

profile of v8, /device:TPU:0, one launch (start us, length us, event | category | flops | bytes accessed | tf_op | source)
XLA Modules:
  0.0 42.4 jit_solution(9136721486892958279)
XLA Ops:
  0.6 1.1 %shard_map.86 = (f32[2,256,256]{2,1,0:T(8,128)S(1)}, f32[8,8,128]{2,1,0:T(8,128)S(1)}) custom-call(f32[1,256,256]{2,1,0:T(8,128)} %source_ref.1, s32[1,256,256]{2,1,0:T(8,128)} %regions_ref.1, f32[4]{0:T(128)} %reluct_hbm.1, f32[4]{0:T(128)} %levels_hbm.1, s32[4,4]{1,0:T(4,128)} %seeds_hbm.1), custom_call_target="tpu_custom_call" | custom-call | tf_op jit(solution)/shard_map/pallas_call | solution.py:481
  1.7 1.3 %collective-permute-start.1 = (f32[2,256,256]{2,1,0:T(8,128)S(1)}, f32[2,256,256]{2,1,0:T(8,128)S(1)}, u32[]{:S(2)}, u32[]{:S(2)}) collective-permute-start(f32[2,256,256]{2,1,0:T(8,128)S(1)} %get-tuple-element.42.x_ref), channel_id=1, source_target_pairs={{1,0},{2,1},{3,2},{4,3},{5,4},{6,5},{7,6},{8,7},{9,8},{10,9},{11,1... | collective-permute-start | bytes 1572872 | tf_op jit(solution)/shard_map/ppermute | solution.py:493
  3.0 3.3 %shard_map.87 = (f32[130,8,256]{2,1,0:T(8,128)S(1)}, f32[130,8,256]{2,1,0:T(8,128)S(1)}, f32[128,8,256]{2,1,0:T(8,128)S(1)}, f32[128,8,256]{2,1,0:T(8,128)S(1)},...) custom-call(f32[8,8,128]{2,1,0:T(8,128)S(1)} %get-tuple-element.26.tab_re, ...), custom_call_target="tpu_custom_call" | custom-call | flops 3000000 | bytes 9000000 | tf_op jit(solution)/shard_map/pallas_call | solution.py:496
  6.4 3.1 %collective-permute-start = (f32[2,256,256]{2,1,0:T(8,128)S(1)}, f32[2,256,256]{2,1,0:T(8,128)S(1)}, u32[]{:S(2)}, u32[]{:S(2)}) collective-permute-start(f32[2,256,256]{2,1,0:T(8,128)S(1)} %get-tuple-element.42.x_ref), channel_id=1, source_target_pairs={{0,1},{1,2},{2,3},{3,4},{4,5},{5,6},{6,7},{7,8},{8,9},{9,10},{10,1... | collective-permute-start | bytes 1572872 | tf_op jit(solution)/shard_map/ppermute | solution.py:504
  9.4 0.0 collective-permute-done.1.high_ref
  9.4 1.8 %shard_map.88 = (f32[128,8,256]{2,1,0:T(8,128)S(1)}, f32[130,8,256]{2,1,0:T(8,128)S(1)}, f32[130,8,256]{2,1,0:T(8,128)S(1)}) custom-call(f32[8,8,128]{2,1,0:T(8,128)S(1)} %get-tuple-element.26.tab_ref, f32[130,8,256]{2,1,0:T(8,128)S(1)} %get-tuple-element.28.b_ref, f32[130,8,256]{2,1,0:T(8,128)S(1)} %get-tuple-element.29.rho_ref, ...), custom_call_target="tpu_custom_call" | custom-call | flops 3000000 | bytes 9000000 | tf_op jit(solution)/shard_map/pallas_call | solution.py:505
  11.3 0.7 %collective-permute-start.2 = (f32[2,256,256]{2,1,0:T(8,128)S(1)}, f32[2,256,256]{2,1,0:T(8,128)S(1)}, u32[]{:S(2)}, u32[]{:S(2)}) collective-permute-start(f32[2,256,256]{2,1,0:T(8,128)S(1)} %get-tuple-element.42.x_ref), channel_id=1, source_target_pairs={{3,1},{5,3},{7,5},{9,7},{11,9},{13,11},{15,13},{19,17},{21,19},{23... | collective-permute-start | bytes 1572872 | tf_op jit(solution)/shard_map/ppermute | solution.py:513
  12.0 1.3 %collective-permute-start.3 = (f32[2,256,256]{2,1,0:T(8,128)S(1)}, f32[2,256,256]{2,1,0:T(8,128)S(1)}, u32[]{:S(2)}, u32[]{:S(2)}) collective-permute-start(f32[2,256,256]{2,1,0:T(8,128)S(1)} %collective-permute-done.1.high_ref), channel_id=1, source_target_pairs={{1,0},{3,2},{5,4},{7,6},{9,8},{11,10},{13,12},{15,14},{17,16},{19,... | collective-permute-start | bytes 1572872 | tf_op jit(solution)/shard_map/ppermute | solution.py:512
  13.3 0.0 collective-permute-done.low_ref
  13.3 5.7 %shard_map.89 = (f32[130,8,256]{2,1,0:T(8,128)S(1)}, f32[5,8,128]{2,1,0:T(8,128)S(1)}, f32[16,8,128]{2,1,0:T(8,128)S(1)}, f32[12288,128]{1,0:T(8,128)S(1)}) custom-call(f32[130,8,256]{2,1,0:T(8,128)S(1)} %get-tuple-element.28.b_ref, f32[130,8,256]{2,1,0:T(8,128)S(1)} %get-tuple-element.29.rho_ref, ...), custom_call_target="tpu_custom_call", output_to_operand_aliasing={{3}: (7, {})} | custom-call | flops 7000000 | bytes 21000000 | tf_op jit(solution)/shard_map/pallas_call | solution.py:514
  19.0 0.0 collective-permute-done.2.far_ref
  19.0 0.4 collective-permute-done.3.relay_ref
  19.4 3.0 %shard_map.90 = f32[16,128]{1,0:T(8,128)S(1)} custom-call(f32[130,8,256]{2,1,0:T(8,128)S(1)} %get-tuple-element.28.b_ref, f32[130,8,256]{2,1,0:T(8,128)S(1)} %get-tuple-element.29.rho_ref, f32[128,8,256]{2,1,0:T(8,128)S(1)} %get-tuple-element.30.weight_ref, f32[130,8,256]{2,1,0:T(8,128)S(1)} %get-tuple-element.39.w_ref, ...), custom_call_target="tpu_custom_call" | custom-call | flops 4000000 | bytes 12000000 | tf_op jit(solution)/shard_map/pallas_call | solution.py:528
  22.3 18.5 %all_to_all.11 = f32[16,1,128]{2,1,0:T(1,128)S(1)} all-to-all(f32[16,1,128]{2,1,0:T(1,128)S(1)} %bitcast.11), channel_id=1, replica_groups=mesh['pos'=2,'gz'=16] {'gz'}, dimensions={0} | all-to-all | bytes 16384 | tf_op jit(solution)/shard_map/all_to_all | solution.py:534
  40.9 1.5 %shard_map.91 = (f32[8,128,256]{2,1,0:T(8,128)}, f32[2,4,2,16]{3,2,1,0:T(2,128)}) custom-call(f32[16,128]{1,0:T(8,128)S(1)} %bitcast.12, f32[130,8,256]{2,1,0:T(8,128)S(1)} %get-tuple-element.28.b_ref, f32[130,8,256]{2,1,0:T(8,128)S(1)} %get-tuple-element.39.w_ref), custom_call_target="tpu_custom_call" | custom-call | flops 2000000 | bytes 6000000 | tf_op jit(solution)/shard_map/pallas_call | solution.py:535
Async XLA Ops:
  1.7 7.7 %collective-permute-start.1 = (f32[2,256,256]{2,1,0:T(8,128)S(1)}, f32[2,256,256]{2,1,0:T(8,128)S(1)}, u32[]{:S(2)}, u32[]{:S(2)}) collective-permute-start(f32[2,256,256]{2,1,0:T(8,128)S(1)} %get-tuple-element.42.x_ref), channel_id=1, source_target_pairs={{1,0},{2,1},{3,2},{4,3},{5,4},{6,5},{7,6},{8,7},{9,8},{10,9},{11,1... | collective-permute-start | bytes 1572872 | tf_op jit(solution)/shard_map/ppermute | solution.py:493
  6.4 6.9 %collective-permute-start = (f32[2,256,256]{2,1,0:T(8,128)S(1)}, f32[2,256,256]{2,1,0:T(8,128)S(1)}, u32[]{:S(2)}, u32[]{:S(2)}) collective-permute-start(f32[2,256,256]{2,1,0:T(8,128)S(1)} %get-tuple-element.42.x_ref), channel_id=1, source_target_pairs={{0,1},{1,2},{2,3},{3,4},{4,5},{5,6},{6,7},{7,8},{8,9},{9,10},{10,1... | collective-permute-start | bytes 1572872 | tf_op jit(solution)/shard_map/ppermute | solution.py:504
  11.3 7.7 %collective-permute-start.2 = (f32[2,256,256]{2,1,0:T(8,128)S(1)}, f32[2,256,256]{2,1,0:T(8,128)S(1)}, u32[]{:S(2)}, u32[]{:S(2)}) collective-permute-start(f32[2,256,256]{2,1,0:T(8,128)S(1)} %get-tuple-element.42.x_ref), channel_id=1, source_target_pairs={{3,1},{5,3},{7,5},{9,7},{11,9},{13,11},{15,13},{19,17},{21,19},{23... | collective-permute-start | bytes 1572872 | tf_op jit(solution)/shard_map/ppermute | solution.py:513
  12.0 7.4 %collective-permute-start.3 = (f32[2,256,256]{2,1,0:T(8,128)S(1)}, f32[2,256,256]{2,1,0:T(8,128)S(1)}, u32[]{:S(2)}, u32[]{:S(2)}) collective-permute-start(f32[2,256,256]{2,1,0:T(8,128)S(1)} %collective-permute-done.1.high_ref), channel_id=1, source_target_pairs={{1,0},{3,2},{5,4},{7,6},{9,8},{11,10},{13,12},{15,14},{17,16},{19,... | collective-permute-start | bytes 1572872 | tf_op jit(solution)/shard_map/ppermute | solution.py:512

commit v9 on v8

--- a/solution.py
+++ b/solution.py
@@ -24,13 +24,11 @@
     return lax.broadcasted_iota(jnp.int32, shape, dim)
 
 
-def build(x_refs, row, half, even, table):
+def build(x_ref, row, half, even, table):
     strength, reluct = table
 
     def pick(part):
-        lower = sum(x_ref[part, pl.ds(row, 1), :] for x_ref in x_refs)
-        upper = sum(x_ref[part, pl.ds(row + half, 1), :] for x_ref in x_refs)
-        return jnp.where(even, lower, upper)
+        return jnp.where(even, x_ref[part, pl.ds(row, 1), :], x_ref[part, pl.ds(row + half, 1), :])
 
     source, region = pick(0), pick(1)
     scale = strength[0]
@@ -82,8 +80,8 @@
         b_ref[row + 1], rho_ref[row + 1] = pair
         return pair
 
-    start = put(0, build((x_ref,), 0, half, even, table))
-    last = build((x_ref,), half - 1, half, even, table)
+    start = put(0, build(x_ref, 0, half, even, table))
+    last = build(x_ref, half - 1, half, even, table)
     below = put(-1, tuple(jnp.where(even, 0.0, pltpu.roll(value, 1, 0)) for value in last))
     above = tuple(jnp.where(even, pltpu.roll(value, 7, 0), 0.0) for value in start)
 
@@ -92,10 +90,10 @@
         for step in range(16):
             row = block * 16 + step
             if step < 15:
-                value_next, rho_next = put(row + 1, build((x_ref,), row + 1, half, even, table))
+                value_next, rho_next = put(row + 1, build(x_ref, row + 1, half, even, table))
             else:
                 end = row + 1 == half
-                built = build((x_ref,), jnp.where(end, 0, row + 1), half, even, table)
+                built = build(x_ref, jnp.where(end, 0, row + 1), half, even, table)
                 value_next, rho_next = put(
                     row + 1, tuple(jnp.where(end, edge, inner) for edge, inner in zip(above, built))
                 )
@@ -250,7 +248,7 @@
         for step in range(8):
             row = block * 8 + step
             b, rho = b_ref[row + 1], rho_ref[row + 1]
-            b_low, rho_low = build((low_ref,), row, half, even, table)
+            b_low, rho_low = build(low_ref, row, half, even, table)
             b_high, rho_high = b1_ref[row + 1], rho1_ref[row + 1]
             w = 0.5 * (part_ref[row] + (rho + rho_low) * (b - b_low) + (rho + rho_high) * (b - b_high))
             w_ref[row + 1] = w
@@ -315,7 +313,7 @@
 
 
 def face_kernel(
-    b_ref, rho_ref, weight_ref, w_ref, b1_ref, rho1_ref, upper_ref, tab_ref, far_ref, relay_ref, sums_ref, mom_ref, out_ref
+    b_ref, rho_ref, weight_ref, w_ref, b1_ref, rho1_ref, upper_ref, tab_ref, far_ref, sums_ref, mom_ref, out_ref
 ):
     half, _, width = upper_ref.shape
     table = load_table(tab_ref, width)
@@ -333,7 +331,7 @@
             w_next, rho_next = w_ref[row + 2], rho_ref[row + 2]
             p_next = b_ref[row + 2] - shift * w_next
             b1, rho1 = b1_ref[row + 1], rho1_ref[row + 1]
-            b2, rho2 = build((far_ref, relay_ref), row, half, even, table)
+            b2, rho2 = build(far_ref, row, half, even, table)
             w1 = 0.5 * (upper_ref[row] + (rho1 + rho2) * (b1 - b2))
             p1 = b1 - shift * w1
             pp, pw = pp + p * p, pw + p * w
@@ -502,15 +500,13 @@
     )(table, own, in_hbm(band_cells.reshape(lists)), in_hbm(sector_order.reshape(lists)))
     own_second, b = ORDER((own, b))
     low = lax.ppermute(own_second, "gz", [(i, i + 1) for i in range(count - 1)])
+    far = lax.ppermute(high, "gz", [(i + 1, i) for i in range(count - 1)])
     upper, b1, rho1 = call(
         upper_kernel,
         [packed, padded, padded],
         [VMEM] * 4,
         cost=estimate(3),
     )(table, b, rho, high)
-    upper, own_third, high_second = ORDER((upper, own_second, high))
-    relay = lax.ppermute(high_second, "gz", [(i + 1, i) for i in range(0, count - 1, 2)])
-    far = lax.ppermute(own_third, "gz", [(i + 2, i) for i in range(1, count - 2, 2)])
     w, moments, sums, _ = call(
         field_kernel,
         [padded, (5, 8, LANES), (count, 8, LANES), (tile_rows, LANES)],
@@ -523,14 +519,14 @@
             dma((2,)),
         ],
         limit=10 * 2**20,
-        cost=estimate(7),
+        cost=estimate(1),
     )(b, rho, part, table, low, b1, rho1, own_tiles, starts.reshape(-1), lanes.reshape(-1), gx)
     (payload,) = call(
         face_kernel,
         [(count, LANES)],
-        [VMEM] * 12,
+        [VMEM] * 11,
         cost=estimate(4),
-    )(b, rho, weights, w, b1, rho1, upper, table, far, relay, sums, moments)
+    )(b, rho, weights, w, b1, rho1, upper, table, far, sums, moments)
     got = lax.all_to_all(payload, "gz", split_axis=0, concat_axis=0, tiled=True)
     solved, forces = call(
         final_kernel,

time: 42.6 us -> 42.2 us (level)
  blocking collectives: 18.5 us -> 19.4 us
  starting transfers between devices: 6.34 us -> 5.65 us
    all_to_all x1, blocking collectives: 18.5 us -> 19.4 us  [body(): got = lax.all_to_all(payload, 'gz', split_axis=0, concat_axis=0, tiled=True)]
    ppermute x2 -> x1, starting transfers between devices: 1.99 us -> 1.29 us  [body(): far = lax.ppermute(high, 'gz', [(i + 1, i) for i in range(count - 1)])]
  transfers between devices with their start and end apart: 4 -> 3, of which waited for: 1 -> 0; matrix products, arithmetic and copies ran while one was open for 0% -> 0% of each run, Pallas kernels for 26% -> 26%
where the time goes in v9:
time: 42.2 us; the launch traced here: 41.9 us
  blocking collectives  19.4 us (46%)
  Pallas kernels  16.2 us (38%)
  starting transfers between devices  5.65 us (13%)
  between operations  0.72 us (2%)
    all_to_all x1, blocking collectives, body(): got = lax.all_to_all(payload, 'gz', split_axis=0, concat_axis=0, tiled=True)  19.4 us
    pallas_call x1, Pallas kernels, body(): call(field_kernel, [padded, (5, 8, LANES), (count, 8, LANES), (tile_rows,...  5.69 us
    pallas_call x1, Pallas kernels, body(): call(own_kernel, [padded, padded, packed, packed, packed, (tile_rows, LAN...  3.33 us
    ppermute x1, starting transfers between devices, body(): low = lax.ppermute(own_second, 'gz', [(i, i + 1) for i in range(count - 1)])  3.06 us
    pallas_call x1, Pallas kernels, body(): call(face_kernel, [(count, LANES)], [VMEM] * 11, cost=estimate(4))  2.72 us
    pallas_call x1, Pallas kernels, body(): call(upper_kernel, [packed, padded, padded], [VMEM] * 4, cost=estimate(3))  1.8 us
    pallas_call x1, Pallas kernels, body(): call(final_kernel, [(8, half, width_y), (2, cols, sectors, count)], [VMEM...  1.54 us
    ppermute x1, starting transfers between devices, body(): high = lax.ppermute(own, 'gz', [(i + 1, i) for i in range(count - 1)])  1.29 us
  transfers between devices with their start and end apart: 3, of which 0 were waited for; matrix products, arithmetic and copies ran while one was open for 0% of the time, Pallas kernels for 26%

profile of v9, /device:TPU:0, one launch (start us, length us, event | category | flops | bytes accessed | tf_op | source)
XLA Modules:
  0.0 41.9 jit_solution(690956759855459352)
XLA Ops:
  0.6 1.1 %shard_map.86 = (f32[2,256,256]{2,1,0:T(8,128)S(1)}, f32[8,8,128]{2,1,0:T(8,128)S(1)}) custom-call(f32[1,256,256]{2,1,0:T(8,128)} %source_ref.1, s32[1,256,256]{2,1,0:T(8,128)} %regions_ref.1, f32[4]{0:T(128)} %reluct_hbm.1, f32[4]{0:T(128)} %levels_hbm.1, s32[4,4]{1,0:T(4,128)} %seeds_hbm.1), custom_call_target="tpu_custom_call" | custom-call | tf_op jit(solution)/shard_map/pallas_call | solution.py:479
  1.7 1.3 %collective-permute-start.1 = (f32[2,256,256]{2,1,0:T(8,128)S(1)}, f32[2,256,256]{2,1,0:T(8,128)S(1)}, u32[]{:S(2)}, u32[]{:S(2)}) collective-permute-start(f32[2,256,256]{2,1,0:T(8,128)S(1)} %get-tuple-element.29.x_ref), channel_id=1, source_target_pairs={{1,0},{2,1},{3,2},{4,3},{5,4},{6,5},{7,6},{8,7},{9,8},{10,9},{11,1... | collective-permute-start | bytes 1572872 | tf_op jit(solution)/shard_map/ppermute | solution.py:491
  3.0 3.3 %shard_map.87 = (f32[130,8,256]{2,1,0:T(8,128)S(1)}, f32[130,8,256]{2,1,0:T(8,128)S(1)}, f32[128,8,256]{2,1,0:T(8,128)S(1)}, f32[128,8,256]{2,1,0:T(8,128)S(1)},...) custom-call(f32[8,8,128]{2,1,0:T(8,128)S(1)} %get-tuple-element.23.tab_re, ...), custom_call_target="tpu_custom_call" | custom-call | flops 3000000 | bytes 9000000 | tf_op jit(solution)/shard_map/pallas_call | solution.py:494
  6.4 3.1 %collective-permute-start = (f32[2,256,256]{2,1,0:T(8,128)S(1)}, f32[2,256,256]{2,1,0:T(8,128)S(1)}, u32[]{:S(2)}, u32[]{:S(2)}) collective-permute-start(f32[2,256,256]{2,1,0:T(8,128)S(1)} %get-tuple-element.29.x_ref), channel_id=1, source_target_pairs={{0,1},{1,2},{2,3},{3,4},{4,5},{5,6},{6,7},{7,8},{8,9},{9,10},{10,1... | collective-permute-start | bytes 1572872 | tf_op jit(solution)/shard_map/ppermute | solution.py:502
  9.4 0.0 collective-permute-done.1.high_ref
  9.4 1.3 %collective-permute-start.2 = (f32[2,256,256]{2,1,0:T(8,128)S(1)}, f32[2,256,256]{2,1,0:T(8,128)S(1)}, u32[]{:S(2)}, u32[]{:S(2)}) collective-permute-start(f32[2,256,256]{2,1,0:T(8,128)S(1)} %collective-permute-done.1.high_ref), channel_id=1, source_target_pairs={{1,0},{2,1},{3,2},{4,3},{5,4},{6,5},{7,6},{8,7},{9,8},{10,9},{11,1... | collective-permute-start | bytes 1572872 | tf_op jit(solution)/shard_map/ppermute | solution.py:503
  10.7 1.8 %shard_map.88 = (f32[128,8,256]{2,1,0:T(8,128)S(1)}, f32[130,8,256]{2,1,0:T(8,128)S(1)}, f32[130,8,256]{2,1,0:T(8,128)S(1)}) custom-call(f32[8,8,128]{2,1,0:T(8,128)S(1)} %get-tuple-element.23.tab_ref, f32[130,8,256]{2,1,0:T(8,128)S(1)} %get-tuple-element.25.b_ref, f32[130,8,256]{2,1,0:T(8,128)S(1)} %get-tuple-element.26.rho_ref, ...), custom_call_target="tpu_custom_call" | custom-call | flops 3000000 | bytes 9000000 | tf_op jit(solution)/shard_map/pallas_call | solution.py:504
  12.6 0.0 collective-permute-done.low_ref
  12.6 5.7 %shard_map.89 = (f32[130,8,256]{2,1,0:T(8,128)S(1)}, f32[5,8,128]{2,1,0:T(8,128)S(1)}, f32[16,8,128]{2,1,0:T(8,128)S(1)}, f32[12288,128]{1,0:T(8,128)S(1)}) custom-call(f32[130,8,256]{2,1,0:T(8,128)S(1)} %get-tuple-element.25.b_ref, f32[130,8,256]{2,1,0:T(8,128)S(1)} %get-tuple-element.26.rho_ref, ...), custom_call_target="tpu_custom_call", output_to_operand_aliasing={{3}: (7, {})} | custom-call | flops 1000000 | bytes 3000000 | tf_op jit(solution)/shard_map/pallas_call | solution.py:510
  18.3 0.0 collective-permute-done.2.far_ref
  18.3 2.7 %shard_map.90 = f32[16,128]{1,0:T(8,128)S(1)} custom-call(f32[130,8,256]{2,1,0:T(8,128)S(1)} %get-tuple-element.25.b_ref, f32[130,8,256]{2,1,0:T(8,128)S(1)} %get-tuple-element.26.rho_ref, f32[128,8,256]{2,1,0:T(8,128)S(1)} %get-tuple-element.27.weight_ref, f32[130,8,256]{2,1,0:T(8,128)S(1)} %get-tuple-element.36.w_ref, ...), custom_call_target="tpu_custom_call" | custom-call | flops 4000000 | bytes 12000000 | tf_op jit(solution)/shard_map/pallas_call | solution.py:524
  21.0 19.4 %all_to_all.11 = f32[16,1,128]{2,1,0:T(1,128)S(1)} all-to-all(f32[16,1,128]{2,1,0:T(1,128)S(1)} %bitcast.12), channel_id=1, replica_groups=mesh['pos'=2,'gz'=16] {'gz'}, dimensions={0} | all-to-all | bytes 16384 | tf_op jit(solution)/shard_map/all_to_all | solution.py:530
  40.4 1.5 %shard_map.91 = (f32[8,128,256]{2,1,0:T(8,128)}, f32[2,4,2,16]{3,2,1,0:T(2,128)}) custom-call(f32[16,128]{1,0:T(8,128)S(1)} %bitcast.11, f32[130,8,256]{2,1,0:T(8,128)S(1)} %get-tuple-element.25.b_ref, f32[130,8,256]{2,1,0:T(8,128)S(1)} %get-tuple-element.36.w_ref), custom_call_target="tpu_custom_call" | custom-call | flops 2000000 | bytes 6000000 | tf_op jit(solution)/shard_map/pallas_call | solution.py:531
Async XLA Ops:
  1.7 7.7 %collective-permute-start.1 = (f32[2,256,256]{2,1,0:T(8,128)S(1)}, f32[2,256,256]{2,1,0:T(8,128)S(1)}, u32[]{:S(2)}, u32[]{:S(2)}) collective-permute-start(f32[2,256,256]{2,1,0:T(8,128)S(1)} %get-tuple-element.29.x_ref), channel_id=1, source_target_pairs={{1,0},{2,1},{3,2},{4,3},{5,4},{6,5},{7,6},{8,7},{9,8},{10,9},{11,1... | collective-permute-start | bytes 1572872 | tf_op jit(solution)/shard_map/ppermute | solution.py:491
  6.4 6.2 %collective-permute-start = (f32[2,256,256]{2,1,0:T(8,128)S(1)}, f32[2,256,256]{2,1,0:T(8,128)S(1)}, u32[]{:S(2)}, u32[]{:S(2)}) collective-permute-start(f32[2,256,256]{2,1,0:T(8,128)S(1)} %get-tuple-element.29.x_ref), channel_id=1, source_target_pairs={{0,1},{1,2},{2,3},{3,4},{4,5},{5,6},{6,7},{7,8},{8,9},{9,10},{10,1... | collective-permute-start | bytes 1572872 | tf_op jit(solution)/shard_map/ppermute | solution.py:502
  9.4 8.8 %collective-permute-start.2 = (f32[2,256,256]{2,1,0:T(8,128)S(1)}, f32[2,256,256]{2,1,0:T(8,128)S(1)}, u32[]{:S(2)}, u32[]{:S(2)}) collective-permute-start(f32[2,256,256]{2,1,0:T(8,128)S(1)} %collective-permute-done.1.high_ref), channel_id=1, source_target_pairs={{1,0},{2,1},{3,2},{4,3},{5,4},{6,5},{7,6},{8,7},{9,8},{10,9},{11,1... | collective-permute-start | bytes 1572872 | tf_op jit(solution)/shard_map/ppermute | solution.py:503

commit v10 on v9

--- a/solution.py
+++ b/solution.py
@@ -232,7 +232,7 @@
 
 
 def field_kernel(
-    b_ref, rho_ref, part_ref, tab_ref, low_ref, b1_ref, rho1_ref, _aliased, start_any, lane_any, gx_ref,
+    b_ref, rho_ref, part_ref, tab_ref, low_ref, b1_ref, rho1_ref, _aliased, start_any, lane_any, gx_ref, weight_ref,
     w_ref, mom_ref, sums_ref, field_ref, acc_ref, start_smem, lane_smem, sems,
 ):
     half, _, width = part_ref.shape
@@ -266,12 +266,30 @@
     mom_ref[0], mom_ref[1], mom_ref[2] = bb, bw, ww
     mom_ref[3] = jnp.minimum(jnp.maximum(shift, 0.0), 2.0)
 
+    shift = jnp.concatenate([mom_ref[3]] * (width // LANES), axis=1)
+    outside = jnp.where(first_lane, 1.0, 0.0) + jnp.concatenate([mom_ref[4]] * (width // LANES), axis=1)
+
     def forces(block, carry):
-        for step in range(32):
-            row = block * 32 + step
-            w = w_ref[row + 1]
+        w, p, rho, pp, pw, fpp, fpw, fww = carry
+        for step in range(16):
+            row = block * 16 + step
+            w_next, rho_next = w_ref[row + 2], rho_ref[row + 2]
+            p_next = b_ref[row + 2] - shift * w_next
+            w_after = after(w, last_lane)
+            pp, pw = pp + p * p, pw + p * w
+            coef = 1.0 + rho * outside
+            up, uw = coef * p, coef * w
+            fpp, fpw, fww = fpp + up * p, fpw + up * w, fww + uw * w
+            for weight, other_p, other_w in (
+                (rho + rho_next, p_next, w_next),
+                (weight_ref[row], after(p, last_lane), w_after),
+            ):
+                dp, dw = p - other_p, w - other_w
+                up, uw = weight * dp, weight * dw
+                fpp, fpw, fww = fpp + up * dp, fpw + up * dw, fww + uw * dw
             gx_b = gx_ref[row]
-            gx_w = after(w, last_lane) - before(w, first_lane)
+            gx_w = w_after - before(w, first_lane)
+            w, p, rho = w_next, p_next, rho_next
             gy_b = b_ref[row + 2] - b_ref[row]
             gy_w = w_ref[row + 2] - w_ref[row]
             components = forces_of(row, half, even, lane)
@@ -279,9 +297,15 @@
             square = components(0.5 * (gx_w * gx_w - gy_w * gy_w), gx_w * gy_w)
             put_tiles(field_ref, row, half, TILE_ROWS, 8, even, *mixed)
             put_tiles(field_ref, row, half, TILE_ROWS, 16, even, *square)
-        return carry
-
-    lax.fori_loop(0, half // 32, forces, 0)
+        return w, p, rho, pp, pw, fpp, fpw, fww
+
+    w, rho = w_ref[1], rho_ref[1]
+    p = b_ref[1] - shift * w
+    edge = jnp.where(even, rho, 0.0)
+    carry = (w, p, rho, zero, zero, edge * p * p, edge * p * w, edge * w * w)
+    carry = lax.fori_loop(0, half // 16, forces, carry)
+    for index, total in enumerate(carry[3:]):
+        mom_ref[5 + index] = lane_sum(total) + tile
     for copy in copies:
         copy.wait()
 
@@ -313,53 +337,35 @@
 
 
 def face_kernel(
-    b_ref, rho_ref, weight_ref, w_ref, b1_ref, rho1_ref, upper_ref, tab_ref, far_ref, sums_ref, mom_ref, out_ref
+    b_ref, rho_ref, w_ref, b1_ref, rho1_ref, upper_ref, tab_ref, far_ref, sums_ref, mom_ref, out_ref
 ):
     half, _, width = upper_ref.shape
     table = load_table(tab_ref, width)
     even = iota((8, width), 0) % 2 == 0
-    lane = iota((8, width), 1)
-    first_lane, last_lane = lane == 0, lane == width - 1
     zero = jnp.zeros((8, width), jnp.float32)
     shift = jnp.concatenate([mom_ref[3]] * (width // LANES), axis=1)
-    outside = jnp.where(first_lane, 1.0, 0.0) + jnp.concatenate([mom_ref[4]] * (width // LANES), axis=1)
 
     def rows(block, carry):
-        w, p, rho, pp, pw, fpp, fpw, fww = carry
+        fpp, fpw, fww = carry
         for step in range(16):
             row = block * 16 + step
-            w_next, rho_next = w_ref[row + 2], rho_ref[row + 2]
-            p_next = b_ref[row + 2] - shift * w_next
+            w, rho = w_ref[row + 1], rho_ref[row + 1]
             b1, rho1 = b1_ref[row + 1], rho1_ref[row + 1]
             b2, rho2 = build(far_ref, row, half, even, table)
             w1 = 0.5 * (upper_ref[row] + (rho1 + rho2) * (b1 - b2))
-            p1 = b1 - shift * w1
-            pp, pw = pp + p * p, pw + p * w
-            coef = 1.0 + rho * outside
-            up, uw = coef * p, coef * w
-            fpp, fpw, fww = fpp + up * p, fpw + up * w, fww + uw * w
-            for weight, other_p, other_w in (
-                (rho + rho_next, p_next, w_next),
-                (weight_ref[row], after(p, last_lane), after(w, last_lane)),
-                (rho + rho1, p1, w1),
-            ):
-                dp, dw = p - other_p, w - other_w
-                up, uw = weight * dp, weight * dw
-                fpp, fpw, fww = fpp + up * dp, fpw + up * dw, fww + uw * dw
-            w, p, rho = w_next, p_next, rho_next
-        return w, p, rho, pp, pw, fpp, fpw, fww
-
-    w, rho = w_ref[1], rho_ref[1]
-    p = b_ref[1] - shift * w
-    edge = jnp.where(even, rho, 0.0)
-    carry = (w, p, rho, zero, zero, edge * p * p, edge * p * w, edge * w * w)
-    carry = lax.fori_loop(0, half // 16, rows, carry)
-    pp, pw, fpp, fpw, fww = carry[-5:]
+            weight, dw = rho + rho1, w - w1
+            dp = (b_ref[row + 1] - b1) - shift * dw
+            up, uw = weight * dp, weight * dw
+            fpp, fpw, fww = fpp + up * dp, fpw + up * dw, fww + uw * dw
+        return fpp, fpw, fww
+
+    fpp, fpw, fww = lax.fori_loop(0, half // 16, rows, (zero, zero, zero))
     lane_tile = iota((8, LANES), 1)
     scalars = {
         M_BB: mom_ref[0], M_BW: mom_ref[1], M_WW: mom_ref[2], M_SIG: mom_ref[3],
-        M_PP: lane_sum(pp), M_PW: lane_sum(pw),
-        M_FPP: 0.5 * lane_sum(fpp), M_FPW: 0.5 * lane_sum(fpw), M_FWW: 0.5 * lane_sum(fww),
+        M_PP: mom_ref[5], M_PW: mom_ref[6],
+        M_FPP: 0.5 * (mom_ref[7] + lane_sum(fpp)), M_FPW: 0.5 * (mom_ref[8] + lane_sum(fpw)),
+        M_FWW: 0.5 * (mom_ref[9] + lane_sum(fww)),
     }
     tile = jnp.zeros((8, LANES), jnp.float32)
     for spot, value in scalars.items():
@@ -509,8 +515,8 @@
     )(table, b, rho, high)
     w, moments, sums, _ = call(
         field_kernel,
-        [padded, (5, 8, LANES), (count, 8, LANES), (tile_rows, LANES)],
-        [VMEM] * 8 + [ANY] * 2 + [VMEM],
+        [padded, (10, 8, LANES), (count, 8, LANES), (tile_rows, LANES)],
+        [VMEM] * 8 + [ANY] * 2 + [VMEM] * 2,
         alias={7: 3},
         scratch=[
             pltpu.VMEM((band // PER_SEC * 3, 8, LANES), jnp.float32),
@@ -520,13 +526,13 @@
         ],
         limit=10 * 2**20,
         cost=estimate(1),
-    )(b, rho, part, table, low, b1, rho1, own_tiles, starts.reshape(-1), lanes.reshape(-1), gx)
+    )(b, rho, part, table, low, b1, rho1, own_tiles, starts.reshape(-1), lanes.reshape(-1), gx, weights)
     (payload,) = call(
         face_kernel,
         [(count, LANES)],
-        [VMEM] * 11,
+        [VMEM] * 10,
         cost=estimate(4),
-    )(b, rho, weights, w, b1, rho1, upper, table, far, sums, moments)
+    )(b, rho, w, b1, rho1, upper, table, far, sums, moments)
     got = lax.all_to_all(payload, "gz", split_axis=0, concat_axis=0, tiled=True)
     solved, forces = call(
         final_kernel,

time: 42.2 us -> 42.2 us (level)
  transfers between devices with their start and end apart: 3 -> 3, of which waited for: 0 -> 0; matrix products, arithmetic and copies ran while one was open for 0% -> 0% of each run, Pallas kernels for 26% -> 29%
where the time goes in v10:
time: 42.2 us; the launch traced here: 41.9 us
  blocking collectives  19.4 us (46%)
  Pallas kernels  16.2 us (38%)
  starting transfers between devices  5.65 us (13%)
  between operations  0.72 us (2%)
    all_to_all x1, blocking collectives, body(): got = lax.all_to_all(payload, 'gz', split_axis=0, concat_axis=0, tiled=True)  19.4 us
    pallas_call x1, Pallas kernels, body(): call(field_kernel, [padded, (10, 8, LANES), (count, 8, LANES), (tile_rows...  7.01 us
    pallas_call x1, Pallas kernels, body(): call(own_kernel, [padded, padded, packed, packed, packed, (tile_rows, LAN...  3.33 us
    ppermute x1, starting transfers between devices, body(): low = lax.ppermute(own_second, 'gz', [(i, i + 1) for i in range(count - 1)])  3.06 us
    pallas_call x1, Pallas kernels, body(): call(upper_kernel, [packed, padded, padded], [VMEM] * 4, cost=estimate(3))  1.82 us
    pallas_call x1, Pallas kernels, body(): call(final_kernel, [(8, half, width_y), (2, cols, sectors, count)], [VMEM...  1.54 us
    pallas_call x1, Pallas kernels, body(): call(face_kernel, [(count, LANES)], [VMEM] * 10, cost=estimate(4))  1.41 us
    ppermute x1, starting transfers between devices, body(): high = lax.ppermute(own, 'gz', [(i + 1, i) for i in range(count - 1)])  1.29 us
  transfers between devices with their start and end apart: 3, of which 0 were waited for; matrix products, arithmetic and copies ran while one was open for 0% of the time, Pallas kernels for 29%

profile of v10, /device:TPU:0, one launch (start us, length us, event | category | flops | bytes accessed | tf_op | source)
XLA Modules:
  0.0 41.9 jit_solution(3375198798863441550)
XLA Ops:
  0.6 1.1 %shard_map.86 = (f32[2,256,256]{2,1,0:T(8,128)S(1)}, f32[8,8,128]{2,1,0:T(8,128)S(1)}) custom-call(f32[1,256,256]{2,1,0:T(8,128)} %source_ref.1, s32[1,256,256]{2,1,0:T(8,128)} %regions_ref.1, f32[4]{0:T(128)} %reluct_hbm.1, f32[4]{0:T(128)} %levels_hbm.1, s32[4,4]{1,0:T(4,128)} %seeds_hbm.1), custom_call_target="tpu_custom_call" | custom-call | tf_op jit(solution)/shard_map/pallas_call | solution.py:485
  1.7 1.3 %collective-permute-start.1 = (f32[2,256,256]{2,1,0:T(8,128)S(1)}, f32[2,256,256]{2,1,0:T(8,128)S(1)}, u32[]{:S(2)}, u32[]{:S(2)}) collective-permute-start(f32[2,256,256]{2,1,0:T(8,128)S(1)} %get-tuple-element.28.x_ref), channel_id=1, source_target_pairs={{1,0},{2,1},{3,2},{4,3},{5,4},{6,5},{7,6},{8,7},{9,8},{10,9},{11,1... | collective-permute-start | bytes 1572872 | tf_op jit(solution)/shard_map/ppermute | solution.py:497
  3.0 3.3 %shard_map.87 = (f32[130,8,256]{2,1,0:T(8,128)S(1)}, f32[130,8,256]{2,1,0:T(8,128)S(1)}, f32[128,8,256]{2,1,0:T(8,128)S(1)}, f32[128,8,256]{2,1,0:T(8,128)S(1)},...) custom-call(f32[8,8,128]{2,1,0:T(8,128)S(1)} %get-tuple-element.23.tab_re, ...), custom_call_target="tpu_custom_call" | custom-call | flops 3000000 | bytes 9000000 | tf_op jit(solution)/shard_map/pallas_call | solution.py:500
  6.4 3.1 %collective-permute-start = (f32[2,256,256]{2,1,0:T(8,128)S(1)}, f32[2,256,256]{2,1,0:T(8,128)S(1)}, u32[]{:S(2)}, u32[]{:S(2)}) collective-permute-start(f32[2,256,256]{2,1,0:T(8,128)S(1)} %get-tuple-element.28.x_ref), channel_id=1, source_target_pairs={{0,1},{1,2},{2,3},{3,4},{4,5},{5,6},{6,7},{7,8},{8,9},{9,10},{10,1... | collective-permute-start | bytes 1572872 | tf_op jit(solution)/shard_map/ppermute | solution.py:508
  9.4 0.0 collective-permute-done.1.high_ref
  9.4 1.3 %collective-permute-start.2 = (f32[2,256,256]{2,1,0:T(8,128)S(1)}, f32[2,256,256]{2,1,0:T(8,128)S(1)}, u32[]{:S(2)}, u32[]{:S(2)}) collective-permute-start(f32[2,256,256]{2,1,0:T(8,128)S(1)} %collective-permute-done.1.high_ref), channel_id=1, source_target_pairs={{1,0},{2,1},{3,2},{4,3},{5,4},{6,5},{7,6},{8,7},{9,8},{10,9},{11,1... | collective-permute-start | bytes 1572872 | tf_op jit(solution)/shard_map/ppermute | solution.py:509
  10.7 1.8 %shard_map.88 = (f32[128,8,256]{2,1,0:T(8,128)S(1)}, f32[130,8,256]{2,1,0:T(8,128)S(1)}, f32[130,8,256]{2,1,0:T(8,128)S(1)}) custom-call(f32[8,8,128]{2,1,0:T(8,128)S(1)} %get-tuple-element.23.tab_ref, f32[130,8,256]{2,1,0:T(8,128)S(1)} %get-tuple-element.25.b_ref, f32[130,8,256]{2,1,0:T(8,128)S(1)} %get-tuple-element.26.rho_ref, ...), custom_call_target="tpu_custom_call" | custom-call | flops 3000000 | bytes 9000000 | tf_op jit(solution)/shard_map/pallas_call | solution.py:510
  12.6 0.0 collective-permute-done.low_ref
  12.6 7.0 %shard_map.89 = (f32[130,8,256]{2,1,0:T(8,128)S(1)}, f32[10,8,128]{2,1,0:T(8,128)S(1)}, f32[16,8,128]{2,1,0:T(8,128)S(1)}, f32[12288,128]{1,0:T(8,128)S(1)}) custom-call(f32[130,8,256]{2,1,0:T(8,128)S(1)} %get-tuple-element.25.b_ref, f32[130,8,256]{2,1,0:T(8,128)S(1)} %get-tuple-element.26.rho_ref, ...), custom_call_target="tpu_custom_call", output_to_operand_aliasing={{3}: (7, {})} | custom-call | flops 1000000 | bytes 3000000 | tf_op jit(solution)/shard_map/pallas_call | solution.py:516
  19.6 0.0 collective-permute-done.2.far_ref
  19.6 1.4 %shard_map.90 = f32[16,128]{1,0:T(8,128)S(1)} custom-call(f32[130,8,256]{2,1,0:T(8,128)S(1)} %get-tuple-element.25.b_ref, f32[130,8,256]{2,1,0:T(8,128)S(1)} %get-tuple-element.26.rho_ref, f32[130,8,256]{2,1,0:T(8,128)S(1)} %get-tuple-element.36.w_ref, f32[130,8,256]{2,1,0:T(8,128)S(1)} %get-tuple-element.29.b1_ref, ...), custom_call_target="tpu_custom_call" | custom-call | flops 4000000 | bytes 12000000 | tf_op jit(solution)/shard_map/pallas_call | solution.py:530
  21.0 19.4 %all_to_all.11 = f32[16,1,128]{2,1,0:T(1,128)S(1)} all-to-all(f32[16,1,128]{2,1,0:T(1,128)S(1)} %bitcast.11), channel_id=1, replica_groups=mesh['pos'=2,'gz'=16] {'gz'}, dimensions={0} | all-to-all | bytes 16384 | tf_op jit(solution)/shard_map/all_to_all | solution.py:536
  40.4 1.5 %shard_map.91 = (f32[8,128,256]{2,1,0:T(8,128)}, f32[2,4,2,16]{3,2,1,0:T(2,128)}) custom-call(f32[16,128]{1,0:T(8,128)S(1)} %bitcast.12, f32[130,8,256]{2,1,0:T(8,128)S(1)} %get-tuple-element.25.b_ref, f32[130,8,256]{2,1,0:T(8,128)S(1)} %get-tuple-element.36.w_ref), custom_call_target="tpu_custom_call" | custom-call | flops 2000000 | bytes 6000000 | tf_op jit(solution)/shard_map/pallas_call | solution.py:537
Async XLA Ops:
  1.7 7.7 %collective-permute-start.1 = (f32[2,256,256]{2,1,0:T(8,128)S(1)}, f32[2,256,256]{2,1,0:T(8,128)S(1)}, u32[]{:S(2)}, u32[]{:S(2)}) collective-permute-start(f32[2,256,256]{2,1,0:T(8,128)S(1)} %get-tuple-element.28.x_ref), channel_id=1, source_target_pairs={{1,0},{2,1},{3,2},{4,3},{5,4},{6,5},{7,6},{8,7},{9,8},{10,9},{11,1... | collective-permute-start | bytes 1572872 | tf_op jit(solution)/shard_map/ppermute | solution.py:497
  6.4 6.2 %collective-permute-start = (f32[2,256,256]{2,1,0:T(8,128)S(1)}, f32[2,256,256]{2,1,0:T(8,128)S(1)}, u32[]{:S(2)}, u32[]{:S(2)}) collective-permute-start(f32[2,256,256]{2,1,0:T(8,128)S(1)} %get-tuple-element.28.x_ref), channel_id=1, source_target_pairs={{0,1},{1,2},{2,3},{3,4},{4,5},{5,6},{6,7},{7,8},{8,9},{9,10},{10,1... | collective-permute-start | bytes 1572872 | tf_op jit(solution)/shard_map/ppermute | solution.py:508
  9.4 10.2 %collective-permute-start.2 = (f32[2,256,256]{2,1,0:T(8,128)S(1)}, f32[2,256,256]{2,1,0:T(8,128)S(1)}, u32[]{:S(2)}, u32[]{:S(2)}) collective-permute-start(f32[2,256,256]{2,1,0:T(8,128)S(1)} %collective-permute-done.1.high_ref), channel_id=1, source_target_pairs={{1,0},{2,1},{3,2},{4,3},{5,4},{6,5},{7,6},{8,7},{9,8},{10,9},{11,1... | collective-permute-start | bytes 1572872 | tf_op jit(solution)/shard_map/ppermute | solution.py:509

commit v11 on v10

--- a/solution.py
+++ b/solution.py
@@ -159,10 +159,8 @@
 
 
 def own_kernel(
-    tab_ref, x_ref, band_hbm, order_hbm, b_ref, rho_ref, part_ref, weight_ref, gx_ref, tile_ref, start_ref, lane_ref,
-    band_ref, order_ref, sems,
+    tab_ref, x_ref, b_ref, rho_ref, part_ref, weight_ref, gx_ref, tile_ref
 ):
-    copies = fetch([(band_hbm, band_ref), (order_hbm, order_ref)], sems)
     half, _, width = part_ref.shape
     even = iota((8, width), 0) % 2 == 0
     lane = iota((8, width), 1)
@@ -186,9 +184,6 @@
         return carry
 
     lax.fori_loop(0, half // 16, forces, 0)
-    for copy in copies:
-        copy.wait()
-    locate(band_ref, order_ref, start_ref, lane_ref)
 
 
 def lane_sum(value):
@@ -220,7 +215,11 @@
     lax.fori_loop(0, order_ref.shape[0], chunk, 0, unroll=True if order_ref.shape[0] <= 16 else 8)
 
 
-def upper_kernel(tab_ref, b_ref, rho_ref, high_ref, part_ref, b1_ref, rho1_ref):
+def upper_kernel(
+    tab_ref, b_ref, rho_ref, high_ref, band_hbm, order_hbm, part_ref, b1_ref, rho1_ref, start_ref, lane_ref,
+    band_ref, order_ref, sems,
+):
+    copies = fetch([(band_hbm, band_ref), (order_hbm, order_ref)], sems)
     width = part_ref.shape[2]
     even = iota((8, width), 0) % 2 == 0
 
@@ -229,6 +228,9 @@
         part_ref[row] = jnp.where(rho > 0.0, total, 0.0)
 
     sweep(high_ref, b1_ref, rho1_ref, even, load_table(tab_ref, width), emit)
+    for copy in copies:
+        copy.wait()
+    locate(band_ref, order_ref, start_ref, lane_ref)
 
 
 def field_kernel(
@@ -497,22 +499,22 @@
     high = lax.ppermute(own, "gz", [(i + 1, i) for i in range(count - 1)])
     lists = (band // LANES, LANES)
     tile_rows = width_x * (width_y // LANES) * TILE_ROWS
-    b, rho, part, weights, gx, own_tiles, starts, lanes = call(
+    b, rho, part, weights, gx, own_tiles = call(
         own_kernel,
-        [padded, padded, packed, packed, packed, (tile_rows, LANES)] + [jax.ShapeDtypeStruct(lists, jnp.int32)] * 2,
-        [VMEM] * 2 + [HBM] * 2,
-        scratch=[pltpu.VMEM(lists, jnp.int32), pltpu.VMEM(lists, jnp.int32), dma((2,))],
+        [padded, padded, packed, packed, packed, (tile_rows, LANES)],
+        [VMEM] * 2,
         cost=estimate(3),
-    )(table, own, in_hbm(band_cells.reshape(lists)), in_hbm(sector_order.reshape(lists)))
+    )(table, own)
     own_second, b = ORDER((own, b))
     low = lax.ppermute(own_second, "gz", [(i, i + 1) for i in range(count - 1)])
     far = lax.ppermute(high, "gz", [(i + 1, i) for i in range(count - 1)])
-    upper, b1, rho1 = call(
+    upper, b1, rho1, starts, lanes = call(
         upper_kernel,
-        [packed, padded, padded],
-        [VMEM] * 4,
+        [packed, padded, padded] + [jax.ShapeDtypeStruct(lists, jnp.int32)] * 2,
+        [VMEM] * 4 + [HBM] * 2,
+        scratch=[pltpu.VMEM(lists, jnp.int32), pltpu.VMEM(lists, jnp.int32), dma((2,))],
         cost=estimate(3),
-    )(table, b, rho, high)
+    )(table, b, rho, high, in_hbm(band_cells.reshape(lists)), in_hbm(sector_order.reshape(lists)))
     w, moments, sums, _ = call(
         field_kernel,
         [padded, (10, 8, LANES), (count, 8, LANES), (tile_rows, LANES)],

time: 42.2 us -> 41.9 us (level)
  no operation moved by 1% of the time
where the time goes in v11:
time: 41.9 us; the launch traced here: 41.6 us
  blocking collectives  19.1 us (46%)
  Pallas kernels  16.2 us (39%)
  starting transfers between devices  5.65 us (13%)
  between operations  0.72 us (2%)
    all_to_all x1, blocking collectives, body(): got = lax.all_to_all(payload, 'gz', split_axis=0, concat_axis=0, tiled=True)  19.1 us
    pallas_call x1, Pallas kernels, body(): call(field_kernel, [padded, (10, 8, LANES), (count, 8, LANES), (tile_rows...  7.01 us
    ppermute x1, starting transfers between devices, body(): low = lax.ppermute(own_second, 'gz', [(i, i + 1) for i in range(count - 1)])  3.06 us
    pallas_call x1, Pallas kernels, body(): call(own_kernel, [padded, padded, packed, packed, packed, (tile_rows, LAN...  3.02 us
    pallas_call x1, Pallas kernels, body(): call(upper_kernel, [packed, padded, padded] + [jax.ShapeDtypeStruct(lists...  2.09 us
    pallas_call x1, Pallas kernels, body(): call(final_kernel, [(8, half, width_y), (2, cols, sectors, count)], [VMEM...  1.54 us
    pallas_call x1, Pallas kernels, body(): call(face_kernel, [(count, LANES)], [VMEM] * 10, cost=estimate(4))  1.4 us
    ppermute x1, starting transfers between devices, body(): high = lax.ppermute(own, 'gz', [(i + 1, i) for i in range(count - 1)])  1.29 us
  transfers between devices with their start and end apart: 3, of which 0 were waited for; matrix products, arithmetic and copies ran while one was open for 0% of the time, Pallas kernels for 29%

profile of v11, /device:TPU:0, one launch (start us, length us, event | category | flops | bytes accessed | tf_op | source)
XLA Modules:
  0.0 41.6 jit_solution(8367002114621808695)
XLA Ops:
  0.6 1.1 %shard_map.86 = (f32[2,256,256]{2,1,0:T(8,128)S(1)}, f32[8,8,128]{2,1,0:T(8,128)S(1)}) custom-call(f32[1,256,256]{2,1,0:T(8,128)} %source_ref.1, s32[1,256,256]{2,1,0:T(8,128)} %regions_ref.1, f32[4]{0:T(128)} %reluct_hbm.1, f32[4]{0:T(128)} %levels_hbm.1, s32[4,4]{1,0:T(4,128)} %seeds_hbm.1), custom_call_target="tpu_custom_call" | custom-call | tf_op jit(solution)/shard_map/pallas_call | solution.py:487
  1.7 1.3 %collective-permute-start.1 = (f32[2,256,256]{2,1,0:T(8,128)S(1)}, f32[2,256,256]{2,1,0:T(8,128)S(1)}, u32[]{:S(2)}, u32[]{:S(2)}) collective-permute-start(f32[2,256,256]{2,1,0:T(8,128)S(1)} %get-tuple-element.28.x_ref), channel_id=1, source_target_pairs={{1,0},{2,1},{3,2},{4,3},{5,4},{6,5},{7,6},{8,7},{9,8},{10,9},{11,1... | collective-permute-start | bytes 1572872 | tf_op jit(solution)/shard_map/ppermute | solution.py:499
  3.0 3.0 %shard_map.87 = (f32[130,8,256]{2,1,0:T(8,128)S(1)}, f32[130,8,256]{2,1,0:T(8,128)S(1)}, f32[128,8,256]{2,1,0:T(8,128)S(1)}, f32[128,8,256]{2,1,0:T(8,128)S(1)},...) custom-call(f32[8,8,128]{2,1,0:T(8,128)S(1)} %get-tuple-element.23.tab_ref, f32[2,256,256]{2,1,0:T(8,128)S(1)} %get-tuple-element.28.x_ref), custom_call_target="tpu_custom_call" | custom-call | flops 3000000 | bytes 9000000 | tf_op jit(solution)/shard_map/pallas_call | solution.py:502
  6.1 3.1 %collective-permute-start = (f32[2,256,256]{2,1,0:T(8,128)S(1)}, f32[2,256,256]{2,1,0:T(8,128)S(1)}, u32[]{:S(2)}, u32[]{:S(2)}) collective-permute-start(f32[2,256,256]{2,1,0:T(8,128)S(1)} %get-tuple-element.28.x_ref), channel_id=1, source_target_pairs={{0,1},{1,2},{2,3},{3,4},{4,5},{5,6},{6,7},{7,8},{8,9},{9,10},{10,1... | collective-permute-start | bytes 1572872 | tf_op jit(solution)/shard_map/ppermute | solution.py:509
  9.1 0.0 collective-permute-done.1.high_ref
  9.1 1.3 %collective-permute-start.2 = (f32[2,256,256]{2,1,0:T(8,128)S(1)}, f32[2,256,256]{2,1,0:T(8,128)S(1)}, u32[]{:S(2)}, u32[]{:S(2)}) collective-permute-start(f32[2,256,256]{2,1,0:T(8,128)S(1)} %collective-permute-done.1.high_ref), channel_id=1, source_target_pairs={{1,0},{2,1},{3,2},{4,3},{5,4},{6,5},{7,6},{8,7},{9,8},{10,9},{11,1... | collective-permute-start | bytes 1572872 | tf_op jit(solution)/shard_map/ppermute | solution.py:510
  10.4 2.1 %shard_map.88 = (f32[128,8,256]{2,1,0:T(8,128)S(1)}, f32[130,8,256]{2,1,0:T(8,128)S(1)}, f32[130,8,256]{2,1,0:T(8,128)S(1)}, s32[16,128]{1,0:T(8,128)S(1)}, s32[16,128]{1,0:T(8,128)S(1)}) custom-call(f32[8,8,128]{2,1,0:T(8,128)S(1)} %get-tuple-element.23.tab_ref, f32[130,8,256]{2,1,0:T(8,128)S(1)} %get-tuple-element.25.b_ref, ...), custom_call_target="tpu_custom_call" | custom-call | flops 3000000 | bytes 9000000 | tf_op jit(solution)/shard_map/pallas_call | solution.py:511
  12.5 0.0 collective-permute-done.low_ref
  12.5 7.0 %shard_map.89 = (f32[130,8,256]{2,1,0:T(8,128)S(1)}, f32[10,8,128]{2,1,0:T(8,128)S(1)}, f32[16,8,128]{2,1,0:T(8,128)S(1)}, f32[12288,128]{1,0:T(8,128)S(1)}) custom-call(f32[130,8,256]{2,1,0:T(8,128)S(1)} %get-tuple-element.25.b_ref, f32[130,8,256]{2,1,0:T(8,128)S(1)} %get-tuple-element.26.rho_ref, ...), custom_call_target="tpu_custom_call", output_to_operand_aliasing={{3}: (7, {})} | custom-call | flops 1000000 | bytes 3000000 | tf_op jit(solution)/shard_map/pallas_call | solution.py:518
  19.6 0.0 collective-permute-done.2.far_ref
  19.6 1.4 %shard_map.90 = f32[16,128]{1,0:T(8,128)S(1)} custom-call(f32[130,8,256]{2,1,0:T(8,128)S(1)} %get-tuple-element.25.b_ref, f32[130,8,256]{2,1,0:T(8,128)S(1)} %get-tuple-element.26.rho_ref, f32[130,8,256]{2,1,0:T(8,128)S(1)} %get-tuple-element.36.w_ref, f32[130,8,256]{2,1,0:T(8,128)S(1)} %get-tuple-element.29.b1_ref, ...), custom_call_target="tpu_custom_call" | custom-call | flops 4000000 | bytes 12000000 | tf_op jit(solution)/shard_map/pallas_call | solution.py:532
  21.0 19.1 %all_to_all.11 = f32[16,1,128]{2,1,0:T(1,128)S(1)} all-to-all(f32[16,1,128]{2,1,0:T(1,128)S(1)} %bitcast.11), channel_id=1, replica_groups=mesh['pos'=2,'gz'=16] {'gz'}, dimensions={0} | all-to-all | bytes 16384 | tf_op jit(solution)/shard_map/all_to_all | solution.py:538
  40.1 1.5 %shard_map.91 = (f32[8,128,256]{2,1,0:T(8,128)}, f32[2,4,2,16]{3,2,1,0:T(2,128)}) custom-call(f32[16,128]{1,0:T(8,128)S(1)} %bitcast.12, f32[130,8,256]{2,1,0:T(8,128)S(1)} %get-tuple-element.25.b_ref, f32[130,8,256]{2,1,0:T(8,128)S(1)} %get-tuple-element.36.w_ref), custom_call_target="tpu_custom_call" | custom-call | flops 2000000 | bytes 6000000 | tf_op jit(solution)/shard_map/pallas_call | solution.py:539
Async XLA Ops:
  1.7 7.4 %collective-permute-start.1 = (f32[2,256,256]{2,1,0:T(8,128)S(1)}, f32[2,256,256]{2,1,0:T(8,128)S(1)}, u32[]{:S(2)}, u32[]{:S(2)}) collective-permute-start(f32[2,256,256]{2,1,0:T(8,128)S(1)} %get-tuple-element.28.x_ref), channel_id=1, source_target_pairs={{1,0},{2,1},{3,2},{4,3},{5,4},{6,5},{7,6},{8,7},{9,8},{10,9},{11,1... | collective-permute-start | bytes 1572872 | tf_op jit(solution)/shard_map/ppermute | solution.py:499
  6.1 6.5 %collective-permute-start = (f32[2,256,256]{2,1,0:T(8,128)S(1)}, f32[2,256,256]{2,1,0:T(8,128)S(1)}, u32[]{:S(2)}, u32[]{:S(2)}) collective-permute-start(f32[2,256,256]{2,1,0:T(8,128)S(1)} %get-tuple-element.28.x_ref), channel_id=1, source_target_pairs={{0,1},{1,2},{2,3},{3,4},{4,5},{5,6},{6,7},{7,8},{8,9},{9,10},{10,1... | collective-permute-start | bytes 1572872 | tf_op jit(solution)/shard_map/ppermute | solution.py:509
  9.1 10.4 %collective-permute-start.2 = (f32[2,256,256]{2,1,0:T(8,128)S(1)}, f32[2,256,256]{2,1,0:T(8,128)S(1)}, u32[]{:S(2)}, u32[]{:S(2)}) collective-permute-start(f32[2,256,256]{2,1,0:T(8,128)S(1)} %collective-permute-done.1.high_ref), channel_id=1, source_target_pairs={{1,0},{2,1},{3,2},{4,3},{5,4},{6,5},{7,6},{8,7},{9,8},{10,9},{11,1... | collective-permute-start | bytes 1572872 | tf_op jit(solution)/shard_map/ppermute | solution.py:510
